TPU v7x, 32 devices: a whole 2x2x4 slice. The times are simulated.
32 devices in a mesh: rep: 8 (over z, x), grp: 4 (over y, core).
Axes of the slice: x: 2, y: 2, z: 4, core: 2. Of those that a mesh axis runs over, the one named last changes fastest.
Arguments:
- tokens: bfloat16 [8, 512, 1088], P('rep', 'grp'), may hold values from -24 to 24
- segments: int32 [8, 512], P('rep'), may hold values from 0 to 3, never falling along the last dimension, each value on 1 to 256 neighbouring positions
- cotangent: bfloat16 [8, 512, 1088], P('rep', 'grp'), may hold values from -6 to 6
- packed_weight: bfloat16 [1088, 3264], P('grp')
- output_weight: bfloat16 [1088, 1088], P('grp'), may hold values from -0.5 to 0.5
- up_weight: bfloat16 [1088, 4352], P('grp'), may hold values from -0.1875 to 0.1875
- down_weight: bfloat16 [4352, 1088], P('grp'), may hold values from -0.09375 to 0.09375
- first_gain: bfloat16 [1088], P('grp'), may hold values from 0.099609375 to 1.8984375
- first_shift: bfloat16 [1088], P('grp'), may hold values from -3 to 3
- query_bias: bfloat16 [1088], P('grp'), may hold values from -3 to 3
- value_bias: bfloat16 [1088], P('grp'), may hold values from -3 to 3
- output_bias: bfloat16 [1088], P('grp'), may hold values from -3 to 3
- second_gain: bfloat16 [1088], P('grp'), may hold values from 0.099609375 to 1.8984375
- second_shift: bfloat16 [1088], P('grp'), may hold values from -3 to 3
- hidden_bias: bfloat16 [4352], P('grp'), may hold values from -3 to 3
- down_bias: bfloat16 [1088], P('grp'), may hold values from -3 to 3
Outputs:
- layer_out: float32 [8, 512, 1088], P('rep', 'grp')
- grad_tokens: float32 [8, 512, 1088], P('rep', 'grp')
- grad_packed_weight: float32 [1088, 3264], P('grp', 'rep')
- grad_output_weight: float32 [1088, 1088], P('grp', 'rep')
- grad_up_weight: float32 [1088, 4352], P('grp', 'rep')
- grad_down_weight: float32 [4352, 1088], P('grp', 'rep')
- grad_first_gain: float32 [1088], replicated
- grad_first_shift: float32 [1088], replicated
- grad_query_bias: float32 [1088], replicated
- grad_value_bias: float32 [1088], replicated
- grad_output_bias: float32 [1088], replicated
- grad_second_gain: float32 [1088], replicated
- grad_second_shift: float32 [1088], replicated
- grad_hidden_bias: float32 [4352], replicated
- grad_down_bias: float32 [1088], replicated
Inputs may be any that keep to these rules, and one draw needn't show every extreme that they name: `segments`: within each sequence the document numbers never fall, every number appears, and each document has at most 256 tokens; some document has exactly that many.
All inputs are finite; a program needn't handle non-finite values.
Results may differ from a plain program's by a relative error of at most 0.02.
The roundings to bfloat16 on the way count: a program that leaves them out, or rounds other values in their place, can miss the bound.
Values may be sent and summed in bfloat16 or wider, within the bound.
No kernel may reach another device: no remote copies, remote signals or barrier semaphores. Data moves between devices by JAX's collectives and lax.ppermute only.
A program may use at most 256 MiB of HBM per device.

v0:
```python
import math

import jax
import jax.numpy as jnp
from jax import lax
from jax.experimental import pallas as pl
from jax.experimental.pallas import tpu as pltpu
from jax.sharding import PartitionSpec as P

D = 1088
HEADS = 17
HD = 64

epsilon = 1e-05
gelu_factor = 0.7978845608028654
masked_score = -1e30
f32 = jnp.float32
bf16 = jnp.bfloat16


def gelu_parts(pre_act):
    inner = gelu_factor * (pre_act + 0.044715 * pre_act * pre_act * pre_act)
    tanh_value = jnp.tanh(inner)
    gelu_value = 0.5 * pre_act * (1.0 + tanh_value)
    gelu_slope = 0.5 * (1.0 + tanh_value) + 0.5 * pre_act * (
        1.0 - tanh_value * tanh_value
    ) * gelu_factor * (1.0 + 3.0 * 0.044715 * pre_act * pre_act)
    return (gelu_value, gelu_slope)


def norm_rows(field):
    row_mean = jnp.mean(field, axis=-1, keepdims=True)
    centered = field - row_mean
    inv_std = lax.rsqrt(jnp.mean(centered * centered, axis=-1, keepdims=True) + epsilon)
    return (centered * inv_std, inv_std)


def norm_back(grad_out, normed, inv_std, gain_row):
    scaled = grad_out * gain_row
    return inv_std * (
        scaled
        - jnp.mean(scaled, axis=-1, keepdims=True)
        - normed * jnp.mean(scaled * normed, axis=-1, keepdims=True)
    )


def contract(left, right, left_dim, right_dim):
    return lax.dot_general(
        left, right, (((left_dim,), (right_dim,)), ((), ())), preferred_element_type=f32
    )


def swap(value, axis, size, bit):
    return lax.ppermute(value, axis, [(i, i ^ bit) for i in range(size)])


def starts_at(value, start, axis):
    starts = [0] * value.ndim
    starts[axis] = start
    return starts


def cut(value, start, length, axis):
    sizes = list(value.shape)
    sizes[axis] = length
    starts = starts_at(value, start, axis)
    return lax.dynamic_slice(value, starts, sizes, allow_negative_indices=False)


def pick(value, index, axis):
    return lax.squeeze(cut(value, index, 1, axis), (axis,))


def put(whole, part, start, axis):
    starts = starts_at(whole, start, axis)
    return lax.dynamic_update_slice(whole, part, starts, allow_negative_indices=False)


def log2(count):
    return count.bit_length() - 1


def relative_order(size):
    order = [0]
    bit = size // 2
    while bit:
        order = order + [o ^ bit for o in order]
        bit //= 2
    return order


def group_gather(value, size):
    bit = size // 2
    while bit:
        value = jnp.concatenate([value, swap(value, "grp", size, bit)])
        bit //= 2
    return value


def group_scatter_sum(value, size):
    bit = 1
    while bit < size:
        half = value.shape[0] // 2
        moved = swap(value[half:].astype(bf16), "grp", size, bit)
        value = value[:half] + moved.astype(f32)
        bit *= 2
    return value


def place_kernel(rank_ref, *refs):
    out_ref = refs[-1]
    for j, ref in enumerate(refs[:-1]):
        rows = ref.shape[0]
        out_ref[pl.ds(pl.multiple_of((rank_ref[0] ^ j) * rows, 16), rows), :] = ref[...]


def place_rows(blocks, rank):
    rows, cols = blocks[0].shape
    size = len(blocks)
    if rows % 16:
        whole = jnp.zeros((rows * size, cols), blocks[0].dtype)
        for j, block in enumerate(blocks):
            whole = put(whole, block, (rank ^ j) * rows, 0)
        return whole
    return pl.pallas_call(
        place_kernel,
        grid_spec=pltpu.PrefetchScalarGridSpec(
            num_scalar_prefetch=1,
            grid=(1,),
            in_specs=[pl.BlockSpec((rows, cols), lambda i, _: (0, 0))] * size,
            out_specs=pl.BlockSpec((rows * size, cols), lambda i, _: (0, 0)),
        ),
        out_shape=jax.ShapeDtypeStruct((rows * size, cols), blocks[0].dtype),
        cost_estimate=pl.CostEstimate(
            flops=0, transcendentals=0, bytes_accessed=4 * rows * size * cols
        ),
    )(rank.reshape(1), *blocks)


def first_head(rank, size):
    return lax.div(rank * (D // size), HD)


def pack_kernel(width, rank_ref, source_ref, *out_refs):
    for j, out_ref in enumerate(out_refs):
        begin = first_head(rank_ref[0] ^ j, len(out_refs)) * HD
        parts = []
        for t in range(3):
            shift = D * t % 128
            start = pl.multiple_of(begin + (D * t - shift), 128)
            parts.append(source_ref[:, pl.ds(start, shift + width)][:, shift:])
        out_ref[...] = jnp.concatenate(parts, axis=1)


def pack_columns(weight, begins, width, rank, size):
    starts = [min(b * HD, D - width) for b in begins]
    if any(start % 128 or start != b * HD for start, b in zip(starts, begins)):
        sets = jnp.stack(
            [
                jnp.concatenate([weight[:, D * t + o : D * t + o + width] for t in range(3)], axis=1)
                for o in starts
            ]
        )
        return [pick(sets, rank ^ j, 0) for j in range(size)]
    rows = weight.shape[0]
    return pl.pallas_call(
        lambda *refs: pack_kernel(width, *refs),
        grid_spec=pltpu.PrefetchScalarGridSpec(
            num_scalar_prefetch=1,
            grid=(1,),
            in_specs=[pl.BlockSpec(weight.shape, lambda i, _: (0, 0))],
            out_specs=[pl.BlockSpec((rows, 3 * width), lambda i, _: (0, 0))] * size,
        ),
        out_shape=[jax.ShapeDtypeStruct((rows, 3 * width), weight.dtype)] * size,
        cost_estimate=pl.CostEstimate(
            flops=0, transcendentals=0, bytes_accessed=14 * rows * width * size
        ),
        name="pack_columns",
    )(rank.reshape(1), weight)


def tie(values, deps):
    return lax.optimization_barrier((values, deps))[0]


def sum_over(vector, axis, count):
    bit = 1
    while bit < count:
        moved = swap(vector, axis, count, bit)
        vector = vector + moved
        bit *= 2
    return vector


def rep_bit(bit):
    return (lax.axis_index("rep") >> bit) & 1


def add_parts(parts, dtype):
    total = parts[0].astype(f32)
    for part in parts[1:]:
        total = total + part.astype(f32)
    return total.astype(dtype)


def halve_rows(value, bit, reps, axis):
    mine = rep_bit(bit)
    half = value.shape[axis] // 2
    keep = cut(value, mine * half, half, axis)
    give = cut(value, (1 - mine) * half, half, axis).astype(bf16)
    return keep, swap(give, "rep", reps, 1 << bit)


def halve_lanes(value, bit, reps):
    mine = rep_bit(bit) == 1
    half = value.shape[-1] // 2
    low, high = value[..., :half], value[..., half:]
    give = jnp.where(mine, low, high).astype(bf16)
    return jnp.where(mine, high, low), swap(give, "rep", reps, 1 << bit)


def natural_rows(value, reps):
    return value.reshape((2,) * log2(reps) + (value.shape[0] // reps,) + value.shape[1:])


def quad_step(value, axis, reps, size):
    low = lax.axis_index("rep") & (size - 1)
    block = lambda o: pick(value, low ^ o, axis)
    gives = [block(o).astype(bf16) for o in range(1, size)]
    return [block(0)] + [swap(give, "rep", reps, o + 1) for o, give in enumerate(gives)]


def piece_of(rep, reps, size):
    row_part = 0
    for bit in range(log2(size), log2(reps)):
        row_part = 2 * row_part + ((rep >> bit) & 1)
    return row_part, rep & (size - 1)


def match_rounds(reps, kinds):
    left = {v: set(range(kinds)) for v in range(reps)}
    rounds = []
    for _ in range(kinds):
        owner = {}

        def place(v, seen):
            for kind in sorted(left[v]):
                target = (reps * kind + v) // kinds
                if target in seen:
                    continue
                seen.add(target)
                if target not in owner or place(owner[target][0], seen):
                    owner[target] = (v, kind)
                    return True
            return False

        for v in range(reps):
            place(v, set())
        chosen = [0] * reps
        for v, kind in owner.values():
            chosen[v] = kind
            left[v].discard(kind)
        rounds.append(chosen)
    return rounds


def mask_bias(bias_ref, bounds_ref, rank_ref, blocks):
    order = relative_order(blocks)
    tokens = bias_ref.shape[0] // blocks
    for block in range(blocks):
        for part in range(bias_ref.shape[1] // 128):
            lanes = slice(128 * part, 128 * (part + 1))
            shape = (tokens, 128)
            key_pos = (rank_ref[0] ^ order[block]) * tokens + lax.broadcasted_iota(jnp.int32, shape, 0)
            inside = (key_pos >= bounds_ref[0:1, lanes]) & (key_pos <= bounds_ref[1:2, lanes])
            bias_ref[pl.ds(block * tokens, tokens), lanes] = jnp.where(inside, 0.0, masked_score)


def attend_kernel(blocks, rank_ref, bounds_ref, query_ref, key_ref, value_ref, mixed_ref, total_ref, bias_ref):
    @pl.when(pl.program_id(0) == 0)
    def _():
        mask_bias(bias_ref, bounds_ref, rank_ref, blocks)

    keys = key_ref[...]
    values = value_ref[...]
    for part in range(query_ref.shape[1] // 128):
        lanes = slice(128 * part, 128 * (part + 1))
        queries = query_ref[:, lanes]
        scores = contract(keys, queries, 0, 0) * (1.0 / math.sqrt(HD)) + bias_ref[:, lanes]
        row_max = jnp.max(scores, axis=0, keepdims=True)
        weights = jnp.exp(scores - row_max)
        row_sum = jnp.sum(weights, axis=0, keepdims=True)
        total_ref[0, :, lanes] = row_max + jnp.log(row_sum)
        probs = (weights * (1.0 / row_sum)).astype(bf16)
        mixed_ref[:, lanes] = contract(values, probs, 1, 0).astype(bf16)


def attend_back_kernel(
    blocks,
    rank_ref,
    bounds_ref,
    query_ref,
    key_ref,
    value_ref,
    mixed_ref,
    grad_ref,
    total_ref,
    out_ref,
    bias_ref,
    probs_ref,
    slope_ref,
):
    @pl.when(pl.program_id(0) == 0)
    def _():
        mask_bias(bias_ref, bounds_ref, rank_ref, blocks)

    keys = key_ref[...]
    values = value_ref[...]
    scale = 1.0 / math.sqrt(HD)
    for part in range(query_ref.shape[1] // 128):
        lanes = slice(128 * part, 128 * (part + 1))
        queries = query_ref[:, lanes]
        grads = grad_ref[:, lanes]
        scores = contract(keys, queries, 0, 0) * scale + bias_ref[:, lanes]
        probs = jnp.exp(scores - total_ref[0, :, lanes])
        delta = jnp.sum(grads.astype(f32) * mixed_ref[:, lanes].astype(f32), axis=0, keepdims=True)
        grad_probs = contract(values, grads, 0, 0)
        slope = (probs * (grad_probs - delta) * scale).astype(bf16)
        probs_ref[:, lanes] = probs.astype(bf16)
        slope_ref[:, lanes] = slope
        out_ref[0, :, lanes] = contract(keys, slope, 1, 0).astype(bf16)
    slope = slope_ref[...]
    out_ref[1] = contract(query_ref[...], slope, 1, 1).astype(bf16)
    out_ref[2] = contract(grad_ref[...], probs_ref[...], 1, 1).astype(bf16)


def attend(projected, bounds, rank, blocks, heads):
    seq = projected.shape[1]
    row = lambda shift: pl.BlockSpec((HD, seq), lambda h, _: (h + shift, 0))
    return pl.pallas_call(
        lambda *refs: attend_kernel(blocks, *refs),
        grid_spec=pltpu.PrefetchScalarGridSpec(
            num_scalar_prefetch=1,
            grid=(heads,),
            in_specs=[pl.BlockSpec((8, seq), lambda h, _: (0, 0)), row(0), row(heads), row(2 * heads)],
            out_specs=[row(0), pl.BlockSpec((1, 1, seq), lambda h, _: (h, 0, 0))],
            scratch_shapes=[pltpu.VMEM((seq, seq), f32)],
        ),
        out_shape=[
            jax.ShapeDtypeStruct((heads * HD, seq), bf16),
            jax.ShapeDtypeStruct((heads, 1, seq), f32),
        ],
        cost_estimate=pl.CostEstimate(
            flops=4 * heads * seq * seq * HD,
            transcendentals=heads * seq * seq,
            bytes_accessed=8 * heads * HD * seq,
        ),
        name="attend",
    )(rank.reshape(1), bounds, projected, projected, projected)


def attend_back(projected, mixed, grad_mixed, totals, bounds, rank, blocks, heads):
    seq = projected.shape[1]
    row = lambda shift: pl.BlockSpec((HD, seq), lambda h, _: (h + shift, 0))
    return pl.pallas_call(
        lambda *refs: attend_back_kernel(blocks, *refs),
        grid_spec=pltpu.PrefetchScalarGridSpec(
            num_scalar_prefetch=1,
            grid=(heads,),
            in_specs=[
                pl.BlockSpec((8, seq), lambda h, _: (0, 0)),
                row(0),
                row(heads),
                row(2 * heads),
                row(0),
                row(0),
                pl.BlockSpec((1, 1, seq), lambda h, _: (h, 0, 0)),
            ],
            out_specs=pl.BlockSpec((3, HD, seq), lambda h, _: (0, h, 0)),
            scratch_shapes=[
                pltpu.VMEM((seq, seq), f32),
                pltpu.VMEM((seq, seq), bf16),
                pltpu.VMEM((seq, seq), bf16),
            ],
        ),
        out_shape=jax.ShapeDtypeStruct((3, heads * HD, seq), bf16),
        cost_estimate=pl.CostEstimate(
            flops=10 * heads * seq * seq * HD,
            transcendentals=heads * seq * seq,
            bytes_accessed=16 * heads * HD * seq,
        ),
        name="attend_back",
    )(rank.reshape(1), bounds, projected, projected, projected, mixed, grad_mixed, totals)


def shards(
    reps,
    size,
    tokens,
    segments,
    cotangent,
    packed_weight,
    output_weight,
    up_weight,
    down_weight,
    first_gain,
    first_shift,
    query_bias,
    value_bias,
    output_bias,
    second_gain,
    second_shift,
    hidden_bias,
    down_bias,
):
    rank = lax.axis_index("grp")
    rep_rank = lax.axis_index("rep")
    own = D // size
    hidden_own = hidden_bias.shape[0]
    hidden_all = hidden_own * size
    count = tokens.shape[1]
    seq = segments.shape[1]

    begins = [own * g // HD for g in range(size)]
    heads = max(-(-own * (g + 1) // HD) - begins[g] for g in range(size))
    width = heads * HD
    offsets = [own * g - HD * min(b, HEADS - heads) for g, b in enumerate(begins)]
    margin = max(max(offsets), max(width - own - o for o in offsets))
    begin = first_head(rank, size)
    if begins[-1] * HD > D - width:
        begin = jnp.minimum(begin, HEADS - heads)
    offset = rank * own - HD * begin

    order = relative_order(size)
    rows_own = tokens[0]
    rows_all = group_gather(rows_own, size)
    packed_give = pack_columns(packed_weight, begins, width, rank, size)
    packed_blocks = [packed_give[0]] + [None] * (size - 1)
    for j in reversed(range(1, size)):
        packed_blocks[j] = swap(packed_give[j], "grp", size, j)
    shorts = (
        first_gain,
        first_shift,
        query_bias,
        value_bias,
        output_bias,
        second_gain,
        second_shift,
        down_bias,
    )
    small = jnp.stack(tie(shorts, packed_give))
    kinds = small.shape[0]
    small = group_gather(small, size).reshape(size, kinds, own)
    vectors = jnp.zeros((size, kinds, own), bf16)
    for i, o in enumerate(order):
        vectors = put(vectors, small[i][None], rank ^ o, 0)
    vectors = vectors.transpose(1, 0, 2).reshape(kinds, D).astype(f32)
    packed_cols = place_rows(packed_blocks, rank)

    up_sets = jnp.stack([up_weight[:, hidden_own * g : hidden_own * (g + 1)] for g in range(size)])
    up_give = [pick(up_sets, rank ^ j, 0) for j in range(size)]
    moving = [up_give[j] for j in range(1, size)]
    moving, cot_held, packed_cols = lax.optimization_barrier((moving, cotangent[0], packed_cols))
    up_blocks = [up_give[0]] + [None] * (size - 1)
    for j in reversed(range(1, size)):
        up_blocks[j] = swap(moving[j - 1], "grp", size, j)
    up_cols = place_rows(up_blocks, rank)
    edge_low, edge_high = tie(
        (output_weight[:margin], output_weight[own - margin :]), up_blocks
    )
    grad_rows = group_gather(cot_held, size)
    ahead = lax.ppermute(edge_high, "grp", [(i, i + 1) for i in range(size - 1)])
    behind = lax.ppermute(edge_low, "grp", [(i + 1, i) for i in range(size - 1)])
    output_wide = cut(
        jnp.concatenate([ahead, output_weight, behind]), margin - offset, width, 0
    )
    wide_row = jnp.arange(width, dtype=jnp.int32)[:, None]
    wide_mine = (wide_row >= offset) & (wide_row < offset + own)
    output_mine = put(
        jnp.zeros((width, D), bf16), output_weight, offset, 0
    )

    segment_ids = segments[0]
    relative = lambda whole: jnp.concatenate(
        [cut(whole, (rank ^ o) * count, count, 0) for o in order]
    )
    position = relative(jnp.arange(seq, dtype=jnp.int32))
    segment_rows = relative(segment_ids)
    doc_begin = jnp.sum((segment_ids[:, None] < segment_rows[None, :]).astype(jnp.int32), axis=0)
    bounds = jnp.concatenate([doc_begin[None], position[None], jnp.zeros((6, seq), jnp.int32)])

    normal_a = (norm_rows(rows_all.astype(f32))[0] * vectors[0] + vectors[1]).astype(bf16)
    take = lambda vector: cut(vector, begin * HD, width, 0)
    packed_bias = jnp.concatenate([take(vectors[2]), jnp.zeros((width,), f32), take(vectors[3])])
    projected = (contract(packed_cols, normal_a, 0, 1) + packed_bias[:, None]).astype(bf16)
    mixed, totals = attend(projected, bounds, rank, size, heads)
    attn_part = contract(mixed, output_mine, 0, 0)
    rows_float = rows_own.astype(f32)
    residual = rows_float + group_scatter_sum(attn_part, size) + vectors[4]
    normed_second, inv_second = norm_rows(residual)
    normal_c_own = (normed_second * vectors[5] + vectors[6]).astype(bf16)
    normal_c = group_gather(normal_c_own, size)
    pre_act = contract(normal_c, up_cols, 1, 0) + hidden_bias.astype(f32)
    gelu_value, gelu_slope = gelu_parts(pre_act)
    hidden = gelu_value.astype(bf16)

    grad_hidden = contract(grad_rows, down_weight, 1, 1)
    grad_pre = (grad_hidden * gelu_slope).astype(bf16)
    grad_c_part = contract(grad_pre, up_cols, 1, 1)
    grad_c = group_scatter_sum(grad_c_part, size)
    grad_down = contract(grad_rows, hidden, 0, 0)
    grad_up = contract(normal_c, grad_pre, 0, 0)
    layer_part = contract(hidden, down_weight, 1, 0)

    share = reps // size
    low_bits, all_bits = log2(size), log2(reps)
    down_axis = lambda bit: all_bits - 1 - bit
    down_parts = halve_rows(natural_rows(grad_down, reps), 0, reps, down_axis(0))
    up_order = list(reversed(range(low_bits))) + list(range(low_bits, all_bits))
    up_parts = halve_rows(grad_up, up_order[0], reps, 0)

    grad_float = cotangent[0].astype(f32)
    grad_resid = grad_float + norm_back(grad_c, normed_second, inv_second, vectors[5])
    grad_attn_own = grad_resid.astype(bf16)
    grad_attn = group_gather(grad_attn_own, size)

    grad_mixed = contract(output_wide, grad_attn, 1, 1).astype(bf16)
    mixed_mine = cut(mixed, offset, own, 0)
    grad_output = contract(grad_attn, mixed_mine, 0, 1)
    out_parts = quad_step(grad_output.reshape(share, size, D // reps, own), 1, reps, size)
    down_parts = tie(down_parts, grad_mixed)
    up_parts = tie(up_parts, grad_mixed)
    for step in range(1, all_bits - 1):
        down_piece, up_piece = add_parts(down_parts, bf16), add_parts(up_parts, bf16)
        down_parts = halve_rows(down_piece, step, reps, down_axis(step))
        if step < low_bits:
            up_parts = halve_rows(up_piece, up_order[step], reps, 0)
        else:
            up_parts = halve_lanes(up_piece, up_order[step], reps)
    held = tie(grad_mixed, (down_parts[0], up_parts[0], out_parts[0]))
    grad_packed_rows = attend_back(projected, mixed, held, totals, bounds, rank, size, heads)
    grad_mine = cut(grad_packed_rows, offset, own, 1)
    grad_packed = contract(normal_a, grad_mine.reshape(3 * own, seq), 0, 1)
    packed_parts = quad_step(grad_packed.reshape(size, own, 3 * own), 0, reps, size)

    down_parts, up_parts = tie((down_parts, up_parts), packed_parts[0])
    down_last = halve_rows(add_parts(down_parts, bf16), all_bits - 1, reps, down_axis(all_bits - 1))
    up_last = halve_lanes(add_parts(up_parts, bf16), all_bits - 1, reps)

    grad_masked = jnp.where(wide_mine[None], grad_packed_rows, jnp.zeros_like(grad_packed_rows))
    grad_masked = tie(grad_masked, packed_parts[0])
    grad_a_part = contract(grad_masked.reshape(3 * width, seq), packed_cols, 0, 1)
    grad_a = group_scatter_sum(grad_a_part, size)
    out_parts = tie(out_parts, grad_a)
    out_piece = add_parts(out_parts, bf16)
    for bit in reversed(range(low_bits, all_bits)):
        out_piece = add_parts(halve_rows(out_piece, bit, reps, 0), f32)
    final_output = out_piece.reshape(D // reps, own).T
    layer_rows = residual + group_scatter_sum(layer_part, size) + vectors[7]
    normed_first, inv_first = norm_rows(rows_float)
    grad_in = grad_resid + norm_back(grad_a, normed_first, inv_first, vectors[0])

    def spread(values, length):
        return put(
            jnp.zeros((length,), f32), values, rank * values.shape[0], 0
        )

    sums = jnp.concatenate(
        [
            jnp.sum(grad_a * normed_first, axis=0),
            jnp.sum(grad_a, axis=0),
            spread(jnp.sum(grad_mine[0].astype(f32), axis=1), D),
            spread(jnp.sum(grad_mine[2].astype(f32), axis=1), D),
            jnp.sum(grad_attn_own.astype(f32), axis=0),
            jnp.sum(grad_c * normed_second, axis=0),
            jnp.sum(grad_c, axis=0),
            spread(jnp.sum(grad_pre.astype(f32), axis=0), hidden_all),
            jnp.sum(grad_float, axis=0),
        ]
    )
    sums_begun = sum_over(sums.reshape(-1, 128), "grp", size)

    piece = add_parts(tie(packed_parts, sums_begun), bf16)
    piece = jnp.stack([piece[:, own * t : own * (t + 1)] for t in range(3)])
    for bit in range(low_bits, all_bits):
        halves = halve_lanes(piece, bit, reps)
        piece = add_parts(halves, bf16)
    sums = sum_over(tie(sums_begun, piece), "rep", reps).reshape(-1)
    rounds = match_rounds(reps, 3)
    table = jnp.array(rounds, jnp.int32)
    unit = rank * share + piece_of(rep_rank, reps, size)[0]
    origin = [[0] * 3 for _ in range(reps)]
    received = []
    for turn, chosen in enumerate(rounds):
        route = []
        for r in range(reps):
            row_part, lane_part = piece_of(r, reps, size)
            for g in range(size):
                v = g * share + row_part
                where = reps * chosen[v] + v
                origin[where // 3][where % 3] = turn
                route.append((r * size + g, (where // 3) * size + lane_part))
        sent = pick(piece, table[turn, unit], 0)
        received.append(lax.ppermute(sent, ("rep", "grp"), route))
    down_last, up_last = tie((down_last, up_last), halves[0])
    final_down = add_parts(down_last, f32).reshape(D // reps, hidden_own).T
    route = []
    for r in range(reps):
        row_part, lane_part = piece_of(r, reps, size)
        for g in range(size):
            route.append((r * size + g, (g * share + row_part) * size + lane_part))
    final_up = lax.ppermute(add_parts(up_last, bf16), ("rep", "grp"), route).astype(f32)

    received = jnp.stack(received)
    owner = jnp.array(origin, jnp.int32)[rep_rank]
    final_packed = jnp.concatenate(
        [pick(received, owner[k], 0) for k in range(3)], axis=1
    ).astype(f32)

    ends = [D, 2 * D, 3 * D, 4 * D, 5 * D, 6 * D, 7 * D, 7 * D + hidden_all]
    return (
        layer_rows[None],
        grad_in[None],
        final_packed,
        final_output,
        final_up,
        final_down,
        *jnp.split(sums, ends),
    )


def solution(mesh):
    in_specs = (
        P("rep", "grp", None),
        P("rep", None),
        P("rep", "grp", None),
        P("grp", None),
        P("grp", None),
        P("grp", None),
        P("grp", None),
    ) + (P("grp"),) * 9
    out_specs = (
        P("rep", "grp", None),
        P("rep", "grp", None),
        P("grp", "rep"),
        P("grp", "rep"),
        P("grp", "rep"),
        P("grp", "rep"),
    ) + (P(),) * 9

    def body(*args):
        return shards(mesh.shape["rep"], mesh.shape["grp"], *args)

    return jax.shard_map(body, mesh=mesh, in_specs=in_specs, out_specs=out_specs, check_vma=False)
```

profile of v0, /device:TPU:0, one launch (start us, length us, event | category | flops | bytes accessed | tf_op | source)
XLA Modules:
  0.0 352.6 jit_solution(12735320813017799495)
XLA Ops:
  0.7 3.1 collective-permute-start.3
  3.7 3.1 pack_columns.1
  25.6 9.0 %collective-permute-done.5 = bf16[8,272]{1,0:T(8,128)(2,1)S(1)} collective-permute-done((bf16[8,272]{1,0:T(8,128)(2,1)S(1)}, bf16[8,272]{1,0:T(8,128)(2,1)S(1)}, u32[]{:S(2)}, u32[]{:S(2)}) %collective-permute-start.5) | collective-permute-done | bytes 4384 | tf_op jit(solution)/shard_map/ppermute | solution.py:54
  38.3 3.1 shard_map.289
  45.6 2.5 add_convert_fusion.2.refs_2_.refs_3_.refs_4_
  48.1 9.4 %attend.1 = (bf16[320,512]{1,0:T(8,128)(2,1)}, f32[5,1,512]{2,1,0:T(1,128)}) custom-call(s32[1]{0:T(128)} %bitcast.1.refs_0_.rank_ref, s32[8,512]{1,0:T(8,128)} %add_add_fusion.refs_1_, bf16[960,512]{1,0:T(8,128)(2,1)} %add_convert_fusion.2.refs_2_.refs_3_.refs_4_, bf16[960,512]{1,0:T(8,128)(2,1)} %add_convert_fusion.2.refs_2_.refs_3_.refs_4_, ...), custom_call_target="tpu_custom_call" | custom-call | flops 335544320 | bytes 1310720 | tf_op jit(solution)/shard_map/attend/pallas_call | solution.py:340
  70.1 4.1 %collective-permute-done.8 = bf16[128,1088]{0,1:T(8,128)(2,1)} collective-permute-done((bf16[128,1088]{0,1:T(8,128)(2,1)S(1)}, bf16[128,1088]{0,1:T(8,128)(2,1)}, u32[]{:S(2)}, u32[]{:S(2)}) %collective-permute-start.8) | collective-permute-done | bytes 278560 | tf_op jit(solution)/shard_map/ppermute | solution.py:54
  82.9 29.2 %collective-permute-done.9 = bf16[128,1088]{0,1:T(8,128)(2,1)S(1)} collective-permute-done((bf16[128,1088]{0,1:T(8,128)(2,1)S(1)}, bf16[128,1088]{0,1:T(8,128)(2,1)S(1)}, u32[]{:S(2)}, u32[]{:S(2)}) %collective-permute-start.9) | collective-permute-done | bytes 278560 | tf_op jit(solution)/shard_map/ppermute | solution.py:54
  114.1 3.1 collective-permute-start.20
  118.6 3.3 shard_map.290
  124.4 3.7 %convolution_add_fusion = f32[512,1088]{0,1:T(8,128)S(1)} fusion(bf16[1088,1088]{1,0:T(8,128)(2,1)} %shard_map.290, f32[1088]{0:T(1024)S(1)} %convert_element_type.231, bf16[256,1088]{0,1:T(8,128)(2,1)} %collective-permute-done.10, bf16[128,1088]{0,1:T(8,128)(2,1)} %copy-done.30, bf16[128,1088]{0,1:T(8,128)(2,1)} %copy-done.27), kind=kOutput, calls=%fused_computation.1 | convolution fusion | flops 1216053248 | bytes 5714176 | tf_op jit(solution)/shard_map/dot_general | solution.py:48
  130.0 2.8 convert_reduce_fusion.1
  144.0 6.5 %collective-permute-done.19 = bf16[128,1088]{0,1:T(8,128)(2,1)S(1)} collective-permute-done((bf16[128,1088]{0,1:T(8,128)(2,1)S(1)}, bf16[128,1088]{0,1:T(8,128)(2,1)S(1)}, u32[]{:S(2)}, u32[]{:S(2)}) %collective-permute-start.19) | collective-permute-done | bytes 278560 | tf_op jit(solution)/shard_map/ppermute | solution.py:54
  156.0 2.7 fusion.35
  158.8 3.6 %collective-permute-done.22 = bf16[128,1088]{0,1:T(8,128)(2,1)S(1)} collective-permute-done((bf16[128,1088]{0,1:T(8,128)(2,1)S(1)}, bf16[128,1088]{0,1:T(8,128)(2,1)S(1)}, u32[]{:S(2)}, u32[]{:S(2)}) %collective-permute-start.22) | collective-permute-done | bytes 278560 | tf_op jit(solution)/shard_map/ppermute | solution.py:54
  168.0 2.8 convolution_convert_fusion.refs_6_
  177.3 19.2 %collective-permute-done.25 = bf16[544,1088]{1,0:T(8,128)(2,1)S(1)} collective-permute-done((bf16[544,1088]{1,0:T(8,128)(2,1)}, bf16[544,1088]{1,0:T(8,128)(2,1)S(1)}, u32[]{:S(2)}, u32[]{:S(2)}) %collective-permute-start.25) | collective-permute-done | bytes 1183776 | tf_op jit(solution)/shard_map/ppermute | solution.py:54
  197.9 9.1 %attend_back.1 = bf16[3,320,512]{2,1,0:T(8,128)(2,1)} custom-call(s32[1]{0:T(128)} %bitcast.1.refs_0_.rank_ref, s32[8,512]{1,0:T(8,128)} %add_add_fusion.refs_1_, bf16[960,512]{1,0:T(8,128)(2,1)} %add_convert_fusion.2.refs_2_.refs_3_.refs_4_, bf16[960,512]{1,0:T(8,128)(2,1)} %add_convert_fusion.2.refs_2_.refs_3_.refs_4_, ...), custom_call_target="tpu_custom_call" | custom-call | flops 838860800 | bytes 2621440 | tf_op jit(solution)/shard_map/attend_back/pallas_call | solution.py:365
  228.0 13.0 %collective-permute-done.41 = bf16[2,1,1,136,1088]{4,3,2,1,0:T(8,128)(2,1)} collective-permute-done((bf16[2,1,1,136,1088]{4,3,2,1,0:T(8,128)(2,1)}, bf16[2,1,1,136,1088]{4,3,2,1,0:T(8,128)(2,1)}, u32[]{:S(2)}, u32[]{:S(2)}) %collective-permute-start.41) | collective-permute-done | bytes 591904 | tf_op jit(solution)/shard_map/ppermute | solution.py:54
  247.8 2.6 collective-permute-done.27
  255.8 2.6 collective-permute-start.43
  258.5 3.2 fusion.24
  264.8 3.3 collective-permute-done.32
  268.5 4.9 %collective-permute-done.30 = bf16[272,816]{1,0:T(8,128)(2,1)} collective-permute-done((bf16[272,816]{1,0:T(8,128)(2,1)}, bf16[272,816]{1,0:T(8,128)(2,1)}, u32[]{:S(2)}, u32[]{:S(2)}) %collective-permute-start.30) | collective-permute-done | bytes 443936 | tf_op jit(solution)/shard_map/ppermute | solution.py:54
  273.3 2.5 collective-permute-start.40
  275.8 7.8 %collective-permute-done.29 = bf16[272,816]{1,0:T(8,128)(2,1)} collective-permute-done((bf16[272,816]{1,0:T(8,128)(2,1)}, bf16[272,816]{1,0:T(8,128)(2,1)}, u32[]{:S(2)}, u32[]{:S(2)}) %collective-permute-start.29) | collective-permute-done | bytes 443936 | tf_op jit(solution)/shard_map/ppermute | solution.py:54
  286.9 20.7 %collective-permute-done.40 = bf16[1,136,272]{2,1,0:T(8,128)(2,1)S(1)} collective-permute-done((bf16[1,136,272]{2,1,0:T(8,128)(2,1)S(1)}, bf16[1,136,272]{2,1,0:T(8,128)(2,1)S(1)}, u32[]{:S(2)}, u32[]{:S(2)}) %collective-permute-start.40) | collective-permute-done | bytes 74016 | tf_op jit(solution)/shard_map/ppermute | solution.py:54
  308.4 7.2 %collective-permute-done.33 = bf16[3,272,136]{2,1,0:T(8,128)(2,1)S(1)} collective-permute-done((bf16[3,272,136]{2,1,0:T(8,128)(2,1)S(1)}, bf16[3,272,136]{2,1,0:T(8,128)(2,1)S(1)}, u32[]{:S(2)}, u32[]{:S(2)}) %collective-permute-start.33) | collective-permute-done | bytes 221984 | tf_op jit(solution)/shard_map/ppermute | solution.py:54
  319.9 5.0 %collective-permute-start.35 = (bf16[272,136]{1,0:T(8,128)(2,1)S(1)}, bf16[272,136]{1,0:T(8,128)(2,1)S(1)}, u32[]{:S(2)}, u32[]{:S(2)}) collective-permute-start(bf16[272,136]{1,0:T(8,128)(2,1)S(1)} %get-tuple-element.163), channel_id=1, source_target_pairs={{0,8},{1,0},{2,16},{3,28},{4,9},{5,1},{6,17},{7,29},{8,10},{9,2},{... | collective-permute-start | bytes 221960 | tf_op jit(solution)/shard_map/ppermute | solution.py:604
  327.7 4.6 %collective-permute-start.47 = (f32[102,128]{1,0:T(8,128)S(1)}, f32[102,128]{1,0:T(8,128)S(1)}, u32[]{:S(2)}, u32[]{:S(2)}) collective-permute-start(f32[102,128]{1,0:T(8,128)S(1)} %add.259), channel_id=1, source_target_pairs={{0,8},{4,12},{8,0},{12,4},{16,24},{20,28},{24,16},{28,20},{1,9},{5... | collective-permute-start | bytes 156680 | tf_op jit(solution)/shard_map/ppermute | solution.py:54
  334.3 9.1 %collective-permute-done.47 = f32[102,128]{1,0:T(8,128)S(1)} collective-permute-done((f32[102,128]{1,0:T(8,128)S(1)}, f32[102,128]{1,0:T(8,128)S(1)}, u32[]{:S(2)}, u32[]{:S(2)}) %collective-permute-start.47) | collective-permute-done | bytes 52256 | tf_op jit(solution)/shard_map/ppermute | solution.py:54
  344.5 5.8 %collective-permute-done.48 = f32[102,128]{1,0:T(8,128)S(1)} collective-permute-done((f32[102,128]{1,0:T(8,128)S(1)}, f32[102,128]{1,0:T(8,128)S(1)}, u32[]{:S(2)}, u32[]{:S(2)}) %collective-permute-start.48) | collective-permute-done | bytes 52256 | tf_op jit(solution)/shard_map/ppermute | solution.py:54
  (342 shorter events, 138.6 us)
Async XLA Ops:
  0.7 35.2 %collective-permute-start.3 = (bf16[128,1088]{0,1:T(8,128)(2,1)}, bf16[128,1088]{0,1:T(8,128)(2,1)S(1)}, u32[]{:S(2)}, u32[]{:S(2)}) collective-permute-start(bf16[128,1088]{0,1:T(8,128)(2,1)} %bitcast.152), channel_id=1, source_target_pairs={{0,2},{1,3},{2,0},{3,1},{4,6},{5,7},{6,4},{7,5},{8,10},{9,11},{10,... | collective-permute-start | bytes 835592 | tf_op jit(solution)/shard_map/ppermute | solution.py:54
  6.8 31.5 %collective-permute-start = (bf16[272,960]{1,0:T(8,128)(2,1)}, bf16[272,960]{1,0:T(8,128)(2,1)}, u32[]{:S(2)}, u32[]{:S(2)}) collective-permute-start(bf16[272,960]{1,0:T(8,128)(2,1)} %get-tuple-element.60), channel_id=1, source_target_pairs={{0,1},{1,0},{2,3},{3,2},{4,5},{5,4},{6,7},{7,6},{8,9},{9,8},{10,11... | collective-permute-start | bytes 1566728 | tf_op jit(solution)/shard_map/ppermute | solution.py:54
  6.8 31.5 %collective-permute-start.1 = (bf16[272,960]{1,0:T(8,128)(2,1)}, bf16[272,960]{1,0:T(8,128)(2,1)}, u32[]{:S(2)}, u32[]{:S(2)}) collective-permute-start(bf16[272,960]{1,0:T(8,128)(2,1)} %get-tuple-element.61), channel_id=1, source_target_pairs={{0,2},{1,3},{2,0},{3,1},{4,6},{5,7},{6,4},{7,5},{8,10},{9,11},{10,... | collective-permute-start | bytes 1566728 | tf_op jit(solution)/shard_map/ppermute | solution.py:54
  7.0 31.4 %collective-permute-start.2 = (bf16[272,960]{1,0:T(8,128)(2,1)}, bf16[272,960]{1,0:T(8,128)(2,1)}, u32[]{:S(2)}, u32[]{:S(2)}) collective-permute-start(bf16[272,960]{1,0:T(8,128)(2,1)} %get-tuple-element.62), channel_id=1, source_target_pairs={{0,3},{1,2},{2,1},{3,0},{4,7},{5,6},{6,5},{7,4},{8,11},{9,10},{10,... | collective-permute-start | bytes 1566728 | tf_op jit(solution)/shard_map/ppermute | solution.py:54
  14.2 20.4 %collective-permute-start.5 = (bf16[8,272]{1,0:T(8,128)(2,1)S(1)}, bf16[8,272]{1,0:T(8,128)(2,1)S(1)}, u32[]{:S(2)}, u32[]{:S(2)}) collective-permute-start(bf16[8,272]{1,0:T(8,128)(2,1)S(1)} %concatenate.63), channel_id=1, source_target_pairs={{0,2},{1,3},{2,0},{3,1},{4,6},{5,7},{6,4},{7,5},{8,10},{9,11},{10,... | collective-permute-start | bytes 13064 | tf_op jit(solution)/shard_map/ppermute | solution.py:54
  68.2 44.9 %collective-permute-start.11 = (bf16[272,1088]{1,0:T(8,128)(2,1)}, bf16[272,1088]{1,0:T(8,128)(2,1)}, u32[]{:S(2)}, u32[]{:S(2)}) collective-permute-start(bf16[272,1088]{1,0:T(8,128)(2,1)} %get-tuple-element.73), channel_id=1, source_target_pairs={{0,1},{1,0},{2,3},{3,2},{4,5},{5,4},{6,7},{7,6},{8,9},{9,8},{10,11... | collective-permute-start | bytes 1775624 | tf_op jit(solution)/shard_map/ppermute | solution.py:54
  68.2 44.9 %collective-permute-start.12 = (bf16[272,1088]{1,0:T(8,128)(2,1)}, bf16[272,1088]{1,0:T(8,128)(2,1)}, u32[]{:S(2)}, u32[]{:S(2)}) collective-permute-start(bf16[272,1088]{1,0:T(8,128)(2,1)} %get-tuple-element.74), channel_id=1, source_target_pairs={{0,2},{1,3},{2,0},{3,1},{4,6},{5,7},{6,4},{7,5},{8,10},{9,11},{10,... | collective-permute-start | bytes 1775624 | tf_op jit(solution)/shard_map/ppermute | solution.py:54
  70.0 43.1 %collective-permute-start.13 = (bf16[272,1088]{1,0:T(8,128)(2,1)}, bf16[272,1088]{1,0:T(8,128)(2,1)}, u32[]{:S(2)}, u32[]{:S(2)}) collective-permute-start(bf16[272,1088]{1,0:T(8,128)(2,1)} %get-tuple-element.75), channel_id=1, source_target_pairs={{0,3},{1,2},{2,1},{3,0},{4,7},{5,6},{6,5},{7,4},{8,11},{9,10},{10,... | collective-permute-start | bytes 1775624 | tf_op jit(solution)/shard_map/ppermute | solution.py:54
  76.1 36.0 %collective-permute-start.9 = (bf16[128,1088]{0,1:T(8,128)(2,1)S(1)}, bf16[128,1088]{0,1:T(8,128)(2,1)S(1)}, u32[]{:S(2)}, u32[]{:S(2)}) collective-permute-start(bf16[128,1088]{0,1:T(8,128)(2,1)S(1)} %add_convert_fusion.8), channel_id=1, source_target_pairs={{0,2},{1,3},{2,0},{3,1},{4,6},{5,7},{6,4},{7,5},{8,10},{9,11},{10,... | collective-permute-start | bytes 835592 | tf_op jit(solution)/shard_map/ppermute | solution.py:54
  81.9 40.0 %collective-permute-start.17 = (bf16[256,1088]{0,1:T(8,128)(2,1)}, bf16[256,1088]{0,1:T(8,128)(2,1)}, u32[]{:S(2)}, u32[]{:S(2)}) collective-permute-start(bf16[256,1088]{0,1:T(8,128)(2,1)} %pad_maximum_fusion.7), channel_id=1, source_target_pairs={{0,1},{1,0},{2,3},{3,2},{4,5},{5,4},{6,7},{7,6},{8,9},{9,8},{10,11... | collective-permute-start | bytes 1671176 | tf_op jit(solution)/shard_map/ppermute | solution.py:54
  114.1 52.2 %collective-permute-start.20 = (bf16[48,1088]{1,0:T(8,128)(2,1)}, bf16[48,1088]{1,0:T(8,128)(2,1)}, u32[]{:S(2)}, u32[]{:S(2)}) collective-permute-start(bf16[48,1088]{1,0:T(8,128)(2,1)} %get-tuple-element.77), channel_id=1, source_target_pairs={{0,1},{1,2},{2,3},{4,5},{5,6},{6,7},{8,9},{9,10},{10,11},{12,13},{... | collective-permute-start | bytes 313352 | tf_op jit(solution)/shard_map/ppermute | solution.py:472
  117.2 50.8 %collective-permute-start.21 = (bf16[48,1088]{1,0:T(8,128)(2,1)S(1)}, bf16[48,1088]{1,0:T(8,128)(2,1)}, u32[]{:S(2)}, u32[]{:S(2)}) collective-permute-start(bf16[48,1088]{1,0:T(8,128)(2,1)S(1)} %get-tuple-element.78), channel_id=1, source_target_pairs={{1,0},{2,1},{3,2},{5,4},{6,5},{7,6},{9,8},{10,9},{11,10},{13,12},{... | collective-permute-start | bytes 313352 | tf_op jit(solution)/shard_map/ppermute | solution.py:473
  136.8 76.7 %collective-permute-start.14 = (bf16[256,1088]{0,1:T(8,128)(2,1)}, bf16[256,1088]{0,1:T(8,128)(2,1)}, u32[]{:S(2)}, u32[]{:S(2)}) collective-permute-start(bf16[256,1088]{0,1:T(8,128)(2,1)} %slice.312), channel_id=1, source_target_pairs={{0,1},{1,0},{2,3},{3,2},{4,5},{5,4},{6,7},{7,6},{8,9},{9,8},{10,11... | collective-permute-start | bytes 1671176 | tf_op jit(solution)/shard_map/ppermute | solution.py:54
  139.9 30.9 %collective-permute-start.24 = (bf16[2,2,1,136,1088]{4,3,2,1,0:T(8,128)(2,1)}, bf16[2,2,1,136,1088]{4,3,2,1,0:T(8,128)(2,1)}, u32[]{:S(2)}, u32[]{:S(2)}) collective-permute-start(bf16[2,2,1,136,1088]{4,3,2,1,0:T(8,128)(2,1)} %dynamic-slice_convert_fusion.1), channel_id=1, source_target_pairs={{0,4},{4,0},{8,12},{12,8},{16,20},{20,16},{24,28},{28,24},{1,5},{5... | collective-permute-start | bytes 3551240 | tf_op jit(solution)/shard_map/ppermute | solution.py:54
  166.3 30.2 %collective-permute-start.25 = (bf16[544,1088]{1,0:T(8,128)(2,1)}, bf16[544,1088]{1,0:T(8,128)(2,1)S(1)}, u32[]{:S(2)}, u32[]{:S(2)}) collective-permute-start(bf16[544,1088]{1,0:T(8,128)(2,1)} %dynamic-slice_convert_fusion), channel_id=1, source_target_pairs={{0,8},{4,12},{8,0},{12,4},{16,24},{20,28},{24,16},{28,20},{1,9},{5... | collective-permute-start | bytes 3551240 | tf_op jit(solution)/shard_map/ppermute | solution.py:54
  216.5 41.9 %collective-permute-start.15 = (bf16[128,1088]{0,1:T(8,128)(2,1)}, bf16[128,1088]{0,1:T(8,128)(2,1)}, u32[]{:S(2)}, u32[]{:S(2)}) collective-permute-start(bf16[128,1088]{0,1:T(8,128)(2,1)} %slice.316), channel_id=1, source_target_pairs={{0,2},{1,3},{2,0},{3,1},{4,6},{5,7},{6,4},{7,5},{8,10},{9,11},{10,... | collective-permute-start | bytes 835592 | tf_op jit(solution)/shard_map/ppermute | solution.py:54
  219.9 33.3 %collective-permute-start.39 = (bf16[2,136,272]{2,1,0:T(8,128)(2,1)}, bf16[2,136,272]{2,1,0:T(8,128)(2,1)S(1)}, u32[]{:S(2)}, u32[]{:S(2)}) collective-permute-start(bf16[2,136,272]{2,1,0:T(8,128)(2,1)} %get-tuple-element.140), channel_id=1, source_target_pairs={{0,12},{4,8},{8,4},{12,0},{16,28},{20,24},{24,20},{28,16},{1,13},{... | collective-permute-start | bytes 443912 | tf_op jit(solution)/shard_map/ppermute | solution.py:54
  221.5 19.5 %collective-permute-start.41 = (bf16[2,1,1,136,1088]{4,3,2,1,0:T(8,128)(2,1)}, bf16[2,1,1,136,1088]{4,3,2,1,0:T(8,128)(2,1)}, u32[]{:S(2)}, u32[]{:S(2)}) collective-permute-start(bf16[2,1,1,136,1088]{4,3,2,1,0:T(8,128)(2,1)} %get-tuple-element.145), channel_id=1, source_target_pairs={{0,8},{4,12},{8,0},{12,4},{16,24},{20,28},{24,16},{28,20},{1,9},{5... | collective-permute-start | bytes 1775624 | tf_op jit(solution)/shard_map/ppermute | solution.py:54
  221.9 20.6 %collective-permute-start.42 = (bf16[272,1088]{1,0:T(8,128)(2,1)}, bf16[272,1088]{1,0:T(8,128)(2,1)}, u32[]{:S(2)}, u32[]{:S(2)}) collective-permute-start(bf16[272,1088]{1,0:T(8,128)(2,1)} %get-tuple-element.143), channel_id=1, source_target_pairs={{0,4},{4,0},{8,12},{12,8},{16,20},{20,16},{24,28},{28,24},{1,5},{5... | collective-permute-start | bytes 1775624 | tf_op jit(solution)/shard_map/ppermute | solution.py:54
  225.8 28.6 %collective-permute-start.37 = (bf16[2,136,272]{2,1,0:T(8,128)(2,1)}, bf16[2,136,272]{2,1,0:T(8,128)(2,1)S(1)}, u32[]{:S(2)}, u32[]{:S(2)}) collective-permute-start(bf16[2,136,272]{2,1,0:T(8,128)(2,1)} %get-tuple-element.141), channel_id=1, source_target_pairs={{0,4},{4,0},{8,12},{12,8},{16,20},{20,16},{24,28},{28,24},{1,5},{5... | collective-permute-start | bytes 443912 | tf_op jit(solution)/shard_map/ppermute | solution.py:54
  241.0 14.2 %collective-permute-start.38 = (bf16[2,136,272]{2,1,0:T(8,128)(2,1)}, bf16[2,136,272]{2,1,0:T(8,128)(2,1)S(1)}, u32[]{:S(2)}, u32[]{:S(2)}) collective-permute-start(bf16[2,136,272]{2,1,0:T(8,128)(2,1)} %get-tuple-element.142), channel_id=1, source_target_pairs={{0,8},{4,12},{8,0},{12,4},{16,24},{20,28},{24,16},{28,20},{1,9},{5... | collective-permute-start | bytes 443912 | tf_op jit(solution)/shard_map/ppermute | solution.py:54
  250.4 22.9 %collective-permute-start.30 = (bf16[272,816]{1,0:T(8,128)(2,1)}, bf16[272,816]{1,0:T(8,128)(2,1)}, u32[]{:S(2)}, u32[]{:S(2)}) collective-permute-start(bf16[272,816]{1,0:T(8,128)(2,1)} %get-tuple-element.129), channel_id=1, source_target_pairs={{0,12},{4,8},{8,4},{12,0},{16,28},{20,24},{24,20},{28,16},{1,13},{... | collective-permute-start | bytes 1331720 | tf_op jit(solution)/shard_map/ppermute | solution.py:54
  253.2 30.5 %collective-permute-start.29 = (bf16[272,816]{1,0:T(8,128)(2,1)}, bf16[272,816]{1,0:T(8,128)(2,1)}, u32[]{:S(2)}, u32[]{:S(2)}) collective-permute-start(bf16[272,816]{1,0:T(8,128)(2,1)} %get-tuple-element.130), channel_id=1, source_target_pairs={{0,8},{4,12},{8,0},{12,4},{16,24},{20,28},{24,16},{28,20},{1,9},{5... | collective-permute-start | bytes 1331720 | tf_op jit(solution)/shard_map/ppermute | solution.py:54
  254.4 29.3 %collective-permute-start.28 = (bf16[272,816]{1,0:T(8,128)(2,1)S(1)}, bf16[272,816]{1,0:T(8,128)(2,1)}, u32[]{:S(2)}, u32[]{:S(2)}) collective-permute-start(bf16[272,816]{1,0:T(8,128)(2,1)S(1)} %get-tuple-element.131), channel_id=1, source_target_pairs={{0,4},{4,0},{8,12},{12,8},{16,20},{20,16},{24,28},{28,24},{1,5},{5... | collective-permute-start | bytes 1331720 | tf_op jit(solution)/shard_map/ppermute | solution.py:54
  255.8 64.0 %collective-permute-start.43 = (bf16[1,1,1,136,1088]{4,3,2,1,0:T(8,128)(2,1)}, bf16[1,1,1,136,1088]{4,3,2,1,0:T(8,128)(2,1)}, u32[]{:S(2)}, u32[]{:S(2)}) collective-permute-start(bf16[1,1,1,136,1088]{4,3,2,1,0:T(8,128)(2,1)} %get-tuple-element.149), channel_id=1, source_target_pairs={{0,16},{4,20},{8,24},{12,28},{16,0},{20,4},{24,8},{28,12},{1,17},{... | collective-permute-start | bytes 887816 | tf_op jit(solution)/shard_map/ppermute | solution.py:54
  268.1 56.7 %collective-permute-start.44 = (bf16[272,544]{1,0:T(8,128)(2,1)}, bf16[272,544]{1,0:T(8,128)(2,1)S(1)}, u32[]{:S(2)}, u32[]{:S(2)}) collective-permute-start(bf16[272,544]{1,0:T(8,128)(2,1)} %get-tuple-element.147), channel_id=1, source_target_pairs={{0,16},{4,20},{8,24},{12,28},{16,0},{20,4},{24,8},{28,12},{1,17},{... | collective-permute-start | bytes 887816 | tf_op jit(solution)/shard_map/ppermute | solution.py:54
  273.3 34.3 %collective-permute-start.40 = (bf16[1,136,272]{2,1,0:T(8,128)(2,1)S(1)}, bf16[1,136,272]{2,1,0:T(8,128)(2,1)S(1)}, u32[]{:S(2)}, u32[]{:S(2)}) collective-permute-start(bf16[1,136,272]{2,1,0:T(8,128)(2,1)S(1)} %constant_dynamic-slice_fusion.4), channel_id=1, source_target_pairs={{0,16},{4,20},{8,24},{12,28},{16,0},{20,4},{24,8},{28,12},{1,17},{... | collective-permute-start | bytes 221960 | tf_op jit(solution)/shard_map/ppermute | solution.py:54
  285.8 29.8 %collective-permute-start.33 = (bf16[3,272,136]{2,1,0:T(8,128)(2,1)S(1)}, bf16[3,272,136]{2,1,0:T(8,128)(2,1)S(1)}, u32[]{:S(2)}, u32[]{:S(2)}) collective-permute-start(bf16[3,272,136]{2,1,0:T(8,128)(2,1)S(1)} %broadcast_select_fusion.1), channel_id=1, source_target_pairs={{0,16},{4,20},{8,24},{12,28},{16,0},{20,4},{24,8},{28,12},{1,17},{... | collective-permute-start | bytes 665864 | tf_op jit(solution)/shard_map/ppermute | solution.py:54
  319.1 13.2 %collective-permute-start.34 = (bf16[272,136]{1,0:T(8,128)(2,1)S(1)}, bf16[272,136]{1,0:T(8,128)(2,1)S(1)}, u32[]{:S(2)}, u32[]{:S(2)}) collective-permute-start(bf16[272,136]{1,0:T(8,128)(2,1)S(1)} %get-tuple-element.161), channel_id=1, source_target_pairs={{0,20},{1,24},{2,4},{3,16},{4,21},{5,25},{6,5},{7,17},{8,22},{9,26... | collective-permute-start | bytes 221960 | tf_op jit(solution)/shard_map/ppermute | solution.py:604
  319.2 13.1 %collective-permute-start.36 = (bf16[272,136]{1,0:T(8,128)(2,1)S(1)}, bf16[272,136]{1,0:T(8,128)(2,1)S(1)}, u32[]{:S(2)}, u32[]{:S(2)}) collective-permute-start(bf16[272,136]{1,0:T(8,128)(2,1)S(1)} %get-tuple-element.162), channel_id=1, source_target_pairs={{0,0},{1,12},{2,24},{3,8},{4,1},{5,13},{6,25},{7,9},{8,2},{9,14},{... | collective-permute-start | bytes 221960 | tf_op jit(solution)/shard_map/ppermute | solution.py:604
  324.9 26.7 %collective-permute-start.45 = (bf16[272,544]{1,0:T(8,128)(2,1)S(1)}, bf16[272,544]{1,0:T(8,128)(2,1)S(1)}, u32[]{:S(2)}, u32[]{:S(2)}) collective-permute-start(bf16[272,544]{1,0:T(8,128)(2,1)S(1)} %add_convert_fusion.7), channel_id=1, source_target_pairs={{0,0},{1,8},{2,16},{3,24},{4,1},{5,9},{6,17},{7,25},{8,2},{9,10},{... | collective-permute-start | bytes 887816 | tf_op jit(solution)/shard_map/ppermute | solution.py:612
  327.7 15.8 %collective-permute-start.47 = (f32[102,128]{1,0:T(8,128)S(1)}, f32[102,128]{1,0:T(8,128)S(1)}, u32[]{:S(2)}, u32[]{:S(2)}) collective-permute-start(f32[102,128]{1,0:T(8,128)S(1)} %add.259), channel_id=1, source_target_pairs={{0,8},{4,12},{8,0},{12,4},{16,24},{20,28},{24,16},{28,20},{1,9},{5... | collective-permute-start | bytes 156680 | tf_op jit(solution)/shard_map/ppermute | solution.py:54
  (76 other events, 924.3 us)
where the time goes:
time: 354 us; the launch traced here: 353 us
  waiting for transfers between devices  149 us (42%)
  starting transfers between devices  55.7 us (16%)
  local copies, waits for them, and re-layouts  54 us (15%)
  other arithmetic  37.7 us (11%)
  Pallas kernels  28 us (8%)
  matrix products  26.1 us (7%)
    ppermute x43, waiting for transfers between devices, swap(): return lax.ppermute(value, axis, [(i, i ^ bit) for i in range(size)])  149 us
    ppermute x43, starting transfers between devices, swap(): return lax.ppermute(value, axis, [(i, i ^ bit) for i in range(size)])  44.9 us
    dot_general x12, matrix products, contract(): lax.dot_general(left, right, (((left_dim,), (right_dim,)), ((), ())), pre...  26.1 us
    unnamed x120, local copies, waits for them, and re-layouts  9.68 us
    pallas_call x1, Pallas kernels, attend(): pl.pallas_call(lambda *refs: attend_kernel(blocks, *refs), grid_spec=pltp...  9.37 us
    pallas_call x1, Pallas kernels, attend_back(): pl.pallas_call(lambda *refs: attend_back_kernel(blocks, *refs), grid_spec...  9.12 us
    dynamic_slice x13, local copies, waits for them, and re-layouts, cut(): return lax.dynamic_slice(value, starts, sizes, allow_negative_indices=False)  7.28 us
    convert_element_type x8, other arithmetic, add_parts(): return total.astype(dtype)  7.23 us
  transfers between devices with their start and end apart: 49, of which 18 were waited for; matrix products, arithmetic and copies ran while one was open for 28% of the time, Pallas kernels for 5%

commit v1 on v0

--- a/solution.py
+++ b/solution.py
@@ -28,11 +28,16 @@
     return (gelu_value, gelu_slope)
 
 
-def norm_rows(field):
+def row_stats(field):
     row_mean = jnp.mean(field, axis=-1, keepdims=True)
     centered = field - row_mean
     inv_std = lax.rsqrt(jnp.mean(centered * centered, axis=-1, keepdims=True) + epsilon)
-    return (centered * inv_std, inv_std)
+    return (row_mean, inv_std)
+
+
+def norm_rows(field):
+    row_mean, inv_std = row_stats(field)
+    return ((field - row_mean) * inv_std, inv_std)
 
 
 def norm_back(grad_out, normed, inv_std, gain_row):
@@ -107,34 +112,39 @@
     return value
 
 
-def place_kernel(rank_ref, *refs):
+def place_of(j, flip, size):
+    return j ^ flip if 2 * j >= size else j
+
+
+def place_kernel(rank_ref, flip_ref, *refs):
     out_ref = refs[-1]
     for j, ref in enumerate(refs[:-1]):
         rows = ref.shape[0]
-        out_ref[pl.ds(pl.multiple_of((rank_ref[0] ^ j) * rows, 16), rows), :] = ref[...]
-
-
-def place_rows(blocks, rank):
+        place = rank_ref[0] ^ place_of(j, flip_ref[0], len(refs) - 1)
+        out_ref[pl.ds(pl.multiple_of(place * rows, 16), rows), :] = ref[...]
+
+
+def place_rows(blocks, rank, flip):
     rows, cols = blocks[0].shape
     size = len(blocks)
     if rows % 16:
         whole = jnp.zeros((rows * size, cols), blocks[0].dtype)
         for j, block in enumerate(blocks):
-            whole = put(whole, block, (rank ^ j) * rows, 0)
+            whole = put(whole, block, (rank ^ place_of(j, flip, size)) * rows, 0)
         return whole
     return pl.pallas_call(
         place_kernel,
         grid_spec=pltpu.PrefetchScalarGridSpec(
-            num_scalar_prefetch=1,
+            num_scalar_prefetch=2,
             grid=(1,),
-            in_specs=[pl.BlockSpec((rows, cols), lambda i, _: (0, 0))] * size,
-            out_specs=pl.BlockSpec((rows * size, cols), lambda i, _: (0, 0)),
+            in_specs=[pl.BlockSpec((rows, cols), lambda i, *_: (0, 0))] * size,
+            out_specs=pl.BlockSpec((rows * size, cols), lambda i, *_: (0, 0)),
         ),
         out_shape=jax.ShapeDtypeStruct((rows * size, cols), blocks[0].dtype),
         cost_estimate=pl.CostEstimate(
             flops=0, transcendentals=0, bytes_accessed=4 * rows * size * cols
         ),
-    )(rank.reshape(1), *blocks)
+    )(rank.reshape(1), flip.reshape(1), *blocks)
 
 
 def first_head(rank, size):
@@ -433,7 +443,8 @@
 
     order = relative_order(size)
     rows_own = tokens[0]
-    rows_all = group_gather(rows_own, size)
+    rows_all = group_gather(rows_own, size).astype(f32)
+    row_mean, row_inv = row_stats(rows_all)
     packed_give = pack_columns(packed_weight, begins, width, rank, size)
     packed_blocks = [packed_give[0]] + [None] * (size - 1)
     for j in reversed(range(1, size)):
@@ -455,22 +466,24 @@
     for i, o in enumerate(order):
         vectors = put(vectors, small[i][None], rank ^ o, 0)
     vectors = vectors.transpose(1, 0, 2).reshape(kinds, D).astype(f32)
-    packed_cols = place_rows(packed_blocks, rank)
+    packed_cols = place_rows(packed_blocks, rank, jnp.zeros((), jnp.int32))
 
     up_sets = jnp.stack([up_weight[:, hidden_own * g : hidden_own * (g + 1)] for g in range(size)])
-    up_give = [pick(up_sets, rank ^ j, 0) for j in range(size)]
-    moving = [up_give[j] for j in range(1, size)]
-    moving, cot_held, packed_cols = lax.optimization_barrier((moving, cotangent[0], packed_cols))
-    up_blocks = [up_give[0]] + [None] * (size - 1)
-    for j in reversed(range(1, size)):
-        up_blocks[j] = swap(moving[j - 1], "grp", size, j)
-    up_cols = place_rows(up_blocks, rank)
-    edge_low, edge_high = tie(
-        (output_weight[:margin], output_weight[own - margin :]), up_blocks
-    )
-    grad_rows = group_gather(cot_held, size)
-    ahead = lax.ppermute(edge_high, "grp", [(i, i + 1) for i in range(size - 1)])
-    behind = lax.ppermute(edge_low, "grp", [(i + 1, i) for i in range(size - 1)])
+    flip = rep_rank & 1 if size == 4 else jnp.zeros((), jnp.int32)
+    up_blocks = [pick(up_sets, rank, 0)] + [None] * (size - 1)
+    if size == 4:
+        route = [(r * 4 + g, r * 4 + (g ^ 2 ^ (r & 1))) for r in range(reps) for g in range(4)]
+        up_blocks[2] = lax.ppermute(pick(up_sets, rank ^ 2 ^ flip, 0), ("rep", "grp"), route)
+        up_blocks[1] = swap(pick(up_sets, rank ^ 1, 0), "grp", size, 1)
+        up_blocks[3] = swap(up_blocks[2], "rep", reps, 1)
+    else:
+        for j in range(1, size):
+            up_blocks[j] = swap(pick(up_sets, rank ^ j, 0), "grp", size, j)
+    up_cols = place_rows(up_blocks, rank, flip)
+    grad_rows = group_gather(cotangent[0], size)
+    edge_pairs = [(i, i + 1) for i in range(size - 1)]
+    ahead = lax.ppermute(output_weight[own - margin :], "grp", edge_pairs)
+    behind = lax.ppermute(output_weight[:margin], "grp", [(j, i) for i, j in edge_pairs])
     output_wide = cut(
         jnp.concatenate([ahead, output_weight, behind]), margin - offset, width, 0
     )
@@ -489,7 +502,7 @@
     doc_begin = jnp.sum((segment_ids[:, None] < segment_rows[None, :]).astype(jnp.int32), axis=0)
     bounds = jnp.concatenate([doc_begin[None], position[None], jnp.zeros((6, seq), jnp.int32)])
 
-    normal_a = (norm_rows(rows_all.astype(f32))[0] * vectors[0] + vectors[1]).astype(bf16)
+    normal_a = ((rows_all - row_mean) * row_inv * vectors[0] + vectors[1]).astype(bf16)
     take = lambda vector: cut(vector, begin * HD, width, 0)
     packed_bias = jnp.concatenate([take(vectors[2]), jnp.zeros((width,), f32), take(vectors[3])])
     projected = (contract(packed_cols, normal_a, 0, 1) + packed_bias[:, None]).astype(bf16)
@@ -525,37 +538,29 @@
     grad_attn = group_gather(grad_attn_own, size)
 
     grad_mixed = contract(output_wide, grad_attn, 1, 1).astype(bf16)
-    mixed_mine = cut(mixed, offset, own, 0)
-    grad_output = contract(grad_attn, mixed_mine, 0, 1)
-    out_parts = quad_step(grad_output.reshape(share, size, D // reps, own), 1, reps, size)
-    down_parts = tie(down_parts, grad_mixed)
-    up_parts = tie(up_parts, grad_mixed)
     for step in range(1, all_bits - 1):
-        down_piece, up_piece = add_parts(down_parts, bf16), add_parts(up_parts, bf16)
-        down_parts = halve_rows(down_piece, step, reps, down_axis(step))
+        down_parts = halve_rows(add_parts(down_parts, bf16), step, reps, down_axis(step))
+    held = grad_mixed
+    grad_packed_rows = attend_back(projected, mixed, held, totals, bounds, rank, size, heads)
+    grad_mine = cut(grad_packed_rows, offset, own, 1)
+    grad_packed = contract(normal_a, grad_mine.reshape(3 * own, seq), 0, 1)
+    packed_parts = quad_step(grad_packed.reshape(size, own, 3 * own), 0, reps, size)
+
+    down_last = halve_rows(add_parts(down_parts, bf16), all_bits - 1, reps, down_axis(all_bits - 1))
+    for step in range(1, all_bits - 1):
+        up_piece = add_parts(up_parts, bf16)
         if step < low_bits:
             up_parts = halve_rows(up_piece, up_order[step], reps, 0)
         else:
             up_parts = halve_lanes(up_piece, up_order[step], reps)
-    held = tie(grad_mixed, (down_parts[0], up_parts[0], out_parts[0]))
-    grad_packed_rows = attend_back(projected, mixed, held, totals, bounds, rank, size, heads)
-    grad_mine = cut(grad_packed_rows, offset, own, 1)
-    grad_packed = contract(normal_a, grad_mine.reshape(3 * own, seq), 0, 1)
-    packed_parts = quad_step(grad_packed.reshape(size, own, 3 * own), 0, reps, size)
-
-    down_parts, up_parts = tie((down_parts, up_parts), packed_parts[0])
-    down_last = halve_rows(add_parts(down_parts, bf16), all_bits - 1, reps, down_axis(all_bits - 1))
-    up_last = halve_lanes(add_parts(up_parts, bf16), all_bits - 1, reps)
 
     grad_masked = jnp.where(wide_mine[None], grad_packed_rows, jnp.zeros_like(grad_packed_rows))
-    grad_masked = tie(grad_masked, packed_parts[0])
     grad_a_part = contract(grad_masked.reshape(3 * width, seq), packed_cols, 0, 1)
     grad_a = group_scatter_sum(grad_a_part, size)
-    out_parts = tie(out_parts, grad_a)
-    out_piece = add_parts(out_parts, bf16)
-    for bit in reversed(range(low_bits, all_bits)):
-        out_piece = add_parts(halve_rows(out_piece, bit, reps, 0), f32)
-    final_output = out_piece.reshape(D // reps, own).T
+    mixed_mine = cut(mixed, offset, own, 0)
+    grad_output = contract(grad_attn, mixed_mine, 0, 1)
+    out_parts = quad_step(grad_output.reshape(share, size, D // reps, own), 1, reps, size)
+    up_last = halve_lanes(add_parts(up_parts, bf16), all_bits - 1, reps)
     layer_rows = residual + group_scatter_sum(layer_part, size) + vectors[7]
     normed_first, inv_first = norm_rows(rows_float)
     grad_in = grad_resid + norm_back(grad_a, normed_first, inv_first, vectors[0])
@@ -578,14 +583,14 @@
             jnp.sum(grad_float, axis=0),
         ]
     )
-    sums_begun = sum_over(sums.reshape(-1, 128), "grp", size)
-
-    piece = add_parts(tie(packed_parts, sums_begun), bf16)
+    sums = sum_over(sum_over(sums.reshape(-1, 128), "grp", size), "rep", reps)
+
+    packed_parts, sums = lax.optimization_barrier((packed_parts, sums))
+    piece = add_parts(packed_parts, bf16)
     piece = jnp.stack([piece[:, own * t : own * (t + 1)] for t in range(3)])
     for bit in range(low_bits, all_bits):
         halves = halve_lanes(piece, bit, reps)
         piece = add_parts(halves, bf16)
-    sums = sum_over(tie(sums_begun, piece), "rep", reps).reshape(-1)
     rounds = match_rounds(reps, 3)
     table = jnp.array(rounds, jnp.int32)
     unit = rank * share + piece_of(rep_rank, reps, size)[0]
@@ -602,7 +607,10 @@
                 route.append((r * size + g, (where // 3) * size + lane_part))
         sent = pick(piece, table[turn, unit], 0)
         received.append(lax.ppermute(sent, ("rep", "grp"), route))
-    down_last, up_last = tie((down_last, up_last), halves[0])
+    out_piece = add_parts(out_parts, bf16)
+    for bit in reversed(range(low_bits, all_bits)):
+        out_piece = add_parts(halve_rows(out_piece, bit, reps, 0), f32)
+    final_output = out_piece.reshape(D // reps, own).T
     final_down = add_parts(down_last, f32).reshape(D // reps, hidden_own).T
     route = []
     for r in range(reps):
@@ -625,7 +633,7 @@
         final_output,
         final_up,
         final_down,
-        *jnp.split(sums, ends),
+        *jnp.split(sums.reshape(-1), ends),
     )
 
 

time: 354 us -> 343 us (0.969)
  the two profiles are of different devices: /device:TPU:0 before, /device:TPU:1 now
where the time goes in v1:
time: 343 us; the launch traced here: 342 us
  waiting for transfers between devices  136 us (40%)
  starting transfers between devices  64.8 us (19%)
  local copies, waits for them, and re-layouts  45.7 us (13%)
  other arithmetic  36.9 us (11%)
  matrix products  28.9 us (8%)
  Pallas kernels  28 us (8%)
    ppermute x42, waiting for transfers between devices, swap(): return lax.ppermute(value, axis, [(i, i ^ bit) for i in range(size)])  126 us
    ppermute x42, starting transfers between devices, swap(): return lax.ppermute(value, axis, [(i, i ^ bit) for i in range(size)])  42.6 us
    dot_general x12, matrix products, contract(): lax.dot_general(left, right, (((left_dim,), (right_dim,)), ((), ())), pre...  28.9 us
    ppermute x3, starting transfers between devices, shards(): received.append(lax.ppermute(sent, ('rep', 'grp'), route))  12.8 us
    pallas_call x1, Pallas kernels, attend(): pl.pallas_call(lambda *refs: attend_kernel(blocks, *refs), grid_spec=pltp...  9.38 us
    pallas_call x1, Pallas kernels, attend_back(): pl.pallas_call(lambda *refs: attend_back_kernel(blocks, *refs), grid_spec...  9.02 us
    convert_element_type x8, other arithmetic, add_parts(): return total.astype(dtype)  8.5 us
  transfers between devices with their start and end apart: 49, of which 19 were waited for; matrix products, arithmetic and copies ran while one was open for 27% of the time, Pallas kernels for 4%

profile of v1, /device:TPU:1, one launch (start us, length us, event | category | flops | bytes accessed | tf_op | source)
XLA Modules:
  0.0 342.1 jit_solution(16344059810437500900)
XLA Ops:
  0.7 3.2 pack_columns.1
  3.9 2.7 collective-permute-start.1
  15.0 3.9 %slice_bitcast_fusion.3 = (bf16[1,272,1088]{2,1,0:T(8,128)(2,1)}, bf16[1,272,1088]{2,1,0:T(8,128)(2,1)}, bf16[1,272,1088]{2,1,0:T(8,128)(2,1)}, bf16[1,272,1088]{2,1,0:T(8,128)(2,1)}) fusion(bf16[272,4352]{1,0:T(8,128)(2,1)} %param.23), kind=kLoop, calls=%fused_computation.73 | loop fusion | bytes 4734976 | tf_op jit(solution)/shard_map/stack | solution.py:471
  21.6 10.3 %collective-permute-done.5 = bf16[8,272]{1,0:T(8,128)(2,1)S(1)} collective-permute-done((bf16[8,272]{1,0:T(8,128)(2,1)S(1)}, bf16[8,272]{1,0:T(8,128)(2,1)S(1)}, u32[]{:S(2)}, u32[]{:S(2)}) %collective-permute-start.5) | collective-permute-done | bytes 4384 | tf_op jit(solution)/shard_map/ppermute | solution.py:59
  33.6 4.3 %collective-permute-done.3 = bf16[128,1088]{0,1:T(8,128)(2,1)S(1)} collective-permute-done((bf16[128,1088]{0,1:T(8,128)(2,1)}, bf16[128,1088]{0,1:T(8,128)(2,1)S(1)}, u32[]{:S(2)}, u32[]{:S(2)}) %collective-permute-start.3) | collective-permute-done | bytes 278560 | tf_op jit(solution)/shard_map/ppermute | solution.py:59
  40.8 3.1 shard_map.289
  50.3 9.4 %attend.1 = (bf16[320,512]{1,0:T(8,128)(2,1)}, f32[5,1,512]{2,1,0:T(1,128)}) custom-call(s32[1]{0:T(128)} %bitcast.1.refs_0_.rank_ref, s32[8,512]{1,0:T(8,128)} %add_add_fusion.refs_1_, bf16[960,512]{1,0:T(8,128)(2,1)} %add_convert_fusion.2.refs_2_.refs_3_.refs_4_, bf16[960,512]{1,0:T(8,128)(2,1)} %add_convert_fusion.2.refs_2_.refs_3_.refs_4_, ...), custom_call_target="tpu_custom_call" | custom-call | flops 335544320 | bytes 1310720 | tf_op jit(solution)/shard_map/attend/pallas_call | solution.py:350
  67.2 18.2 %collective-permute-done.8 = bf16[128,1088]{0,1:T(8,128)(2,1)} collective-permute-done((bf16[128,1088]{0,1:T(8,128)(2,1)S(1)}, bf16[128,1088]{0,1:T(8,128)(2,1)}, u32[]{:S(2)}, u32[]{:S(2)}) %collective-permute-start.8) | collective-permute-done | bytes 278560 | tf_op jit(solution)/shard_map/ppermute | solution.py:59
  91.1 3.4 collective-permute-start.20
  108.0 4.9 %collective-permute-done.13.refs_3_ = bf16[272,1088]{1,0:T(8,128)(2,1)} collective-permute-done((bf16[272,1088]{1,0:T(8,128)(2,1)}, bf16[272,1088]{1,0:T(8,128)(2,1)}, u32[]{:S(2)}, u32[]{:S(2)}) %collective-permute-start.13) | collective-permute-done | bytes 591904 | tf_op jit(solution)/shard_map/ppermute | solution.py:59
  112.9 3.3 shard_map.290
  116.7 3.7 %convolution_add_fusion = f32[512,1088]{0,1:T(8,128)S(1)} fusion(bf16[1088,1088]{1,0:T(8,128)(2,1)} %shard_map.290, f32[1088]{0:T(1024)S(1)} %convert_element_type.231, bf16[256,1088]{0,1:T(8,128)(2,1)} %collective-permute-done.10, bf16[128,1088]{0,1:T(8,128)(2,1)} %collective-permute-done.9, bf16[128,1088]{0,1:T(8,128)(2,1)} %add_convert_fusion.8), kind=kOutput, calls=%fused_computation.1 | convolution fusion | flops 1216053248 | bytes 5714176 | tf_op jit(solution)/shard_map/dot_general | solution.py:53
  122.3 4.8 %convert_reduce_fusion.1 = (f32[1088]{0:T(1024)S(1)}, bf16[512,1088]{0,1:T(8,128)(2,1)S(1)}) fusion(f32[512,1088]{0,1:T(8,128)S(1)} %convolution_add_fusion, bf16[1088,1088]{1,0:T(8,128)(2,1)S(1)} %copy-done, bf16[256,1088]{0,1:T(8,128)(2,1)} %collective-permute-done.17, bf16[128,1088]{0,1:T(8,128)(2,1)} %collective-permute-done.16, ...), kind=kOutput, calls=%fused_computation.23 | convolution fusion | flops 1227193344 | bytes 6828288 | tf_op jit(solution)/shard_map/dot_general | solution.py:53
  131.5 2.9 fusion.36
  139.4 3.8 %fusion.35 = f32[1088,1088]{1,0:T(8,128)S(1)} fusion(bf16[256,1088]{0,1:T(8,128)(2,1)} %collective-permute-done.17, bf16[128,1088]{0,1:T(8,128)(2,1)} %collective-permute-done.16, bf16[128,1088]{0,1:T(8,128)(2,1)S(1)} %bitcast.168, f32[512,1088]{0,1:T(8,128)} %copy-done.59), kind=kOutput, calls=%fused_computation.111 | convolution fusion | flops 1220509696 | bytes 8077312 | tf_op jit(solution)/shard_map/dot_general | solution.py:53
  146.2 6.0 %collective-permute-done.19 = bf16[128,1088]{0,1:T(8,128)(2,1)S(1)} collective-permute-done((bf16[128,1088]{0,1:T(8,128)(2,1)S(1)}, bf16[128,1088]{0,1:T(8,128)(2,1)S(1)}, u32[]{:S(2)}, u32[]{:S(2)}) %collective-permute-start.19) | collective-permute-done | bytes 278560 | tf_op jit(solution)/shard_map/ppermute | solution.py:59
  159.3 3.1 collective-permute-done.22
  163.8 3.0 collective-permute-done.42
  170.6 9.3 %collective-permute-done.46 = bf16[2,2,1,136,1088]{4,3,2,1,0:T(8,128)(2,1)S(1)} collective-permute-done((bf16[2,2,1,136,1088]{4,3,2,1,0:T(8,128)(2,1)S(1)}, bf16[2,2,1,136,1088]{4,3,2,1,0:T(8,128)(2,1)S(1)}, u32[]{:S(2)}, u32[]{:S(2)}) %collective-permute-start.46) | collective-permute-done | bytes 1183776 | tf_op jit(solution)/shard_map/ppermute | solution.py:59
  185.2 9.0 %attend_back.1 = bf16[3,320,512]{2,1,0:T(8,128)(2,1)} custom-call(s32[1]{0:T(128)} %bitcast.1.refs_0_.rank_ref, s32[8,512]{1,0:T(8,128)} %add_add_fusion.refs_1_, bf16[960,512]{1,0:T(8,128)(2,1)} %add_convert_fusion.2.refs_2_.refs_3_.refs_4_, bf16[960,512]{1,0:T(8,128)(2,1)} %add_convert_fusion.2.refs_2_.refs_3_.refs_4_, ...), custom_call_target="tpu_custom_call" | custom-call | flops 838860800 | bytes 2621440 | tf_op jit(solution)/shard_map/attend_back/pallas_call | solution.py:375
  198.7 3.0 collective-permute-start.24
  218.8 3.6 %collective-permute-done.25 = bf16[128,1088]{0,1:T(8,128)(2,1)S(1)} collective-permute-done((bf16[128,1088]{0,1:T(8,128)(2,1)S(1)}, bf16[128,1088]{0,1:T(8,128)(2,1)S(1)}, u32[]{:S(2)}, u32[]{:S(2)}) %collective-permute-start.25) | collective-permute-done | bytes 278560 | tf_op jit(solution)/shard_map/ppermute | solution.py:59
  224.9 3.1 fusion.24
  231.4 3.0 collective-permute-start.29
  243.9 8.0 %collective-permute-done.41 = bf16[1,136,272]{2,1,0:T(8,128)(2,1)S(1)} collective-permute-done((bf16[1,136,272]{2,1,0:T(8,128)(2,1)S(1)}, bf16[1,136,272]{2,1,0:T(8,128)(2,1)S(1)}, u32[]{:S(2)}, u32[]{:S(2)}) %collective-permute-start.41) | collective-permute-done | bytes 74016 | tf_op jit(solution)/shard_map/ppermute | solution.py:59
  252.6 11.2 %collective-permute-done.32 = f32[102,128]{1,0:T(8,128)S(1)} collective-permute-done((f32[102,128]{1,0:T(8,128)S(1)}, f32[102,128]{1,0:T(8,128)S(1)}, u32[]{:S(2)}, u32[]{:S(2)}) %collective-permute-start.32) | collective-permute-done | bytes 52256 | tf_op jit(solution)/shard_map/ppermute | solution.py:59
  266.5 16.4 %collective-permute-done.33 = f32[102,128]{1,0:T(8,128)S(1)} collective-permute-done((f32[102,128]{1,0:T(8,128)S(1)}, f32[102,128]{1,0:T(8,128)S(1)}, u32[]{:S(2)}, u32[]{:S(2)}) %collective-permute-start.33) | collective-permute-done | bytes 52256 | tf_op jit(solution)/shard_map/ppermute | solution.py:59
  288.7 5.6 %collective-permute-done.45 = bf16[272,544]{1,0:T(8,128)(2,1)S(1)} collective-permute-done((bf16[272,544]{1,0:T(8,128)(2,1)S(1)}, bf16[272,544]{1,0:T(8,128)(2,1)S(1)}, u32[]{:S(2)}, u32[]{:S(2)}) %collective-permute-start.45) | collective-permute-done | bytes 295968 | tf_op jit(solution)/shard_map/ppermute | solution.py:620
  295.2 23.1 %collective-permute-done.34 = bf16[3,272,136]{2,1,0:T(8,128)(2,1)S(1)} collective-permute-done((bf16[3,272,136]{2,1,0:T(8,128)(2,1)S(1)}, bf16[3,272,136]{2,1,0:T(8,128)(2,1)S(1)}, u32[]{:S(2)}, u32[]{:S(2)}) %collective-permute-start.34) | collective-permute-done | bytes 221984 | tf_op jit(solution)/shard_map/ppermute | solution.py:59
  322.6 2.7 collective-permute-start.36
  325.4 8.1 %collective-permute-start.35 = (bf16[272,136]{1,0:T(8,128)(2,1)S(1)}, bf16[272,136]{1,0:T(8,128)(2,1)S(1)}, u32[]{:S(2)}, u32[]{:S(2)}) collective-permute-start(bf16[272,136]{1,0:T(8,128)(2,1)S(1)} %get-tuple-element.99), channel_id=1, source_target_pairs={{0,20},{1,24},{2,4},{3,16},{4,21},{5,25},{6,5},{7,17},{8,22},{9,26... | collective-permute-start | bytes 221960 | tf_op jit(solution)/shard_map/ppermute | solution.py:609
  334.9 4.2 %collective-permute-done.35 = bf16[272,136]{1,0:T(8,128)(2,1)S(1)} collective-permute-done((bf16[272,136]{1,0:T(8,128)(2,1)S(1)}, bf16[272,136]{1,0:T(8,128)(2,1)S(1)}, u32[]{:S(2)}, u32[]{:S(2)}) %collective-permute-start.35) | collective-permute-done | bytes 74016 | tf_op jit(solution)/shard_map/ppermute | solution.py:609
  (343 shorter events, 136.3 us)
Async XLA Ops:
  3.9 36.8 %collective-permute-start = (bf16[272,960]{1,0:T(8,128)(2,1)}, bf16[272,960]{1,0:T(8,128)(2,1)}, u32[]{:S(2)}, u32[]{:S(2)}) collective-permute-start(bf16[272,960]{1,0:T(8,128)(2,1)} %get-tuple-element.35), channel_id=1, source_target_pairs={{0,1},{1,0},{2,3},{3,2},{4,5},{5,4},{6,7},{7,6},{8,9},{9,8},{10,11... | collective-permute-start | bytes 1566728 | tf_op jit(solution)/shard_map/ppermute | solution.py:59
  3.9 36.8 %collective-permute-start.1 = (bf16[272,960]{1,0:T(8,128)(2,1)}, bf16[272,960]{1,0:T(8,128)(2,1)}, u32[]{:S(2)}, u32[]{:S(2)}) collective-permute-start(bf16[272,960]{1,0:T(8,128)(2,1)} %get-tuple-element.36), channel_id=1, source_target_pairs={{0,2},{1,3},{2,0},{3,1},{4,6},{5,7},{6,4},{7,5},{8,10},{9,11},{10,... | collective-permute-start | bytes 1566728 | tf_op jit(solution)/shard_map/ppermute | solution.py:59
  6.6 34.1 %collective-permute-start.2 = (bf16[272,960]{1,0:T(8,128)(2,1)}, bf16[272,960]{1,0:T(8,128)(2,1)}, u32[]{:S(2)}, u32[]{:S(2)}) collective-permute-start(bf16[272,960]{1,0:T(8,128)(2,1)} %get-tuple-element.37), channel_id=1, source_target_pairs={{0,3},{1,2},{2,1},{3,0},{4,7},{5,6},{6,5},{7,4},{8,11},{9,10},{10,... | collective-permute-start | bytes 1566728 | tf_op jit(solution)/shard_map/ppermute | solution.py:59
  12.1 19.8 %collective-permute-start.5 = (bf16[8,272]{1,0:T(8,128)(2,1)S(1)}, bf16[8,272]{1,0:T(8,128)(2,1)S(1)}, u32[]{:S(2)}, u32[]{:S(2)}) collective-permute-start(bf16[8,272]{1,0:T(8,128)(2,1)S(1)} %concatenate.63), channel_id=1, source_target_pairs={{0,2},{1,3},{2,0},{3,1},{4,6},{5,7},{6,4},{7,5},{8,10},{9,11},{10,... | collective-permute-start | bytes 13064 | tf_op jit(solution)/shard_map/ppermute | solution.py:59
  13.8 24.1 %collective-permute-start.3 = (bf16[128,1088]{0,1:T(8,128)(2,1)}, bf16[128,1088]{0,1:T(8,128)(2,1)S(1)}, u32[]{:S(2)}, u32[]{:S(2)}) collective-permute-start(bf16[128,1088]{0,1:T(8,128)(2,1)} %bitcast.154), channel_id=1, source_target_pairs={{0,2},{1,3},{2,0},{3,1},{4,6},{5,7},{6,4},{7,5},{8,10},{9,11},{10,... | collective-permute-start | bytes 835592 | tf_op jit(solution)/shard_map/ppermute | solution.py:59
  63.9 32.9 %collective-permute-start.12 = (bf16[272,1088]{1,0:T(8,128)(2,1)}, bf16[272,1088]{1,0:T(8,128)(2,1)}, u32[]{:S(2)}, u32[]{:S(2)}) collective-permute-start(bf16[272,1088]{1,0:T(8,128)(2,1)} %get-tuple-element.79), channel_id=1, source_target_pairs={{0,2},{1,3},{2,0},{3,1},{4,7},{5,6},{6,5},{7,4},{8,10},{9,11},{10,... | collective-permute-start | bytes 1775624 | tf_op jit(solution)/shard_map/ppermute | solution.py:476
  66.6 18.8 %collective-permute-start.8 = (bf16[128,1088]{0,1:T(8,128)(2,1)S(1)}, bf16[128,1088]{0,1:T(8,128)(2,1)}, u32[]{:S(2)}, u32[]{:S(2)}) collective-permute-start(bf16[128,1088]{0,1:T(8,128)(2,1)S(1)} %slice.327), channel_id=1, source_target_pairs={{0,2},{1,3},{2,0},{3,1},{4,6},{5,7},{6,4},{7,5},{8,10},{9,11},{10,... | collective-permute-start | bytes 835592 | tf_op jit(solution)/shard_map/ppermute | solution.py:59
  91.1 91.4 %collective-permute-start.20 = (bf16[48,1088]{1,0:T(8,128)(2,1)}, bf16[48,1088]{1,0:T(8,128)(2,1)}, u32[]{:S(2)}, u32[]{:S(2)}) collective-permute-start(bf16[48,1088]{1,0:T(8,128)(2,1)} %get-tuple-element.90), channel_id=1, source_target_pairs={{0,1},{1,2},{2,3},{4,5},{5,6},{6,7},{8,9},{9,10},{10,11},{12,13},{... | collective-permute-start | bytes 313352 | tf_op jit(solution)/shard_map/ppermute | solution.py:485
  96.7 16.2 %collective-permute-start.13 = (bf16[272,1088]{1,0:T(8,128)(2,1)}, bf16[272,1088]{1,0:T(8,128)(2,1)}, u32[]{:S(2)}, u32[]{:S(2)}) collective-permute-start(bf16[272,1088]{1,0:T(8,128)(2,1)} %collective-permute-done.12.refs_2_), channel_id=1, source_target_pairs={{0,4},{4,0},{8,12},{12,8},{16,20},{20,16},{24,28},{28,24},{1,5},{5... | collective-permute-start | bytes 1775624 | tf_op jit(solution)/shard_map/ppermute | solution.py:59
  100.4 16.3 %collective-permute-start.10 = (bf16[256,1088]{0,1:T(8,128)(2,1)}, bf16[256,1088]{0,1:T(8,128)(2,1)}, u32[]{:S(2)}, u32[]{:S(2)}) collective-permute-start(bf16[256,1088]{0,1:T(8,128)(2,1)} %pad_maximum_fusion.7), channel_id=1, source_target_pairs={{0,1},{1,0},{2,3},{3,2},{4,5},{5,4},{6,7},{7,6},{8,9},{9,8},{10,11... | collective-permute-start | bytes 1671176 | tf_op jit(solution)/shard_map/ppermute | solution.py:59
  103.4 79.3 %collective-permute-start.21 = (bf16[48,1088]{1,0:T(8,128)(2,1)S(1)}, bf16[48,1088]{1,0:T(8,128)(2,1)}, u32[]{:S(2)}, u32[]{:S(2)}) collective-permute-start(bf16[48,1088]{1,0:T(8,128)(2,1)S(1)} %get-tuple-element.89), channel_id=1, source_target_pairs={{1,0},{2,1},{3,2},{5,4},{6,5},{7,6},{9,8},{10,9},{11,10},{13,12},{... | collective-permute-start | bytes 313352 | tf_op jit(solution)/shard_map/ppermute | solution.py:486
  108.0 14.2 %collective-permute-start.17 = (bf16[256,1088]{0,1:T(8,128)(2,1)}, bf16[256,1088]{0,1:T(8,128)(2,1)}, u32[]{:S(2)}, u32[]{:S(2)}) collective-permute-start(bf16[256,1088]{0,1:T(8,128)(2,1)} %pad_maximum_fusion.8), channel_id=1, source_target_pairs={{0,1},{1,0},{2,3},{3,2},{4,5},{5,4},{6,7},{7,6},{8,9},{9,8},{10,11... | collective-permute-start | bytes 1671176 | tf_op jit(solution)/shard_map/ppermute | solution.py:59
  129.7 13.6 %collective-permute-start.18 = (bf16[256,1088]{0,1:T(8,128)(2,1)}, bf16[256,1088]{0,1:T(8,128)(2,1)}, u32[]{:S(2)}, u32[]{:S(2)}) collective-permute-start(bf16[256,1088]{0,1:T(8,128)(2,1)} %slice.321), channel_id=1, source_target_pairs={{0,1},{1,0},{2,3},{3,2},{4,5},{5,4},{6,7},{7,6},{8,9},{9,8},{10,11... | collective-permute-start | bytes 1671176 | tf_op jit(solution)/shard_map/ppermute | solution.py:59
  131.5 24.4 %collective-permute-start.14 = (bf16[256,1088]{0,1:T(8,128)(2,1)}, bf16[256,1088]{0,1:T(8,128)(2,1)}, u32[]{:S(2)}, u32[]{:S(2)}) collective-permute-start(bf16[256,1088]{0,1:T(8,128)(2,1)} %slice.322), channel_id=1, source_target_pairs={{0,1},{1,0},{2,3},{3,2},{4,5},{5,4},{6,7},{7,6},{8,9},{9,8},{10,11... | collective-permute-start | bytes 1671176 | tf_op jit(solution)/shard_map/ppermute | solution.py:59
  137.8 28.9 %collective-permute-start.42 = (bf16[544,1088]{1,0:T(8,128)(2,1)}, bf16[544,1088]{1,0:T(8,128)(2,1)}, u32[]{:S(2)}, u32[]{:S(2)}) collective-permute-start(bf16[544,1088]{1,0:T(8,128)(2,1)} %dynamic-slice_convert_fusion.1), channel_id=1, source_target_pairs={{0,8},{4,12},{8,0},{12,4},{16,24},{20,28},{24,16},{28,20},{1,9},{5... | collective-permute-start | bytes 3551240 | tf_op jit(solution)/shard_map/ppermute | solution.py:59
  152.3 27.6 %collective-permute-start.46 = (bf16[2,2,1,136,1088]{4,3,2,1,0:T(8,128)(2,1)S(1)}, bf16[2,2,1,136,1088]{4,3,2,1,0:T(8,128)(2,1)S(1)}, u32[]{:S(2)}, u32[]{:S(2)}) collective-permute-start(bf16[2,2,1,136,1088]{4,3,2,1,0:T(8,128)(2,1)S(1)} %dynamic-slice_convert_fusion), channel_id=1, source_target_pairs={{0,4},{4,0},{8,12},{12,8},{16,20},{20,16},{24,28},{28,24},{1,5},{5... | collective-permute-start | bytes 3551240 | tf_op jit(solution)/shard_map/ppermute | solution.py:59
  162.4 62.3 %collective-permute-start.15 = (bf16[128,1088]{0,1:T(8,128)(2,1)}, bf16[128,1088]{0,1:T(8,128)(2,1)}, u32[]{:S(2)}, u32[]{:S(2)}) collective-permute-start(bf16[128,1088]{0,1:T(8,128)(2,1)} %slice.326), channel_id=1, source_target_pairs={{0,2},{1,3},{2,0},{3,1},{4,6},{5,7},{6,4},{7,5},{8,10},{9,11},{10,... | collective-permute-start | bytes 835592 | tf_op jit(solution)/shard_map/ppermute | solution.py:59
  166.7 16.0 %collective-permute-start.23 = (bf16[256,1088]{0,1:T(8,128)(2,1)S(1)}, bf16[256,1088]{0,1:T(8,128)(2,1)S(1)}, u32[]{:S(2)}, u32[]{:S(2)}) collective-permute-start(bf16[256,1088]{0,1:T(8,128)(2,1)S(1)} %pad_maximum_fusion.9), channel_id=1, source_target_pairs={{0,1},{1,0},{2,3},{3,2},{4,5},{5,4},{6,7},{7,6},{8,9},{9,8},{10,11... | collective-permute-start | bytes 1671176 | tf_op jit(solution)/shard_map/ppermute | solution.py:59
  179.8 35.6 %collective-permute-start.43 = (bf16[272,1088]{1,0:T(8,128)(2,1)}, bf16[272,1088]{1,0:T(8,128)(2,1)}, u32[]{:S(2)}, u32[]{:S(2)}) collective-permute-start(bf16[272,1088]{1,0:T(8,128)(2,1)} %constant_dynamic-slice_fusion.2), channel_id=1, source_target_pairs={{0,4},{4,0},{8,12},{12,8},{16,20},{20,16},{24,28},{28,24},{1,5},{5... | collective-permute-start | bytes 1775624 | tf_op jit(solution)/shard_map/ppermute | solution.py:59
  182.5 26.2 %collective-permute-start.47 = (bf16[2,1,1,136,1088]{4,3,2,1,0:T(8,128)(2,1)}, bf16[2,1,1,136,1088]{4,3,2,1,0:T(8,128)(2,1)}, u32[]{:S(2)}, u32[]{:S(2)}) collective-permute-start(bf16[2,1,1,136,1088]{4,3,2,1,0:T(8,128)(2,1)} %constant_dynamic-slice_fusion.1), channel_id=1, source_target_pairs={{0,8},{4,12},{8,0},{12,4},{16,24},{20,28},{24,16},{28,20},{1,9},{5... | collective-permute-start | bytes 1775624 | tf_op jit(solution)/shard_map/ppermute | solution.py:59
  198.7 13.7 %collective-permute-start.24 = (bf16[256,1088]{0,1:T(8,128)(2,1)}, bf16[256,1088]{0,1:T(8,128)(2,1)}, u32[]{:S(2)}, u32[]{:S(2)}) collective-permute-start(bf16[256,1088]{0,1:T(8,128)(2,1)} %slice.320), channel_id=1, source_target_pairs={{0,1},{1,0},{2,3},{3,2},{4,5},{5,4},{6,7},{7,6},{8,9},{9,8},{10,11... | collective-permute-start | bytes 1671176 | tf_op jit(solution)/shard_map/ppermute | solution.py:59
  204.3 80.6 %collective-permute-start.26 = (bf16[272,816]{1,0:T(8,128)(2,1)}, bf16[272,816]{1,0:T(8,128)(2,1)}, u32[]{:S(2)}, u32[]{:S(2)}) collective-permute-start(bf16[272,816]{1,0:T(8,128)(2,1)} %get-tuple-element.78), channel_id=1, source_target_pairs={{0,4},{4,0},{8,12},{12,8},{16,20},{20,16},{24,28},{28,24},{1,5},{5... | collective-permute-start | bytes 1331720 | tf_op jit(solution)/shard_map/ppermute | solution.py:59
  208.8 76.1 %collective-permute-start.27 = (bf16[272,816]{1,0:T(8,128)(2,1)}, bf16[272,816]{1,0:T(8,128)(2,1)}, u32[]{:S(2)}, u32[]{:S(2)}) collective-permute-start(bf16[272,816]{1,0:T(8,128)(2,1)} %get-tuple-element.77), channel_id=1, source_target_pairs={{0,8},{4,12},{8,0},{12,4},{16,24},{20,28},{24,16},{28,20},{1,9},{5... | collective-permute-start | bytes 1331720 | tf_op jit(solution)/shard_map/ppermute | solution.py:59
  212.4 16.6 %collective-permute-start.40 = (bf16[2,136,272]{2,1,0:T(8,128)(2,1)}, bf16[2,136,272]{2,1,0:T(8,128)(2,1)S(1)}, u32[]{:S(2)}, u32[]{:S(2)}) collective-permute-start(bf16[2,136,272]{2,1,0:T(8,128)(2,1)} %get-tuple-element.87), channel_id=1, source_target_pairs={{0,12},{4,8},{8,4},{12,0},{16,28},{20,24},{24,20},{28,16},{1,13},{... | collective-permute-start | bytes 443912 | tf_op jit(solution)/shard_map/ppermute | solution.py:59
  229.0 35.3 %collective-permute-start.44 = (bf16[272,544]{1,0:T(8,128)(2,1)}, bf16[272,544]{1,0:T(8,128)(2,1)S(1)}, u32[]{:S(2)}, u32[]{:S(2)}) collective-permute-start(bf16[272,544]{1,0:T(8,128)(2,1)} %broadcast_select_fusion.2), channel_id=1, source_target_pairs={{0,16},{4,20},{8,24},{12,28},{16,0},{20,4},{24,8},{28,12},{1,17},{... | collective-permute-start | bytes 887816 | tf_op jit(solution)/shard_map/ppermute | solution.py:59
  237.1 14.8 %collective-permute-start.41 = (bf16[1,136,272]{2,1,0:T(8,128)(2,1)S(1)}, bf16[1,136,272]{2,1,0:T(8,128)(2,1)S(1)}, u32[]{:S(2)}, u32[]{:S(2)}) collective-permute-start(bf16[1,136,272]{2,1,0:T(8,128)(2,1)S(1)} %constant_dynamic-slice_fusion.3), channel_id=1, source_target_pairs={{0,16},{4,20},{8,24},{12,28},{16,0},{20,4},{24,8},{28,12},{1,17},{... | collective-permute-start | bytes 221960 | tf_op jit(solution)/shard_map/ppermute | solution.py:59
  242.2 42.7 %collective-permute-start.28 = (bf16[272,816]{1,0:T(8,128)(2,1)S(1)}, bf16[272,816]{1,0:T(8,128)(2,1)S(1)}, u32[]{:S(2)}, u32[]{:S(2)}) collective-permute-start(bf16[272,816]{1,0:T(8,128)(2,1)S(1)} %copy-done.38), channel_id=1, source_target_pairs={{0,12},{4,8},{8,4},{12,0},{16,28},{20,24},{24,20},{28,16},{1,13},{... | collective-permute-start | bytes 1331720 | tf_op jit(solution)/shard_map/ppermute | solution.py:59
  263.8 24.0 %collective-permute-start.48 = (bf16[1,1,1,136,1088]{4,3,2,1,0:T(8,128)(2,1)S(1)}, bf16[1,1,1,136,1088]{4,3,2,1,0:T(8,128)(2,1)S(1)}, u32[]{:S(2)}, u32[]{:S(2)}) collective-permute-start(bf16[1,1,1,136,1088]{4,3,2,1,0:T(8,128)(2,1)S(1)} %constant_dynamic-slice_fusion), channel_id=1, source_target_pairs={{0,16},{4,20},{8,24},{12,28},{16,0},{20,4},{24,8},{28,12},{1,17},{... | collective-permute-start | bytes 887816 | tf_op jit(solution)/shard_map/ppermute | solution.py:59
  264.3 18.6 %collective-permute-start.33 = (f32[102,128]{1,0:T(8,128)S(1)}, f32[102,128]{1,0:T(8,128)S(1)}, u32[]{:S(2)}, u32[]{:S(2)}) collective-permute-start(f32[102,128]{1,0:T(8,128)S(1)} %add.243), channel_id=1, source_target_pairs={{0,16},{4,20},{8,24},{12,28},{16,0},{20,4},{24,8},{28,12},{1,17},{... | collective-permute-start | bytes 156680 | tf_op jit(solution)/shard_map/ppermute | solution.py:59
  286.9 31.4 %collective-permute-start.34 = (bf16[3,272,136]{2,1,0:T(8,128)(2,1)S(1)}, bf16[3,272,136]{2,1,0:T(8,128)(2,1)S(1)}, u32[]{:S(2)}, u32[]{:S(2)}) collective-permute-start(bf16[3,272,136]{2,1,0:T(8,128)(2,1)S(1)} %broadcast_select_fusion.1), channel_id=1, source_target_pairs={{0,16},{4,20},{8,24},{12,28},{16,0},{20,4},{24,8},{28,12},{1,17},{... | collective-permute-start | bytes 665864 | tf_op jit(solution)/shard_map/ppermute | solution.py:59
  320.7 14.1 %collective-permute-start.37 = (bf16[272,136]{1,0:T(8,128)(2,1)S(1)}, bf16[272,136]{1,0:T(8,128)(2,1)S(1)}, u32[]{:S(2)}, u32[]{:S(2)}) collective-permute-start(bf16[272,136]{1,0:T(8,128)(2,1)S(1)} %get-tuple-element.100), channel_id=1, source_target_pairs={{0,0},{1,12},{2,24},{3,8},{4,1},{5,13},{6,25},{7,9},{8,2},{9,14},{... | collective-permute-start | bytes 221960 | tf_op jit(solution)/shard_map/ppermute | solution.py:609
  325.4 13.6 %collective-permute-start.35 = (bf16[272,136]{1,0:T(8,128)(2,1)S(1)}, bf16[272,136]{1,0:T(8,128)(2,1)S(1)}, u32[]{:S(2)}, u32[]{:S(2)}) collective-permute-start(bf16[272,136]{1,0:T(8,128)(2,1)S(1)} %get-tuple-element.99), channel_id=1, source_target_pairs={{0,20},{1,24},{2,4},{3,16},{4,21},{5,25},{6,5},{7,17},{8,22},{9,26... | collective-permute-start | bytes 221960 | tf_op jit(solution)/shard_map/ppermute | solution.py:609
  (79 other events, 918.2 us)

commit v2 on v1

--- a/solution.py
+++ b/solution.py
@@ -11,6 +11,7 @@
 HEADS = 17
 HD = 64
 
+GRP, REP = "grp", "rep"
 epsilon = 1e-05
 gelu_factor = 0.7978845608028654
 masked_score = -1e30
@@ -97,7 +98,7 @@
 def group_gather(value, size):
     bit = size // 2
     while bit:
-        value = jnp.concatenate([value, swap(value, "grp", size, bit)])
+        value = jnp.concatenate([value, swap(value, GRP, size, bit)])
         bit //= 2
     return value
 
@@ -106,7 +107,7 @@
     bit = 1
     while bit < size:
         half = value.shape[0] // 2
-        moved = swap(value[half:].astype(bf16), "grp", size, bit)
+        moved = swap(value[half:].astype(bf16), GRP, size, bit)
         value = value[:half] + moved.astype(f32)
         bit *= 2
     return value
@@ -185,7 +186,7 @@
         cost_estimate=pl.CostEstimate(
             flops=0, transcendentals=0, bytes_accessed=14 * rows * width * size
         ),
-        name="pack_columns",
+        name="pack",
     )(rank.reshape(1), weight)
 
 
@@ -203,7 +204,7 @@
 
 
 def rep_bit(bit):
-    return (lax.axis_index("rep") >> bit) & 1
+    return (lax.axis_index(REP) >> bit) & 1
 
 
 def add_parts(parts, dtype):
@@ -218,7 +219,7 @@
     half = value.shape[axis] // 2
     keep = cut(value, mine * half, half, axis)
     give = cut(value, (1 - mine) * half, half, axis).astype(bf16)
-    return keep, swap(give, "rep", reps, 1 << bit)
+    return keep, swap(give, REP, reps, 1 << bit)
 
 
 def halve_lanes(value, bit, reps):
@@ -226,18 +227,11 @@
     half = value.shape[-1] // 2
     low, high = value[..., :half], value[..., half:]
     give = jnp.where(mine, low, high).astype(bf16)
-    return jnp.where(mine, high, low), swap(give, "rep", reps, 1 << bit)
+    return jnp.where(mine, high, low), swap(give, REP, reps, 1 << bit)
 
 
 def natural_rows(value, reps):
     return value.reshape((2,) * log2(reps) + (value.shape[0] // reps,) + value.shape[1:])
-
-
-def quad_step(value, axis, reps, size):
-    low = lax.axis_index("rep") & (size - 1)
-    block = lambda o: pick(value, low ^ o, axis)
-    gives = [block(o).astype(bf16) for o in range(1, size)]
-    return [block(0)] + [swap(give, "rep", reps, o + 1) for o, give in enumerate(gives)]
 
 
 def piece_of(rep, reps, size):
@@ -399,7 +393,7 @@
             transcendentals=heads * seq * seq,
             bytes_accessed=16 * heads * HD * seq,
         ),
-        name="attend_back",
+        name="back",
     )(rank.reshape(1), bounds, projected, projected, projected, mixed, grad_mixed, totals)
 
 
@@ -423,8 +417,8 @@
     hidden_bias,
     down_bias,
 ):
-    rank = lax.axis_index("grp")
-    rep_rank = lax.axis_index("rep")
+    rank = lax.axis_index(GRP)
+    rep_rank = lax.axis_index(REP)
     own = D // size
     hidden_own = hidden_bias.shape[0]
     hidden_all = hidden_own * size
@@ -448,7 +442,7 @@
     packed_give = pack_columns(packed_weight, begins, width, rank, size)
     packed_blocks = [packed_give[0]] + [None] * (size - 1)
     for j in reversed(range(1, size)):
-        packed_blocks[j] = swap(packed_give[j], "grp", size, j)
+        packed_blocks[j] = swap(packed_give[j], GRP, size, j)
     shorts = (
         first_gain,
         first_shift,
@@ -473,17 +467,17 @@
     up_blocks = [pick(up_sets, rank, 0)] + [None] * (size - 1)
     if size == 4:
         route = [(r * 4 + g, r * 4 + (g ^ 2 ^ (r & 1))) for r in range(reps) for g in range(4)]
-        up_blocks[2] = lax.ppermute(pick(up_sets, rank ^ 2 ^ flip, 0), ("rep", "grp"), route)
-        up_blocks[1] = swap(pick(up_sets, rank ^ 1, 0), "grp", size, 1)
-        up_blocks[3] = swap(up_blocks[2], "rep", reps, 1)
+        up_blocks[2] = lax.ppermute(pick(up_sets, rank ^ 2 ^ flip, 0), (REP, GRP), route)
+        up_blocks[1] = swap(pick(up_sets, rank ^ 1, 0), GRP, size, 1)
+        up_blocks[3] = swap(up_blocks[2], REP, reps, 1)
     else:
         for j in range(1, size):
-            up_blocks[j] = swap(pick(up_sets, rank ^ j, 0), "grp", size, j)
+            up_blocks[j] = swap(pick(up_sets, rank ^ j, 0), GRP, size, j)
     up_cols = place_rows(up_blocks, rank, flip)
     grad_rows = group_gather(cotangent[0], size)
     edge_pairs = [(i, i + 1) for i in range(size - 1)]
-    ahead = lax.ppermute(output_weight[own - margin :], "grp", edge_pairs)
-    behind = lax.ppermute(output_weight[:margin], "grp", [(j, i) for i, j in edge_pairs])
+    ahead = lax.ppermute(output_weight[own - margin :], GRP, edge_pairs)
+    behind = lax.ppermute(output_weight[:margin], GRP, [(j, i) for i, j in edge_pairs])
     output_wide = cut(
         jnp.concatenate([ahead, output_weight, behind]), margin - offset, width, 0
     )
@@ -528,9 +522,18 @@
     share = reps // size
     low_bits, all_bits = log2(size), log2(reps)
     down_axis = lambda bit: all_bits - 1 - bit
+    row_axis = lambda bit: low_bits - 1 - bit
+
+    def step_natural(parts, bit, dtype=bf16):
+        return halve_rows(add_parts(parts, dtype), bit, reps, down_axis(bit))
+
+    def step_piece(value, bit):
+        if bit < low_bits:
+            return halve_rows(value, bit, reps, row_axis(bit))
+        return halve_lanes(value, bit, reps)
+
     down_parts = halve_rows(natural_rows(grad_down, reps), 0, reps, down_axis(0))
-    up_order = list(reversed(range(low_bits))) + list(range(low_bits, all_bits))
-    up_parts = halve_rows(grad_up, up_order[0], reps, 0)
+    up_parts = step_piece(grad_up.reshape((2,) * low_bits + (own, hidden_own)), 0)
 
     grad_float = cotangent[0].astype(f32)
     grad_resid = grad_float + norm_back(grad_c, normed_second, inv_second, vectors[5])
@@ -539,28 +542,25 @@
 
     grad_mixed = contract(output_wide, grad_attn, 1, 1).astype(bf16)
     for step in range(1, all_bits - 1):
-        down_parts = halve_rows(add_parts(down_parts, bf16), step, reps, down_axis(step))
-    held = grad_mixed
-    grad_packed_rows = attend_back(projected, mixed, held, totals, bounds, rank, size, heads)
+        down_parts = step_natural(down_parts, step)
+    grad_packed_rows = attend_back(projected, mixed, grad_mixed, totals, bounds, rank, size, heads)
     grad_mine = cut(grad_packed_rows, offset, own, 1)
     grad_packed = contract(normal_a, grad_mine.reshape(3 * own, seq), 0, 1)
-    packed_parts = quad_step(grad_packed.reshape(size, own, 3 * own), 0, reps, size)
-
-    down_last = halve_rows(add_parts(down_parts, bf16), all_bits - 1, reps, down_axis(all_bits - 1))
-    for step in range(1, all_bits - 1):
-        up_piece = add_parts(up_parts, bf16)
-        if step < low_bits:
-            up_parts = halve_rows(up_piece, up_order[step], reps, 0)
-        else:
-            up_parts = halve_lanes(up_piece, up_order[step], reps)
+    packed_parts = step_piece(grad_packed.reshape((2,) * low_bits + (own, 3 * own)), 0)
+
+    down_last = step_natural(down_parts, all_bits - 1)
+    for step in range(1, all_bits):
+        up_parts = step_piece(add_parts(up_parts, bf16), step)
 
     grad_masked = jnp.where(wide_mine[None], grad_packed_rows, jnp.zeros_like(grad_packed_rows))
     grad_a_part = contract(grad_masked.reshape(3 * width, seq), packed_cols, 0, 1)
     grad_a = group_scatter_sum(grad_a_part, size)
     mixed_mine = cut(mixed, offset, own, 0)
     grad_output = contract(grad_attn, mixed_mine, 0, 1)
-    out_parts = quad_step(grad_output.reshape(share, size, D // reps, own), 1, reps, size)
-    up_last = halve_lanes(add_parts(up_parts, bf16), all_bits - 1, reps)
+    out_parts = halve_rows(natural_rows(grad_output, reps), 0, reps, down_axis(0))
+    for bit in range(1, all_bits):
+        out_parts = step_natural(out_parts, bit)
+    final_output = add_parts(out_parts, f32).reshape(D // reps, own).T
     layer_rows = residual + group_scatter_sum(layer_part, size) + vectors[7]
     normed_first, inv_first = norm_rows(rows_float)
     grad_in = grad_resid + norm_back(grad_a, normed_first, inv_first, vectors[0])
@@ -583,14 +583,14 @@
             jnp.sum(grad_float, axis=0),
         ]
     )
-    sums = sum_over(sum_over(sums.reshape(-1, 128), "grp", size), "rep", reps)
-
-    packed_parts, sums = lax.optimization_barrier((packed_parts, sums))
-    piece = add_parts(packed_parts, bf16)
+    sums = sum_over(sum_over(sums.reshape(-1, 128), GRP, size), REP, reps)
+
+    for bit in range(1, low_bits):
+        packed_parts = step_piece(add_parts(packed_parts, bf16), bit)
+    piece = add_parts(packed_parts, bf16).reshape(own, 3 * own)
     piece = jnp.stack([piece[:, own * t : own * (t + 1)] for t in range(3)])
     for bit in range(low_bits, all_bits):
-        halves = halve_lanes(piece, bit, reps)
-        piece = add_parts(halves, bf16)
+        piece = add_parts(halve_lanes(piece, bit, reps), bf16)
     rounds = match_rounds(reps, 3)
     table = jnp.array(rounds, jnp.int32)
     unit = rank * share + piece_of(rep_rank, reps, size)[0]
@@ -606,18 +606,14 @@
                 origin[where // 3][where % 3] = turn
                 route.append((r * size + g, (where // 3) * size + lane_part))
         sent = pick(piece, table[turn, unit], 0)
-        received.append(lax.ppermute(sent, ("rep", "grp"), route))
-    out_piece = add_parts(out_parts, bf16)
-    for bit in reversed(range(low_bits, all_bits)):
-        out_piece = add_parts(halve_rows(out_piece, bit, reps, 0), f32)
-    final_output = out_piece.reshape(D // reps, own).T
+        received.append(lax.ppermute(sent, (REP, GRP), route))
     final_down = add_parts(down_last, f32).reshape(D // reps, hidden_own).T
     route = []
     for r in range(reps):
         row_part, lane_part = piece_of(r, reps, size)
         for g in range(size):
             route.append((r * size + g, (g * share + row_part) * size + lane_part))
-    final_up = lax.ppermute(add_parts(up_last, bf16), ("rep", "grp"), route).astype(f32)
+    final_up = lax.ppermute(add_parts(up_parts, bf16).reshape(own, hidden_own // share), (REP, GRP), route).astype(f32)
 
     received = jnp.stack(received)
     owner = jnp.array(origin, jnp.int32)[rep_rank]
@@ -639,24 +635,24 @@
 
 def solution(mesh):
     in_specs = (
-        P("rep", "grp", None),
-        P("rep", None),
-        P("rep", "grp", None),
-        P("grp", None),
-        P("grp", None),
-        P("grp", None),
-        P("grp", None),
-    ) + (P("grp"),) * 9
+        P(REP, GRP, None),
+        P(REP, None),
+        P(REP, GRP, None),
+        P(GRP, None),
+        P(GRP, None),
+        P(GRP, None),
+        P(GRP, None),
+    ) + (P(GRP),) * 9
     out_specs = (
-        P("rep", "grp", None),
-        P("rep", "grp", None),
-        P("grp", "rep"),
-        P("grp", "rep"),
-        P("grp", "rep"),
-        P("grp", "rep"),
+        P(REP, GRP, None),
+        P(REP, GRP, None),
+        P(GRP, REP),
+        P(GRP, REP),
+        P(GRP, REP),
+        P(GRP, REP),
     ) + (P(),) * 9
 
     def body(*args):
-        return shards(mesh.shape["rep"], mesh.shape["grp"], *args)
+        return shards(mesh.shape[REP], mesh.shape[GRP], *args)
 
     return jax.shard_map(body, mesh=mesh, in_specs=in_specs, out_specs=out_specs, check_vma=False)

time: 343 us -> 344 us (level)
  the two profiles are of different devices: /device:TPU:1 before, /device:TPU:0 now
where the time goes in v2:
time: 344 us; the launch traced here: 342 us
  waiting for transfers between devices  147 us (43%)
  starting transfers between devices  58.5 us (17%)
  local copies, waits for them, and re-layouts  43.2 us (13%)
  other arithmetic  34.3 us (10%)
  matrix products  30.1 us (9%)
  Pallas kernels  28 us (8%)
    ppermute x40, waiting for transfers between devices, swap(): return lax.ppermute(value, axis, [(i, i ^ bit) for i in range(size)])  135 us
    ppermute x40, starting transfers between devices, swap(): return lax.ppermute(value, axis, [(i, i ^ bit) for i in range(size)])  43.9 us
    dot_general x12, matrix products, contract(): lax.dot_general(left, right, (((left_dim,), (right_dim,)), ((), ())), pre...  30.1 us
    ppermute x3, waiting for transfers between devices, shards(): received.append(lax.ppermute(sent, (REP, GRP), route))  11.2 us
    pallas_call x1, Pallas kernels, attend(): pl.pallas_call(lambda *refs: attend_kernel(blocks, *refs), grid_spec=pltp...  9.38 us
    pallas_call x1, Pallas kernels, attend_back(): pl.pallas_call(lambda *refs: attend_back_kernel(blocks, *refs), grid_spec...  9.01 us
    unnamed x98, local copies, waits for them, and re-layouts  8.24 us
  transfers between devices with their start and end apart: 47, of which 19 were waited for; matrix products, arithmetic and copies ran while one was open for 25% of the time, Pallas kernels for 4%

profile of v2, /device:TPU:0, one launch (start us, length us, event | category | flops | bytes accessed | tf_op | source)
XLA Modules:
  0.0 342.5 jit_solution(15893972438122430551)
XLA Ops:
  0.7 3.2 pack.1
  15.7 3.9 %slice_bitcast_fusion.3 = (bf16[1,272,1088]{2,1,0:T(8,128)(2,1)}, bf16[1,272,1088]{2,1,0:T(8,128)(2,1)}, bf16[1,272,1088]{2,1,0:T(8,128)(2,1)}, bf16[1,272,1088]{2,1,0:T(8,128)(2,1)}) fusion(bf16[272,4352]{1,0:T(8,128)(2,1)} %param.23), kind=kLoop, calls=%fused_computation.73 | loop fusion | bytes 4734976 | tf_op jit(solution)/shard_map/stack | solution.py:465
  22.3 10.3 %collective-permute-done.5 = bf16[8,272]{1,0:T(8,128)(2,1)S(1)} collective-permute-done((bf16[8,272]{1,0:T(8,128)(2,1)S(1)}, bf16[8,272]{1,0:T(8,128)(2,1)S(1)}, u32[]{:S(2)}, u32[]{:S(2)}) %collective-permute-start.5) | collective-permute-done | bytes 4384 | tf_op jit(solution)/shard_map/ppermute | solution.py:60
  33.9 4.5 %collective-permute-done.3 = bf16[128,1088]{0,1:T(8,128)(2,1)S(1)} collective-permute-done((bf16[128,1088]{0,1:T(8,128)(2,1)}, bf16[128,1088]{0,1:T(8,128)(2,1)S(1)}, u32[]{:S(2)}, u32[]{:S(2)}) %collective-permute-start.3) | collective-permute-done | bytes 278560 | tf_op jit(solution)/shard_map/ppermute | solution.py:60
  40.7 3.1 shard_map.289
  50.4 9.4 %attend.1 = (bf16[320,512]{1,0:T(8,128)(2,1)}, f32[5,1,512]{2,1,0:T(1,128)}) custom-call(s32[1]{0:T(128)} %bitcast.1.refs_0_.rank_ref, s32[8,512]{1,0:T(8,128)} %add_add_fusion.refs_1_, bf16[960,512]{1,0:T(8,128)(2,1)} %add_convert_fusion.2.refs_2_.refs_3_.refs_4_, bf16[960,512]{1,0:T(8,128)(2,1)} %add_convert_fusion.2.refs_2_.refs_3_.refs_4_, ...), custom_call_target="tpu_custom_call" | custom-call | flops 335544320 | bytes 1310720 | tf_op jit(solution)/shard_map/attend/pallas_call | solution.py:344
  68.1 18.6 %collective-permute-done.8 = bf16[128,1088]{0,1:T(8,128)(2,1)} collective-permute-done((bf16[128,1088]{0,1:T(8,128)(2,1)S(1)}, bf16[128,1088]{0,1:T(8,128)(2,1)}, u32[]{:S(2)}, u32[]{:S(2)}) %collective-permute-start.8) | collective-permute-done | bytes 278560 | tf_op jit(solution)/shard_map/ppermute | solution.py:60
  101.1 2.9 collective-permute-done.16
  108.6 5.3 %collective-permute-done.13.refs_3_ = bf16[272,1088]{1,0:T(8,128)(2,1)} collective-permute-done((bf16[272,1088]{1,0:T(8,128)(2,1)}, bf16[272,1088]{1,0:T(8,128)(2,1)}, u32[]{:S(2)}, u32[]{:S(2)}) %collective-permute-start.13) | collective-permute-done | bytes 591904 | tf_op jit(solution)/shard_map/ppermute | solution.py:60
  113.9 3.3 shard_map.290
  117.2 3.7 %convolution_add_fusion = f32[512,1088]{0,1:T(8,128)S(1)} fusion(bf16[1088,1088]{1,0:T(8,128)(2,1)} %shard_map.290, f32[1088]{0:T(1024)S(1)} %convert_element_type.207, bf16[256,1088]{0,1:T(8,128)(2,1)} %collective-permute-done.10, bf16[128,1088]{0,1:T(8,128)(2,1)} %collective-permute-done.9, bf16[128,1088]{0,1:T(8,128)(2,1)} %add_convert_fusion.10), kind=kOutput, calls=%fused_computation.1 | convolution fusion | flops 1216053248 | bytes 5714176 | tf_op jit(solution)/shard_map/dot_general | solution.py:54
  122.7 4.8 %convert_reduce_fusion.1 = (f32[1088]{0:T(1024)S(1)}, bf16[512,1088]{0,1:T(8,128)(2,1)S(1)}) fusion(f32[512,1088]{0,1:T(8,128)S(1)} %convolution_add_fusion, bf16[1088,1088]{1,0:T(8,128)(2,1)S(1)} %copy-done, bf16[256,1088]{0,1:T(8,128)(2,1)} %collective-permute-done.17, bf16[128,1088]{0,1:T(8,128)(2,1)} %collective-permute-done.16, ...), kind=kOutput, calls=%fused_computation.23 | convolution fusion | flops 1227193344 | bytes 6828288 | tf_op jit(solution)/shard_map/dot_general | solution.py:54
  131.5 2.8 fusion.34
  139.8 3.8 %fusion.33 = f32[1088,1088]{1,0:T(8,128)S(1)} fusion(bf16[256,1088]{0,1:T(8,128)(2,1)} %collective-permute-done.17, bf16[128,1088]{0,1:T(8,128)(2,1)} %collective-permute-done.16, bf16[128,1088]{0,1:T(8,128)(2,1)S(1)} %bitcast.148, f32[512,1088]{0,1:T(8,128)} %copy-done.46), kind=kOutput, calls=%fused_computation.109 | convolution fusion | flops 1220509696 | bytes 8077312 | tf_op jit(solution)/shard_map/dot_general | solution.py:54
  146.9 6.5 %collective-permute-done.19 = bf16[128,1088]{0,1:T(8,128)(2,1)S(1)} collective-permute-done((bf16[128,1088]{0,1:T(8,128)(2,1)S(1)}, bf16[128,1088]{0,1:T(8,128)(2,1)S(1)}, u32[]{:S(2)}, u32[]{:S(2)}) %collective-permute-start.19) | collective-permute-done | bytes 278560 | tf_op jit(solution)/shard_map/ppermute | solution.py:60
  158.4 3.6 %collective-permute-done.22 = bf16[128,1088]{0,1:T(8,128)(2,1)S(1)} collective-permute-done((bf16[128,1088]{0,1:T(8,128)(2,1)S(1)}, bf16[128,1088]{0,1:T(8,128)(2,1)S(1)}, u32[]{:S(2)}, u32[]{:S(2)}) %collective-permute-start.22) | collective-permute-done | bytes 278560 | tf_op jit(solution)/shard_map/ppermute | solution.py:60
  163.7 4.7 %collective-permute-done.35 = bf16[2,1,272,1088]{3,2,1,0:T(8,128)(2,1)} collective-permute-done((bf16[2,1,272,1088]{3,2,1,0:T(8,128)(2,1)}, bf16[2,1,272,1088]{3,2,1,0:T(8,128)(2,1)}, u32[]{:S(2)}, u32[]{:S(2)}) %collective-permute-start.35) | collective-permute-done | bytes 1183776 | tf_op jit(solution)/shard_map/ppermute | solution.py:60
  171.0 23.3 %collective-permute-done.39 = bf16[2,2,1,136,1088]{4,3,2,1,0:T(8,128)(2,1)S(1)} collective-permute-done((bf16[2,2,1,136,1088]{4,3,2,1,0:T(8,128)(2,1)S(1)}, bf16[2,2,1,136,1088]{4,3,2,1,0:T(8,128)(2,1)S(1)}, u32[]{:S(2)}, u32[]{:S(2)}) %collective-permute-start.39) | collective-permute-done | bytes 1183776 | tf_op jit(solution)/shard_map/ppermute | solution.py:60
  200.0 9.0 %back.1 = bf16[3,320,512]{2,1,0:T(8,128)(2,1)} custom-call(s32[1]{0:T(128)} %bitcast.1.refs_0_.rank_ref, s32[8,512]{1,0:T(8,128)} %add_add_fusion.refs_1_, bf16[960,512]{1,0:T(8,128)(2,1)} %add_convert_fusion.2.refs_2_.refs_3_.refs_4_, bf16[960,512]{1,0:T(8,128)(2,1)} %add_convert_fusion.2.refs_2_.refs_3_.refs_4_, ...), custom_call_target="tpu_custom_call" | custom-call | flops 838860800 | bytes 2621440 | tf_op jit(solution)/shard_map/back/pallas_call | solution.py:369
  224.7 2.7 collective-permute-start.37
  229.4 21.6 %collective-permute-done.32 = bf16[2,2,1,136,272]{4,3,2,1,0:T(8,128)(2,1)S(1)} collective-permute-done((bf16[2,2,1,136,272]{4,3,2,1,0:T(8,128)(2,1)S(1)}, bf16[2,2,1,136,272]{4,3,2,1,0:T(8,128)(2,1)S(1)}, u32[]{:S(2)}, u32[]{:S(2)}) %collective-permute-start.32) | collective-permute-done | bytes 295968 | tf_op jit(solution)/shard_map/ppermute | solution.py:60
  251.0 2.6 collective-permute-start.41
  259.4 4.9 %collective-permute-done.33 = bf16[2,1,1,136,272]{4,3,2,1,0:T(8,128)(2,1)S(1)} collective-permute-done((bf16[2,1,1,136,272]{4,3,2,1,0:T(8,128)(2,1)S(1)}, bf16[2,1,1,136,272]{4,3,2,1,0:T(8,128)(2,1)S(1)}, u32[]{:S(2)}, u32[]{:S(2)}) %collective-permute-start.33) | collective-permute-done | bytes 148000 | tf_op jit(solution)/shard_map/ppermute | solution.py:60
  264.3 4.3 %collective-permute-start.38 = (bf16[272,544]{1,0:T(8,128)(2,1)}, bf16[272,544]{1,0:T(8,128)(2,1)}, u32[]{:S(2)}, u32[]{:S(2)}) collective-permute-start(bf16[272,544]{1,0:T(8,128)(2,1)} %fusion.35), channel_id=1, source_target_pairs={{0,0},{1,8},{2,16},{3,24},{4,1},{5,9},{6,17},{7,25},{8,2},{9,10},{... | collective-permute-start | bytes 887816 | tf_op jit(solution)/shard_map/ppermute | solution.py:616
  272.4 2.7 collective-permute-start.34
  286.1 4.9 %collective-permute-done.34 = bf16[1,1,1,136,272]{4,3,2,1,0:T(8,128)(2,1)S(1)} collective-permute-done((bf16[1,1,1,136,272]{4,3,2,1,0:T(8,128)(2,1)S(1)}, bf16[1,1,1,136,272]{4,3,2,1,0:T(8,128)(2,1)S(1)}, u32[]{:S(2)}, u32[]{:S(2)}) %collective-permute-start.34) | collective-permute-done | bytes 74016 | tf_op jit(solution)/shard_map/ppermute | solution.py:60
  293.6 3.5 %collective-permute-done.45 = f32[102,128]{1,0:T(8,128)S(1)} collective-permute-done((f32[102,128]{1,0:T(8,128)S(1)}, f32[102,128]{1,0:T(8,128)S(1)}, u32[]{:S(2)}, u32[]{:S(2)}) %collective-permute-start.45) | collective-permute-done | bytes 52256 | tf_op jit(solution)/shard_map/ppermute | solution.py:60
  297.8 3.0 collective-permute-start.28
  300.8 9.7 %collective-permute-done.46 = f32[102,128]{1,0:T(8,128)S(1)} collective-permute-done((f32[102,128]{1,0:T(8,128)S(1)}, f32[102,128]{1,0:T(8,128)S(1)}, u32[]{:S(2)}, u32[]{:S(2)}) %collective-permute-start.46) | collective-permute-done | bytes 52256 | tf_op jit(solution)/shard_map/ppermute | solution.py:60
  310.5 8.8 %collective-permute-done.28 = bf16[3,272,136]{2,1,0:T(8,128)(2,1)S(1)} collective-permute-done((bf16[3,272,136]{2,1,0:T(8,128)(2,1)S(1)}, bf16[3,272,136]{2,1,0:T(8,128)(2,1)S(1)}, u32[]{:S(2)}, u32[]{:S(2)}) %collective-permute-start.28) | collective-permute-done | bytes 221984 | tf_op jit(solution)/shard_map/ppermute | solution.py:60
  322.5 4.4 %collective-permute-start.30 = (bf16[272,136]{1,0:T(8,128)(2,1)S(1)}, bf16[272,136]{1,0:T(8,128)(2,1)S(1)}, u32[]{:S(2)}, u32[]{:S(2)}) collective-permute-start(bf16[272,136]{1,0:T(8,128)(2,1)S(1)} %get-tuple-element.85), channel_id=1, source_target_pairs={{0,8},{1,0},{2,16},{3,28},{4,9},{5,1},{6,17},{7,29},{8,10},{9,2},{... | collective-permute-start | bytes 221960 | tf_op jit(solution)/shard_map/ppermute | solution.py:609
  329.5 10.0 %collective-permute-done.29 = bf16[272,136]{1,0:T(8,128)(2,1)S(1)} collective-permute-done((bf16[272,136]{1,0:T(8,128)(2,1)S(1)}, bf16[272,136]{1,0:T(8,128)(2,1)S(1)}, u32[]{:S(2)}, u32[]{:S(2)}) %collective-permute-start.29) | collective-permute-done | bytes 74016 | tf_op jit(solution)/shard_map/ppermute | solution.py:609
  (316 shorter events, 131.0 us)
Async XLA Ops:
  3.9 36.8 %collective-permute-start = (bf16[272,960]{1,0:T(8,128)(2,1)}, bf16[272,960]{1,0:T(8,128)(2,1)}, u32[]{:S(2)}, u32[]{:S(2)}) collective-permute-start(bf16[272,960]{1,0:T(8,128)(2,1)} %get-tuple-element.30), channel_id=1, source_target_pairs={{0,1},{1,0},{2,3},{3,2},{4,5},{5,4},{6,7},{7,6},{8,9},{9,8},{10,11... | collective-permute-start | bytes 1566728 | tf_op jit(solution)/shard_map/ppermute | solution.py:60
  4.4 36.3 %collective-permute-start.1 = (bf16[272,960]{1,0:T(8,128)(2,1)}, bf16[272,960]{1,0:T(8,128)(2,1)}, u32[]{:S(2)}, u32[]{:S(2)}) collective-permute-start(bf16[272,960]{1,0:T(8,128)(2,1)} %get-tuple-element.31), channel_id=1, source_target_pairs={{0,2},{1,3},{2,0},{3,1},{4,6},{5,7},{6,4},{7,5},{8,10},{9,11},{10,... | collective-permute-start | bytes 1566728 | tf_op jit(solution)/shard_map/ppermute | solution.py:60
  6.9 33.8 %collective-permute-start.2 = (bf16[272,960]{1,0:T(8,128)(2,1)}, bf16[272,960]{1,0:T(8,128)(2,1)}, u32[]{:S(2)}, u32[]{:S(2)}) collective-permute-start(bf16[272,960]{1,0:T(8,128)(2,1)} %get-tuple-element.32), channel_id=1, source_target_pairs={{0,3},{1,2},{2,1},{3,0},{4,7},{5,6},{6,5},{7,4},{8,11},{9,10},{10,... | collective-permute-start | bytes 1566728 | tf_op jit(solution)/shard_map/ppermute | solution.py:60
  12.5 20.1 %collective-permute-start.5 = (bf16[8,272]{1,0:T(8,128)(2,1)S(1)}, bf16[8,272]{1,0:T(8,128)(2,1)S(1)}, u32[]{:S(2)}, u32[]{:S(2)}) collective-permute-start(bf16[8,272]{1,0:T(8,128)(2,1)S(1)} %concatenate.63), channel_id=1, source_target_pairs={{0,2},{1,3},{2,0},{3,1},{4,6},{5,7},{6,4},{7,5},{8,10},{9,11},{10,... | collective-permute-start | bytes 13064 | tf_op jit(solution)/shard_map/ppermute | solution.py:60
  14.3 24.1 %collective-permute-start.3 = (bf16[128,1088]{0,1:T(8,128)(2,1)}, bf16[128,1088]{0,1:T(8,128)(2,1)S(1)}, u32[]{:S(2)}, u32[]{:S(2)}) collective-permute-start(bf16[128,1088]{0,1:T(8,128)(2,1)} %bitcast.132), channel_id=1, source_target_pairs={{0,2},{1,3},{2,0},{3,1},{4,6},{5,7},{6,4},{7,5},{8,10},{9,11},{10,... | collective-permute-start | bytes 835592 | tf_op jit(solution)/shard_map/ppermute | solution.py:60
  64.4 32.7 %collective-permute-start.12 = (bf16[272,1088]{1,0:T(8,128)(2,1)}, bf16[272,1088]{1,0:T(8,128)(2,1)}, u32[]{:S(2)}, u32[]{:S(2)}) collective-permute-start(bf16[272,1088]{1,0:T(8,128)(2,1)} %get-tuple-element.66), channel_id=1, source_target_pairs={{0,2},{1,3},{2,0},{3,1},{4,7},{5,6},{6,5},{7,4},{8,10},{9,11},{10,... | collective-permute-start | bytes 1775624 | tf_op jit(solution)/shard_map/ppermute | solution.py:470
  67.4 19.4 %collective-permute-start.8 = (bf16[128,1088]{0,1:T(8,128)(2,1)S(1)}, bf16[128,1088]{0,1:T(8,128)(2,1)}, u32[]{:S(2)}, u32[]{:S(2)}) collective-permute-start(bf16[128,1088]{0,1:T(8,128)(2,1)S(1)} %slice.327), channel_id=1, source_target_pairs={{0,2},{1,3},{2,0},{3,1},{4,6},{5,7},{6,4},{7,5},{8,10},{9,11},{10,... | collective-permute-start | bytes 835592 | tf_op jit(solution)/shard_map/ppermute | solution.py:60
  92.7 104.3 %collective-permute-start.20 = (bf16[48,1088]{1,0:T(8,128)(2,1)}, bf16[48,1088]{1,0:T(8,128)(2,1)}, u32[]{:S(2)}, u32[]{:S(2)}) collective-permute-start(bf16[48,1088]{1,0:T(8,128)(2,1)} %get-tuple-element.74), channel_id=1, source_target_pairs={{0,1},{1,2},{2,3},{4,5},{5,6},{6,7},{8,9},{9,10},{10,11},{12,13},{... | collective-permute-start | bytes 313352 | tf_op jit(solution)/shard_map/ppermute | solution.py:479
  94.7 12.8 %collective-permute-start.11 = (bf16[272,1088]{1,0:T(8,128)(2,1)}, bf16[272,1088]{1,0:T(8,128)(2,1)}, u32[]{:S(2)}, u32[]{:S(2)}) collective-permute-start(bf16[272,1088]{1,0:T(8,128)(2,1)} %get-tuple-element.67), channel_id=1, source_target_pairs={{0,1},{1,0},{2,3},{3,2},{4,5},{5,4},{6,7},{7,6},{8,9},{9,8},{10,11... | collective-permute-start | bytes 1775624 | tf_op jit(solution)/shard_map/ppermute | solution.py:60
  97.1 16.8 %collective-permute-start.13 = (bf16[272,1088]{1,0:T(8,128)(2,1)}, bf16[272,1088]{1,0:T(8,128)(2,1)}, u32[]{:S(2)}, u32[]{:S(2)}) collective-permute-start(bf16[272,1088]{1,0:T(8,128)(2,1)} %collective-permute-done.12.refs_2_), channel_id=1, source_target_pairs={{0,4},{4,0},{8,12},{12,8},{16,20},{20,16},{24,28},{28,24},{1,5},{5... | collective-permute-start | bytes 1775624 | tf_op jit(solution)/shard_map/ppermute | solution.py:60
  101.1 16.1 %collective-permute-start.10 = (bf16[256,1088]{0,1:T(8,128)(2,1)}, bf16[256,1088]{0,1:T(8,128)(2,1)}, u32[]{:S(2)}, u32[]{:S(2)}) collective-permute-start(bf16[256,1088]{0,1:T(8,128)(2,1)} %pad_maximum_fusion.7), channel_id=1, source_target_pairs={{0,1},{1,0},{2,3},{3,2},{4,5},{5,4},{6,7},{7,6},{8,9},{9,8},{10,11... | collective-permute-start | bytes 1671176 | tf_op jit(solution)/shard_map/ppermute | solution.py:60
  104.1 93.5 %collective-permute-start.21 = (bf16[48,1088]{1,0:T(8,128)(2,1)S(1)}, bf16[48,1088]{1,0:T(8,128)(2,1)}, u32[]{:S(2)}, u32[]{:S(2)}) collective-permute-start(bf16[48,1088]{1,0:T(8,128)(2,1)S(1)} %get-tuple-element.73), channel_id=1, source_target_pairs={{1,0},{2,1},{3,2},{5,4},{6,5},{7,6},{9,8},{10,9},{11,10},{13,12},{... | collective-permute-start | bytes 313352 | tf_op jit(solution)/shard_map/ppermute | solution.py:480
  107.4 15.3 %collective-permute-start.17 = (bf16[256,1088]{0,1:T(8,128)(2,1)}, bf16[256,1088]{0,1:T(8,128)(2,1)}, u32[]{:S(2)}, u32[]{:S(2)}) collective-permute-start(bf16[256,1088]{0,1:T(8,128)(2,1)} %pad_maximum_fusion.8), channel_id=1, source_target_pairs={{0,1},{1,0},{2,3},{3,2},{4,5},{5,4},{6,7},{7,6},{8,9},{9,8},{10,11... | collective-permute-start | bytes 1671176 | tf_op jit(solution)/shard_map/ppermute | solution.py:60
  130.1 13.5 %collective-permute-start.18 = (bf16[256,1088]{0,1:T(8,128)(2,1)}, bf16[256,1088]{0,1:T(8,128)(2,1)}, u32[]{:S(2)}, u32[]{:S(2)}) collective-permute-start(bf16[256,1088]{0,1:T(8,128)(2,1)} %slice.321), channel_id=1, source_target_pairs={{0,1},{1,0},{2,3},{3,2},{4,5},{5,4},{6,7},{7,6},{8,9},{9,8},{10,11... | collective-permute-start | bytes 1671176 | tf_op jit(solution)/shard_map/ppermute | solution.py:60
  131.0 23.7 %collective-permute-start.14 = (bf16[256,1088]{0,1:T(8,128)(2,1)}, bf16[256,1088]{0,1:T(8,128)(2,1)}, u32[]{:S(2)}, u32[]{:S(2)}) collective-permute-start(bf16[256,1088]{0,1:T(8,128)(2,1)} %slice.322), channel_id=1, source_target_pairs={{0,1},{1,0},{2,3},{3,2},{4,5},{5,4},{6,7},{7,6},{8,9},{9,8},{10,11... | collective-permute-start | bytes 1671176 | tf_op jit(solution)/shard_map/ppermute | solution.py:60
  137.7 30.7 %collective-permute-start.35 = (bf16[2,1,272,1088]{3,2,1,0:T(8,128)(2,1)}, bf16[2,1,272,1088]{3,2,1,0:T(8,128)(2,1)}, u32[]{:S(2)}, u32[]{:S(2)}) collective-permute-start(bf16[2,1,272,1088]{3,2,1,0:T(8,128)(2,1)} %dynamic-slice_convert_fusion.1), channel_id=1, source_target_pairs={{0,4},{4,0},{8,12},{12,8},{16,20},{20,16},{24,28},{28,24},{1,5},{5... | collective-permute-start | bytes 3551240 | tf_op jit(solution)/shard_map/ppermute | solution.py:60
  153.4 40.9 %collective-permute-start.39 = (bf16[2,2,1,136,1088]{4,3,2,1,0:T(8,128)(2,1)S(1)}, bf16[2,2,1,136,1088]{4,3,2,1,0:T(8,128)(2,1)S(1)}, u32[]{:S(2)}, u32[]{:S(2)}) collective-permute-start(bf16[2,2,1,136,1088]{4,3,2,1,0:T(8,128)(2,1)S(1)} %dynamic-slice_convert_fusion), channel_id=1, source_target_pairs={{0,4},{4,0},{8,12},{12,8},{16,20},{20,16},{24,28},{28,24},{1,5},{5... | collective-permute-start | bytes 3551240 | tf_op jit(solution)/shard_map/ppermute | solution.py:60
  162.0 107.2 %collective-permute-start.15 = (bf16[128,1088]{0,1:T(8,128)(2,1)}, bf16[128,1088]{0,1:T(8,128)(2,1)}, u32[]{:S(2)}, u32[]{:S(2)}) collective-permute-start(bf16[128,1088]{0,1:T(8,128)(2,1)} %slice.326), channel_id=1, source_target_pairs={{0,2},{1,3},{2,0},{3,1},{4,6},{5,7},{6,4},{7,5},{8,10},{9,11},{10,... | collective-permute-start | bytes 835592 | tf_op jit(solution)/shard_map/ppermute | solution.py:60
  168.5 29.1 %collective-permute-start.23 = (bf16[256,1088]{0,1:T(8,128)(2,1)S(1)}, bf16[256,1088]{0,1:T(8,128)(2,1)S(1)}, u32[]{:S(2)}, u32[]{:S(2)}) collective-permute-start(bf16[256,1088]{0,1:T(8,128)(2,1)S(1)} %pad_maximum_fusion.9), channel_id=1, source_target_pairs={{0,1},{1,0},{2,3},{3,2},{4,5},{5,4},{6,7},{7,6},{8,9},{9,8},{10,11... | collective-permute-start | bytes 1671176 | tf_op jit(solution)/shard_map/ppermute | solution.py:60
  194.3 28.7 %collective-permute-start.36 = (bf16[1,1,272,1088]{3,2,1,0:T(8,128)(2,1)}, bf16[1,1,272,1088]{3,2,1,0:T(8,128)(2,1)}, u32[]{:S(2)}, u32[]{:S(2)}) collective-permute-start(bf16[1,1,272,1088]{3,2,1,0:T(8,128)(2,1)} %constant_dynamic-slice_fusion.2), channel_id=1, source_target_pairs={{0,8},{4,12},{8,0},{12,4},{16,24},{20,28},{24,16},{28,20},{1,9},{5... | collective-permute-start | bytes 1775624 | tf_op jit(solution)/shard_map/ppermute | solution.py:60
  197.1 27.6 %collective-permute-start.40 = (bf16[2,1,1,136,1088]{4,3,2,1,0:T(8,128)(2,1)}, bf16[2,1,1,136,1088]{4,3,2,1,0:T(8,128)(2,1)}, u32[]{:S(2)}, u32[]{:S(2)}) collective-permute-start(bf16[2,1,1,136,1088]{4,3,2,1,0:T(8,128)(2,1)} %constant_dynamic-slice_fusion.1), channel_id=1, source_target_pairs={{0,8},{4,12},{8,0},{12,4},{16,24},{20,28},{24,16},{28,20},{1,9},{5... | collective-permute-start | bytes 1775624 | tf_op jit(solution)/shard_map/ppermute | solution.py:60
  213.5 40.2 %collective-permute-start.24 = (bf16[256,1088]{0,1:T(8,128)(2,1)}, bf16[256,1088]{0,1:T(8,128)(2,1)}, u32[]{:S(2)}, u32[]{:S(2)}) collective-permute-start(bf16[256,1088]{0,1:T(8,128)(2,1)} %slice.320), channel_id=1, source_target_pairs={{0,1},{1,0},{2,3},{3,2},{4,5},{5,4},{6,7},{7,6},{8,9},{9,8},{10,11... | collective-permute-start | bytes 1671176 | tf_op jit(solution)/shard_map/ppermute | solution.py:60
  218.4 57.1 %collective-permute-start.26 = (bf16[2,1,272,816]{3,2,1,0:T(8,128)(2,1)}, bf16[2,1,272,816]{3,2,1,0:T(8,128)(2,1)}, u32[]{:S(2)}, u32[]{:S(2)}) collective-permute-start(bf16[2,1,272,816]{3,2,1,0:T(8,128)(2,1)} %dynamic-slice_convert_fusion.2), channel_id=1, source_target_pairs={{0,4},{4,0},{8,12},{12,8},{16,20},{20,16},{24,28},{28,24},{1,5},{5... | collective-permute-start | bytes 2663432 | tf_op jit(solution)/shard_map/ppermute | solution.py:60
  222.9 28.1 %collective-permute-start.32 = (bf16[2,2,1,136,272]{4,3,2,1,0:T(8,128)(2,1)S(1)}, bf16[2,2,1,136,272]{4,3,2,1,0:T(8,128)(2,1)S(1)}, u32[]{:S(2)}, u32[]{:S(2)}) collective-permute-start(bf16[2,2,1,136,272]{4,3,2,1,0:T(8,128)(2,1)S(1)} %dynamic-slice_convert_fusion.3), channel_id=1, source_target_pairs={{0,4},{4,0},{8,12},{12,8},{16,20},{20,16},{24,28},{28,24},{1,5},{5... | collective-permute-start | bytes 887816 | tf_op jit(solution)/shard_map/ppermute | solution.py:60
  224.7 32.1 %collective-permute-start.37 = (bf16[1,1,272,544]{3,2,1,0:T(8,128)(2,1)S(1)}, bf16[1,1,272,544]{3,2,1,0:T(8,128)(2,1)S(1)}, u32[]{:S(2)}, u32[]{:S(2)}) collective-permute-start(bf16[1,1,272,544]{3,2,1,0:T(8,128)(2,1)S(1)} %broadcast_select_fusion.2), channel_id=1, source_target_pairs={{0,16},{4,20},{8,24},{12,28},{16,0},{20,4},{24,8},{28,12},{1,17},{... | collective-permute-start | bytes 887816 | tf_op jit(solution)/shard_map/ppermute | solution.py:60
  251.0 30.0 %collective-permute-start.41 = (bf16[1,1,1,136,1088]{4,3,2,1,0:T(8,128)(2,1)}, bf16[1,1,1,136,1088]{4,3,2,1,0:T(8,128)(2,1)}, u32[]{:S(2)}, u32[]{:S(2)}) collective-permute-start(bf16[1,1,1,136,1088]{4,3,2,1,0:T(8,128)(2,1)} %constant_dynamic-slice_fusion), channel_id=1, source_target_pairs={{0,16},{4,20},{8,24},{12,28},{16,0},{20,4},{24,8},{28,12},{1,17},{... | collective-permute-start | bytes 887816 | tf_op jit(solution)/shard_map/ppermute | solution.py:60
  264.3 27.4 %collective-permute-start.38 = (bf16[272,544]{1,0:T(8,128)(2,1)}, bf16[272,544]{1,0:T(8,128)(2,1)}, u32[]{:S(2)}, u32[]{:S(2)}) collective-permute-start(bf16[272,544]{1,0:T(8,128)(2,1)} %fusion.35), channel_id=1, source_target_pairs={{0,0},{1,8},{2,16},{3,24},{4,1},{5,9},{6,17},{7,25},{8,2},{9,10},{... | collective-permute-start | bytes 887816 | tf_op jit(solution)/shard_map/ppermute | solution.py:616
  272.4 18.6 %collective-permute-start.34 = (bf16[1,1,1,136,272]{4,3,2,1,0:T(8,128)(2,1)S(1)}, bf16[1,1,1,136,272]{4,3,2,1,0:T(8,128)(2,1)S(1)}, u32[]{:S(2)}, u32[]{:S(2)}) collective-permute-start(bf16[1,1,1,136,272]{4,3,2,1,0:T(8,128)(2,1)S(1)} %constant_dynamic-slice_fusion.3), channel_id=1, source_target_pairs={{0,16},{4,20},{8,24},{12,28},{16,0},{20,4},{24,8},{28,12},{1,17},{... | collective-permute-start | bytes 221960 | tf_op jit(solution)/shard_map/ppermute | solution.py:60
  277.6 19.6 %collective-permute-start.27 = (bf16[1,1,272,816]{3,2,1,0:T(8,128)(2,1)S(1)}, bf16[1,1,272,816]{3,2,1,0:T(8,128)(2,1)S(1)}, u32[]{:S(2)}, u32[]{:S(2)}) collective-permute-start(bf16[1,1,272,816]{3,2,1,0:T(8,128)(2,1)S(1)} %constant_dynamic-slice_fusion.7), channel_id=1, source_target_pairs={{0,8},{4,12},{8,0},{12,4},{16,24},{20,28},{24,16},{28,20},{1,9},{5... | collective-permute-start | bytes 1331720 | tf_op jit(solution)/shard_map/ppermute | solution.py:60
  284.1 13.0 %collective-permute-start.45 = (f32[102,128]{1,0:T(8,128)S(1)}, f32[102,128]{1,0:T(8,128)S(1)}, u32[]{:S(2)}, u32[]{:S(2)}) collective-permute-start(f32[102,128]{1,0:T(8,128)S(1)} %add.251), channel_id=1, source_target_pairs={{0,8},{4,12},{8,0},{12,4},{16,24},{20,28},{24,16},{28,20},{1,9},{5... | collective-permute-start | bytes 156680 | tf_op jit(solution)/shard_map/ppermute | solution.py:60
  297.1 13.5 %collective-permute-start.46 = (f32[102,128]{1,0:T(8,128)S(1)}, f32[102,128]{1,0:T(8,128)S(1)}, u32[]{:S(2)}, u32[]{:S(2)}) collective-permute-start(f32[102,128]{1,0:T(8,128)S(1)} %add.252), channel_id=1, source_target_pairs={{0,16},{4,20},{8,24},{12,28},{16,0},{20,4},{24,8},{28,12},{1,17},{... | collective-permute-start | bytes 156680 | tf_op jit(solution)/shard_map/ppermute | solution.py:60
  297.8 21.5 %collective-permute-start.28 = (bf16[3,272,136]{2,1,0:T(8,128)(2,1)S(1)}, bf16[3,272,136]{2,1,0:T(8,128)(2,1)S(1)}, u32[]{:S(2)}, u32[]{:S(2)}) collective-permute-start(bf16[3,272,136]{2,1,0:T(8,128)(2,1)S(1)} %broadcast_select_fusion.1), channel_id=1, source_target_pairs={{0,16},{4,20},{8,24},{12,28},{16,0},{20,4},{24,8},{28,12},{1,17},{... | collective-permute-start | bytes 665864 | tf_op jit(solution)/shard_map/ppermute | solution.py:60
  (64 other events, 706.3 us)

commit v3 on v2

--- a/solution.py
+++ b/solution.py
@@ -235,10 +235,14 @@
 
 
 def piece_of(rep, reps, size):
-    row_part = 0
-    for bit in range(log2(size), log2(reps)):
-        row_part = 2 * row_part + ((rep >> bit) & 1)
-    return row_part, rep & (size - 1)
+    row_part, lane_part = 0, 0
+    for bit in range(log2(reps)):
+        taken = (rep >> bit) & 1
+        if bit < log2(reps // size):
+            row_part = 2 * row_part + taken
+        else:
+            lane_part = 2 * lane_part + taken
+    return row_part, lane_part
 
 
 def match_rounds(reps, kinds):
@@ -516,24 +520,23 @@
     grad_c_part = contract(grad_pre, up_cols, 1, 1)
     grad_c = group_scatter_sum(grad_c_part, size)
     grad_down = contract(grad_rows, hidden, 0, 0)
-    grad_up = contract(normal_c, grad_pre, 0, 0)
+    grad_up = contract(grad_pre, normal_c, 0, 0)
     layer_part = contract(hidden, down_weight, 1, 0)
 
     share = reps // size
-    low_bits, all_bits = log2(size), log2(reps)
+    row_bits, all_bits = log2(share), log2(reps)
     down_axis = lambda bit: all_bits - 1 - bit
-    row_axis = lambda bit: low_bits - 1 - bit
 
     def step_natural(parts, bit, dtype=bf16):
         return halve_rows(add_parts(parts, dtype), bit, reps, down_axis(bit))
 
     def step_piece(value, bit):
-        if bit < low_bits:
-            return halve_rows(value, bit, reps, row_axis(bit))
+        if bit < row_bits:
+            return halve_rows(value, bit, reps, value.ndim - 2 - row_bits + bit)
         return halve_lanes(value, bit, reps)
 
     down_parts = halve_rows(natural_rows(grad_down, reps), 0, reps, down_axis(0))
-    up_parts = step_piece(grad_up.reshape((2,) * low_bits + (own, hidden_own)), 0)
+    up_parts = step_piece(grad_up.reshape((2,) * row_bits + (hidden_own // share, D)), 0)
 
     grad_float = cotangent[0].astype(f32)
     grad_resid = grad_float + norm_back(grad_c, normed_second, inv_second, vectors[5])
@@ -545,8 +548,8 @@
         down_parts = step_natural(down_parts, step)
     grad_packed_rows = attend_back(projected, mixed, grad_mixed, totals, bounds, rank, size, heads)
     grad_mine = cut(grad_packed_rows, offset, own, 1)
-    grad_packed = contract(normal_a, grad_mine.reshape(3 * own, seq), 0, 1)
-    packed_parts = step_piece(grad_packed.reshape((2,) * low_bits + (own, 3 * own)), 0)
+    grad_packed = contract(grad_mine.reshape(3 * own, seq), normal_a, 1, 0)
+    packed_parts = step_piece(grad_packed.reshape((3,) + (2,) * row_bits + (own // share, D)), 0)
 
     down_last = step_natural(down_parts, all_bits - 1)
     for step in range(1, all_bits):
@@ -585,12 +588,9 @@
     )
     sums = sum_over(sum_over(sums.reshape(-1, 128), GRP, size), REP, reps)
 
-    for bit in range(1, low_bits):
+    for bit in range(1, all_bits):
         packed_parts = step_piece(add_parts(packed_parts, bf16), bit)
-    piece = add_parts(packed_parts, bf16).reshape(own, 3 * own)
-    piece = jnp.stack([piece[:, own * t : own * (t + 1)] for t in range(3)])
-    for bit in range(low_bits, all_bits):
-        piece = add_parts(halve_lanes(piece, bit, reps), bf16)
+    piece = add_parts(packed_parts, bf16).reshape(3, own // share, own)
     rounds = match_rounds(reps, 3)
     table = jnp.array(rounds, jnp.int32)
     unit = rank * share + piece_of(rep_rank, reps, size)[0]
@@ -613,13 +613,11 @@
         row_part, lane_part = piece_of(r, reps, size)
         for g in range(size):
             route.append((r * size + g, (g * share + row_part) * size + lane_part))
-    final_up = lax.ppermute(add_parts(up_parts, bf16).reshape(own, hidden_own // share), (REP, GRP), route).astype(f32)
+    final_up = lax.ppermute(add_parts(up_parts, bf16).reshape(hidden_own // share, own), (REP, GRP), route).astype(f32).T
 
     received = jnp.stack(received)
     owner = jnp.array(origin, jnp.int32)[rep_rank]
-    final_packed = jnp.concatenate(
-        [pick(received, owner[k], 0) for k in range(3)], axis=1
-    ).astype(f32)
+    final_packed = jnp.concatenate([pick(received, owner[k], 0) for k in range(3)]).astype(f32).T
 
     ends = [D, 2 * D, 3 * D, 4 * D, 5 * D, 6 * D, 7 * D, 7 * D + hidden_all]
     return (

time: 344 us -> 357 us (1.038)
  the two profiles are of different devices: /device:TPU:0 before, /device:TPU:1 now
where the time goes in v3:
time: 357 us; the launch traced here: 355 us
  waiting for transfers between devices  142 us (40%)
  starting transfers between devices  64.3 us (18%)
  local copies, waits for them, and re-layouts  48.1 us (13%)
  other arithmetic  38.7 us (11%)
  matrix products  32.5 us (9%)
  Pallas kernels  27.9 us (8%)
    ppermute x40, waiting for transfers between devices, swap(): return lax.ppermute(value, axis, [(i, i ^ bit) for i in range(size)])  134 us
    ppermute x40, starting transfers between devices, swap(): return lax.ppermute(value, axis, [(i, i ^ bit) for i in range(size)])  47.4 us
    dot_general x12, matrix products, contract(): lax.dot_general(left, right, (((left_dim,), (right_dim,)), ((), ())), pre...  32.5 us
    pallas_call x1, Pallas kernels, attend(): pl.pallas_call(lambda *refs: attend_kernel(blocks, *refs), grid_spec=pltp...  9.36 us
    pallas_call x1, Pallas kernels, attend_back(): pl.pallas_call(lambda *refs: attend_back_kernel(blocks, *refs), grid_spec...  9.01 us
    ppermute x3, waiting for transfers between devices, shards(): received.append(lax.ppermute(sent, (REP, GRP), route))  8.58 us
    convert_element_type x9, other arithmetic, add_parts(): return total.astype(dtype)  7.43 us
  transfers between devices with their start and end apart: 47, of which 21 were waited for; matrix products, arithmetic and copies ran while one was open for 28% of the time, Pallas kernels for 4%

profile of v3, /device:TPU:1, one launch (start us, length us, event | category | flops | bytes accessed | tf_op | source)
XLA Modules:
  0.0 355.4 jit_solution(14774088020367538944)
XLA Ops:
  0.7 3.2 pack.1
  3.9 2.7 collective-permute-start.1
  15.1 3.9 %slice_bitcast_fusion.3 = (bf16[1,272,1088]{2,1,0:T(8,128)(2,1)}, bf16[1,272,1088]{2,1,0:T(8,128)(2,1)}, bf16[1,272,1088]{2,1,0:T(8,128)(2,1)}, bf16[1,272,1088]{2,1,0:T(8,128)(2,1)}) fusion(bf16[272,4352]{1,0:T(8,128)(2,1)} %param.23), kind=kLoop, calls=%fused_computation.76 | loop fusion | bytes 4734976 | tf_op jit(solution)/shard_map/stack | solution.py:469
  20.1 11.8 %collective-permute-done.5 = bf16[8,272]{1,0:T(8,128)(2,1)} collective-permute-done((bf16[8,272]{1,0:T(8,128)(2,1)S(1)}, bf16[8,272]{1,0:T(8,128)(2,1)}, u32[]{:S(2)}, u32[]{:S(2)}) %collective-permute-start.5) | collective-permute-done | bytes 4384 | tf_op jit(solution)/shard_map/ppermute | solution.py:60
  31.9 2.7 concatenate.64
  46.8 3.1 shard_map.289
  53.5 3.7 %add_convert_fusion.2.refs_2_.refs_3_.refs_4_ = bf16[960,512]{1,0:T(8,128)(2,1)} fusion(bf16[1088,960]{1,0:T(8,128)(2,1)S(1)} %copy-done.20, f32[960]{0:T(1024)S(1)} %copy-done.60, f32[1088]{0:T(1024)S(1)} %copy-done.55, f32[1088]{0:T(1024)S(1)} %mul.196, f32[512]{0:T(512)S(1)} %add_rsqrt_fusion, f32[512]{0:T(512)S(1)} %broadcast_multiply_fusion, ...), kind=kOutput, calls=%fused_computation.25 | convolution fusion | flops 1076658176 | bytes 4202752 | tf_op jit(solution)/shard_map/dot_general | solution.py:54
  57.2 9.4 %attend.1 = (bf16[320,512]{1,0:T(8,128)(2,1)}, f32[5,1,512]{2,1,0:T(1,128)}) custom-call(s32[1]{0:T(128)} %bitcast.1.refs_0_.rank_ref, s32[8,512]{1,0:T(8,128)} %add_add_fusion.refs_1_, bf16[960,512]{1,0:T(8,128)(2,1)} %add_convert_fusion.2.refs_2_.refs_3_.refs_4_, bf16[960,512]{1,0:T(8,128)(2,1)} %add_convert_fusion.2.refs_2_.refs_3_.refs_4_, ...), custom_call_target="tpu_custom_call" | custom-call | flops 335544320 | bytes 1310720 | tf_op jit(solution)/shard_map/attend/pallas_call | solution.py:348
  73.8 18.1 %collective-permute-done.8 = bf16[128,1088]{0,1:T(8,128)(2,1)} collective-permute-done((bf16[128,1088]{0,1:T(8,128)(2,1)S(1)}, bf16[128,1088]{0,1:T(8,128)(2,1)}, u32[]{:S(2)}, u32[]{:S(2)}) %collective-permute-start.8) | collective-permute-done | bytes 278560 | tf_op jit(solution)/shard_map/ppermute | solution.py:60
  97.7 3.4 collective-permute-start.20
  114.6 4.8 %collective-permute-done.13.refs_3_ = bf16[272,1088]{1,0:T(8,128)(2,1)} collective-permute-done((bf16[272,1088]{1,0:T(8,128)(2,1)}, bf16[272,1088]{1,0:T(8,128)(2,1)}, u32[]{:S(2)}, u32[]{:S(2)}) %collective-permute-start.13) | collective-permute-done | bytes 591904 | tf_op jit(solution)/shard_map/ppermute | solution.py:60
  119.4 3.3 shard_map.290
  123.2 3.7 %convolution_add_fusion = f32[512,1088]{0,1:T(8,128)S(1)} fusion(bf16[1088,1088]{1,0:T(8,128)(2,1)} %shard_map.290, f32[1088]{0:T(1024)S(1)} %convert_element_type.203, bf16[256,1088]{0,1:T(8,128)(2,1)} %collective-permute-done.10, bf16[128,1088]{0,1:T(8,128)(2,1)} %collective-permute-done.9, bf16[128,1088]{0,1:T(8,128)(2,1)} %add_convert_fusion.10), kind=kOutput, calls=%fused_computation.1 | convolution fusion | flops 1216053248 | bytes 5714176 | tf_op jit(solution)/shard_map/dot_general | solution.py:54
  128.8 4.8 %convert_reduce_fusion.1 = (f32[1088]{0:T(1024)S(1)}, bf16[512,1088]{0,1:T(8,128)(2,1)S(1)}) fusion(f32[512,1088]{0,1:T(8,128)S(1)} %convolution_add_fusion, bf16[1088,1088]{1,0:T(8,128)(2,1)S(1)} %copy-done, bf16[256,1088]{0,1:T(8,128)(2,1)} %collective-permute-done.17, bf16[128,1088]{0,1:T(8,128)(2,1)} %collective-permute-done.16, ...), kind=kOutput, calls=%fused_computation.23 | convolution fusion | flops 1227193344 | bytes 6828288 | tf_op jit(solution)/shard_map/dot_general | solution.py:54
  138.0 2.9 fusion.35
  146.1 3.8 %fusion.34 = f32[1088,1088]{1,0:T(8,128)S(1)} fusion(bf16[256,1088]{0,1:T(8,128)(2,1)} %collective-permute-done.17, bf16[128,1088]{0,1:T(8,128)(2,1)} %collective-permute-done.16, bf16[128,1088]{0,1:T(8,128)(2,1)S(1)} %bitcast.136, f32[512,1088]{0,1:T(8,128)} %copy-done.70), kind=kOutput, calls=%fused_computation.113 | convolution fusion | flops 1220509696 | bytes 8077312 | tf_op jit(solution)/shard_map/dot_general | solution.py:54
  153.0 6.0 %collective-permute-done.19 = bf16[128,1088]{0,1:T(8,128)(2,1)S(1)} collective-permute-done((bf16[128,1088]{0,1:T(8,128)(2,1)S(1)}, bf16[128,1088]{0,1:T(8,128)(2,1)S(1)}, u32[]{:S(2)}, u32[]{:S(2)}) %collective-permute-start.19) | collective-permute-done | bytes 278560 | tf_op jit(solution)/shard_map/ppermute | solution.py:60
  164.7 3.1 collective-permute-done.22
  169.2 4.0 %collective-permute-done.35 = bf16[1,544,1088]{2,1,0:T(8,128)(2,1)} collective-permute-done((bf16[1,544,1088]{2,1,0:T(8,128)(2,1)}, bf16[1,544,1088]{2,1,0:T(8,128)(2,1)}, u32[]{:S(2)}, u32[]{:S(2)}) %collective-permute-start.35) | collective-permute-done | bytes 1183776 | tf_op jit(solution)/shard_map/ppermute | solution.py:60
  178.3 21.7 %collective-permute-done.39 = bf16[2,2,1,136,1088]{4,3,2,1,0:T(8,128)(2,1)S(1)} collective-permute-done((bf16[2,2,1,136,1088]{4,3,2,1,0:T(8,128)(2,1)S(1)}, bf16[2,2,1,136,1088]{4,3,2,1,0:T(8,128)(2,1)S(1)}, u32[]{:S(2)}, u32[]{:S(2)}) %collective-permute-start.39) | collective-permute-done | bytes 1183776 | tf_op jit(solution)/shard_map/ppermute | solution.py:60
  205.2 9.0 %back.1 = bf16[3,320,512]{2,1,0:T(8,128)(2,1)} custom-call(s32[1]{0:T(128)} %bitcast.1.refs_0_.rank_ref, s32[8,512]{1,0:T(8,128)} %add_add_fusion.refs_1_, bf16[960,512]{1,0:T(8,128)(2,1)} %add_convert_fusion.2.refs_2_.refs_3_.refs_4_, bf16[960,512]{1,0:T(8,128)(2,1)} %add_convert_fusion.2.refs_2_.refs_3_.refs_4_, ...), custom_call_target="tpu_custom_call" | custom-call | flops 838860800 | bytes 2621440 | tf_op jit(solution)/shard_map/back/pallas_call | solution.py:373
  235.6 19.7 %collective-permute-done.32 = bf16[2,2,1,136,272]{4,3,2,1,0:T(8,128)(2,1)S(1)} collective-permute-done((bf16[2,2,1,136,272]{4,3,2,1,0:T(8,128)(2,1)S(1)}, bf16[2,2,1,136,272]{4,3,2,1,0:T(8,128)(2,1)S(1)}, u32[]{:S(2)}, u32[]{:S(2)}) %collective-permute-start.32) | collective-permute-done | bytes 295968 | tf_op jit(solution)/shard_map/ppermute | solution.py:60
  260.2 3.9 %collective-permute-start.38 = (bf16[544,272]{1,0:T(8,128)(2,1)}, bf16[544,272]{1,0:T(8,128)(2,1)}, u32[]{:S(2)}, u32[]{:S(2)}) collective-permute-start(bf16[544,272]{1,0:T(8,128)(2,1)} %fusion.36), channel_id=1, source_target_pairs={{0,0},{1,8},{2,16},{3,24},{4,4},{5,12},{6,20},{7,28},{8,2},{9,10},... | collective-permute-start | bytes 887816 | tf_op jit(solution)/shard_map/ppermute | solution.py:616
  265.5 7.6 %collective-permute-done.41 = bf16[1,1,1,136,1088]{4,3,2,1,0:T(8,128)(2,1)S(1)} collective-permute-done((bf16[1,1,1,136,1088]{4,3,2,1,0:T(8,128)(2,1)S(1)}, bf16[1,1,1,136,1088]{4,3,2,1,0:T(8,128)(2,1)S(1)}, u32[]{:S(2)}, u32[]{:S(2)}) %collective-permute-start.41) | collective-permute-done | bytes 295968 | tf_op jit(solution)/shard_map/ppermute | solution.py:60
  274.1 8.1 %collective-permute-done.25 = bf16[128,1088]{0,1:T(8,128)(2,1)S(1)} collective-permute-done((bf16[128,1088]{0,1:T(8,128)(2,1)S(1)}, bf16[128,1088]{0,1:T(8,128)(2,1)S(1)}, u32[]{:S(2)}, u32[]{:S(2)}) %collective-permute-start.25) | collective-permute-done | bytes 278560 | tf_op jit(solution)/shard_map/ppermute | solution.py:60
  283.4 3.1 fusion.26
  287.4 7.3 %collective-permute-start.42 = (f32[102,128]{1,0:T(8,128)S(1)}, f32[102,128]{1,0:T(8,128)S(1)}, u32[]{:S(2)}, u32[]{:S(2)}) collective-permute-start(f32[102,128]{1,0:T(8,128)S(1)} %bitcast.144), channel_id=1, source_target_pairs={{0,1},{1,0},{2,3},{3,2},{4,5},{5,4},{6,7},{7,6},{8,9},{9,8},{10,11... | collective-permute-start | bytes 156680 | tf_op jit(solution)/shard_map/ppermute | solution.py:60
  297.8 5.1 %collective-permute-start.27 = (bf16[3,1,136,544]{3,2,1,0:T(8,128)(2,1)S(1)}, bf16[3,1,136,544]{3,2,1,0:T(8,128)(2,1)S(1)}, u32[]{:S(2)}, u32[]{:S(2)}) collective-permute-start(bf16[3,1,136,544]{3,2,1,0:T(8,128)(2,1)S(1)} %broadcast_select_fusion.2), channel_id=1, source_target_pairs={{0,8},{4,12},{8,0},{12,4},{16,24},{20,28},{24,16},{28,20},{1,9},{5... | collective-permute-start | bytes 1331720 | tf_op jit(solution)/shard_map/ppermute | solution.py:60
  308.6 7.1 %collective-permute-done.45 = f32[102,128]{1,0:T(8,128)S(1)} collective-permute-done((f32[102,128]{1,0:T(8,128)S(1)}, f32[102,128]{1,0:T(8,128)S(1)}, u32[]{:S(2)}, u32[]{:S(2)}) %collective-permute-start.45) | collective-permute-done | bytes 52256 | tf_op jit(solution)/shard_map/ppermute | solution.py:60
  319.7 15.0 %collective-permute-done.28 = bf16[3,1,136,272]{3,2,1,0:T(8,128)(2,1)S(1)} collective-permute-done((bf16[3,1,136,272]{3,2,1,0:T(8,128)(2,1)S(1)}, bf16[3,1,136,272]{3,2,1,0:T(8,128)(2,1)S(1)}, u32[]{:S(2)}, u32[]{:S(2)}) %collective-permute-start.28) | collective-permute-done | bytes 221984 | tf_op jit(solution)/shard_map/ppermute | solution.py:60
  336.9 3.1 collective-permute-start.31
  343.6 5.2 %collective-permute-done.31 = bf16[136,272]{1,0:T(8,128)(2,1)S(1)} collective-permute-done((bf16[136,272]{1,0:T(8,128)(2,1)S(1)}, bf16[136,272]{1,0:T(8,128)(2,1)S(1)}, u32[]{:S(2)}, u32[]{:S(2)}) %collective-permute-start.31) | collective-permute-done | bytes 74016 | tf_op jit(solution)/shard_map/ppermute | solution.py:609
  (365 shorter events, 139.3 us)
Async XLA Ops:
  3.9 42.9 %collective-permute-start = (bf16[272,960]{1,0:T(8,128)(2,1)}, bf16[272,960]{1,0:T(8,128)(2,1)}, u32[]{:S(2)}, u32[]{:S(2)}) collective-permute-start(bf16[272,960]{1,0:T(8,128)(2,1)} %get-tuple-element.30), channel_id=1, source_target_pairs={{0,1},{1,0},{2,3},{3,2},{4,5},{5,4},{6,7},{7,6},{8,9},{9,8},{10,11... | collective-permute-start | bytes 1566728 | tf_op jit(solution)/shard_map/ppermute | solution.py:60
  3.9 42.9 %collective-permute-start.1 = (bf16[272,960]{1,0:T(8,128)(2,1)}, bf16[272,960]{1,0:T(8,128)(2,1)}, u32[]{:S(2)}, u32[]{:S(2)}) collective-permute-start(bf16[272,960]{1,0:T(8,128)(2,1)} %get-tuple-element.31), channel_id=1, source_target_pairs={{0,2},{1,3},{2,0},{3,1},{4,6},{5,7},{6,4},{7,5},{8,10},{9,11},{10,... | collective-permute-start | bytes 1566728 | tf_op jit(solution)/shard_map/ppermute | solution.py:60
  6.6 40.2 %collective-permute-start.2 = (bf16[272,960]{1,0:T(8,128)(2,1)}, bf16[272,960]{1,0:T(8,128)(2,1)}, u32[]{:S(2)}, u32[]{:S(2)}) collective-permute-start(bf16[272,960]{1,0:T(8,128)(2,1)} %get-tuple-element.32), channel_id=1, source_target_pairs={{0,3},{1,2},{2,1},{3,0},{4,7},{5,6},{6,5},{7,4},{8,11},{9,10},{10,... | collective-permute-start | bytes 1566728 | tf_op jit(solution)/shard_map/ppermute | solution.py:60
  12.2 19.7 %collective-permute-start.5 = (bf16[8,272]{1,0:T(8,128)(2,1)S(1)}, bf16[8,272]{1,0:T(8,128)(2,1)}, u32[]{:S(2)}, u32[]{:S(2)}) collective-permute-start(bf16[8,272]{1,0:T(8,128)(2,1)S(1)} %concatenate.63), channel_id=1, source_target_pairs={{0,2},{1,3},{2,0},{3,1},{4,6},{5,7},{6,4},{7,5},{8,10},{9,11},{10,... | collective-permute-start | bytes 13064 | tf_op jit(solution)/shard_map/ppermute | solution.py:60
  13.9 24.1 %collective-permute-start.3 = (bf16[128,1088]{0,1:T(8,128)(2,1)}, bf16[128,1088]{0,1:T(8,128)(2,1)}, u32[]{:S(2)}, u32[]{:S(2)}) collective-permute-start(bf16[128,1088]{0,1:T(8,128)(2,1)} %bitcast.121), channel_id=1, source_target_pairs={{0,2},{1,3},{2,0},{3,1},{4,6},{5,7},{6,4},{7,5},{8,10},{9,11},{10,... | collective-permute-start | bytes 835592 | tf_op jit(solution)/shard_map/ppermute | solution.py:60
  70.5 32.8 %collective-permute-start.12 = (bf16[272,1088]{1,0:T(8,128)(2,1)}, bf16[272,1088]{1,0:T(8,128)(2,1)}, u32[]{:S(2)}, u32[]{:S(2)}) collective-permute-start(bf16[272,1088]{1,0:T(8,128)(2,1)} %get-tuple-element.96), channel_id=1, source_target_pairs={{0,2},{1,3},{2,0},{3,1},{4,7},{5,6},{6,5},{7,4},{8,10},{9,11},{10,... | collective-permute-start | bytes 1775624 | tf_op jit(solution)/shard_map/ppermute | solution.py:474
  73.2 18.8 %collective-permute-start.8 = (bf16[128,1088]{0,1:T(8,128)(2,1)S(1)}, bf16[128,1088]{0,1:T(8,128)(2,1)}, u32[]{:S(2)}, u32[]{:S(2)}) collective-permute-start(bf16[128,1088]{0,1:T(8,128)(2,1)S(1)} %slice.337), channel_id=1, source_target_pairs={{0,2},{1,3},{2,0},{3,1},{4,6},{5,7},{6,4},{7,5},{8,10},{9,11},{10,... | collective-permute-start | bytes 835592 | tf_op jit(solution)/shard_map/ppermute | solution.py:60
  97.7 104.8 %collective-permute-start.20 = (bf16[48,1088]{1,0:T(8,128)(2,1)}, bf16[48,1088]{1,0:T(8,128)(2,1)}, u32[]{:S(2)}, u32[]{:S(2)}) collective-permute-start(bf16[48,1088]{1,0:T(8,128)(2,1)} %get-tuple-element.104), channel_id=1, source_target_pairs={{0,1},{1,2},{2,3},{4,5},{5,6},{6,7},{8,9},{9,10},{10,11},{12,13},{... | collective-permute-start | bytes 313352 | tf_op jit(solution)/shard_map/ppermute | solution.py:483
  101.1 13.5 %collective-permute-start.11 = (bf16[272,1088]{1,0:T(8,128)(2,1)}, bf16[272,1088]{1,0:T(8,128)(2,1)}, u32[]{:S(2)}, u32[]{:S(2)}) collective-permute-start(bf16[272,1088]{1,0:T(8,128)(2,1)} %get-tuple-element.97), channel_id=1, source_target_pairs={{0,1},{1,0},{2,3},{3,2},{4,5},{5,4},{6,7},{7,6},{8,9},{9,8},{10,11... | collective-permute-start | bytes 1775624 | tf_op jit(solution)/shard_map/ppermute | solution.py:60
  103.2 16.2 %collective-permute-start.13 = (bf16[272,1088]{1,0:T(8,128)(2,1)}, bf16[272,1088]{1,0:T(8,128)(2,1)}, u32[]{:S(2)}, u32[]{:S(2)}) collective-permute-start(bf16[272,1088]{1,0:T(8,128)(2,1)} %collective-permute-done.12.refs_2_), channel_id=1, source_target_pairs={{0,4},{4,0},{8,12},{12,8},{16,20},{20,16},{24,28},{28,24},{1,5},{5... | collective-permute-start | bytes 1775624 | tf_op jit(solution)/shard_map/ppermute | solution.py:60
  106.9 16.3 %collective-permute-start.10 = (bf16[256,1088]{0,1:T(8,128)(2,1)}, bf16[256,1088]{0,1:T(8,128)(2,1)}, u32[]{:S(2)}, u32[]{:S(2)}) collective-permute-start(bf16[256,1088]{0,1:T(8,128)(2,1)} %pad_maximum_fusion.6), channel_id=1, source_target_pairs={{0,1},{1,0},{2,3},{3,2},{4,5},{5,4},{6,7},{7,6},{8,9},{9,8},{10,11... | collective-permute-start | bytes 1671176 | tf_op jit(solution)/shard_map/ppermute | solution.py:60
  110.0 92.7 %collective-permute-start.21 = (bf16[48,1088]{1,0:T(8,128)(2,1)S(1)}, bf16[48,1088]{1,0:T(8,128)(2,1)}, u32[]{:S(2)}, u32[]{:S(2)}) collective-permute-start(bf16[48,1088]{1,0:T(8,128)(2,1)S(1)} %get-tuple-element.103), channel_id=1, source_target_pairs={{1,0},{2,1},{3,2},{5,4},{6,5},{7,6},{9,8},{10,9},{11,10},{13,12},{... | collective-permute-start | bytes 313352 | tf_op jit(solution)/shard_map/ppermute | solution.py:484
  114.6 14.2 %collective-permute-start.17 = (bf16[256,1088]{0,1:T(8,128)(2,1)}, bf16[256,1088]{0,1:T(8,128)(2,1)}, u32[]{:S(2)}, u32[]{:S(2)}) collective-permute-start(bf16[256,1088]{0,1:T(8,128)(2,1)} %pad_maximum_fusion.7), channel_id=1, source_target_pairs={{0,1},{1,0},{2,3},{3,2},{4,5},{5,4},{6,7},{7,6},{8,9},{9,8},{10,11... | collective-permute-start | bytes 1671176 | tf_op jit(solution)/shard_map/ppermute | solution.py:60
  136.2 13.7 %collective-permute-start.18 = (bf16[256,1088]{0,1:T(8,128)(2,1)}, bf16[256,1088]{0,1:T(8,128)(2,1)}, u32[]{:S(2)}, u32[]{:S(2)}) collective-permute-start(bf16[256,1088]{0,1:T(8,128)(2,1)} %slice.331), channel_id=1, source_target_pairs={{0,1},{1,0},{2,3},{3,2},{4,5},{5,4},{6,7},{7,6},{8,9},{9,8},{10,11... | collective-permute-start | bytes 1671176 | tf_op jit(solution)/shard_map/ppermute | solution.py:60
  138.0 23.2 %collective-permute-start.14 = (bf16[256,1088]{0,1:T(8,128)(2,1)}, bf16[256,1088]{0,1:T(8,128)(2,1)}, u32[]{:S(2)}, u32[]{:S(2)}) collective-permute-start(bf16[256,1088]{0,1:T(8,128)(2,1)} %slice.332), channel_id=1, source_target_pairs={{0,1},{1,0},{2,3},{3,2},{4,5},{5,4},{6,7},{7,6},{8,9},{9,8},{10,11... | collective-permute-start | bytes 1671176 | tf_op jit(solution)/shard_map/ppermute | solution.py:60
  144.3 28.9 %collective-permute-start.35 = (bf16[1,544,1088]{2,1,0:T(8,128)(2,1)}, bf16[1,544,1088]{2,1,0:T(8,128)(2,1)}, u32[]{:S(2)}, u32[]{:S(2)}) collective-permute-start(bf16[1,544,1088]{2,1,0:T(8,128)(2,1)} %dynamic-slice_convert_fusion.1), channel_id=1, source_target_pairs={{0,4},{4,0},{8,12},{12,8},{16,20},{20,16},{24,28},{28,24},{1,5},{5... | collective-permute-start | bytes 3551240 | tf_op jit(solution)/shard_map/ppermute | solution.py:60
  159.0 41.0 %collective-permute-start.39 = (bf16[2,2,1,136,1088]{4,3,2,1,0:T(8,128)(2,1)S(1)}, bf16[2,2,1,136,1088]{4,3,2,1,0:T(8,128)(2,1)S(1)}, u32[]{:S(2)}, u32[]{:S(2)}) collective-permute-start(bf16[2,2,1,136,1088]{4,3,2,1,0:T(8,128)(2,1)S(1)} %dynamic-slice_convert_fusion), channel_id=1, source_target_pairs={{0,4},{4,0},{8,12},{12,8},{16,20},{20,16},{24,28},{28,24},{1,5},{5... | collective-permute-start | bytes 3551240 | tf_op jit(solution)/shard_map/ppermute | solution.py:60
  167.8 115.5 %collective-permute-start.15 = (bf16[128,1088]{0,1:T(8,128)(2,1)}, bf16[128,1088]{0,1:T(8,128)(2,1)}, u32[]{:S(2)}, u32[]{:S(2)}) collective-permute-start(bf16[128,1088]{0,1:T(8,128)(2,1)} %slice.336), channel_id=1, source_target_pairs={{0,2},{1,3},{2,0},{3,1},{4,6},{5,7},{6,4},{7,5},{8,10},{9,11},{10,... | collective-permute-start | bytes 835592 | tf_op jit(solution)/shard_map/ppermute | solution.py:60
  173.3 29.4 %collective-permute-start.23 = (bf16[256,1088]{0,1:T(8,128)(2,1)S(1)}, bf16[256,1088]{0,1:T(8,128)(2,1)S(1)}, u32[]{:S(2)}, u32[]{:S(2)}) collective-permute-start(bf16[256,1088]{0,1:T(8,128)(2,1)S(1)} %pad_maximum_fusion.8), channel_id=1, source_target_pairs={{0,1},{1,0},{2,3},{3,2},{4,5},{5,4},{6,7},{7,6},{8,9},{9,8},{10,11... | collective-permute-start | bytes 1671176 | tf_op jit(solution)/shard_map/ppermute | solution.py:60
  200.0 29.4 %collective-permute-start.36 = (bf16[1,544,544]{2,1,0:T(8,128)(2,1)}, bf16[1,544,544]{2,1,0:T(8,128)(2,1)}, u32[]{:S(2)}, u32[]{:S(2)}) collective-permute-start(bf16[1,544,544]{2,1,0:T(8,128)(2,1)} %broadcast_select_fusion.1), channel_id=1, source_target_pairs={{0,8},{4,12},{8,0},{12,4},{16,24},{20,28},{24,16},{28,20},{1,9},{5... | collective-permute-start | bytes 1775624 | tf_op jit(solution)/shard_map/ppermute | solution.py:60
  202.5 29.4 %collective-permute-start.40 = (bf16[2,1,1,136,1088]{4,3,2,1,0:T(8,128)(2,1)}, bf16[2,1,1,136,1088]{4,3,2,1,0:T(8,128)(2,1)}, u32[]{:S(2)}, u32[]{:S(2)}) collective-permute-start(bf16[2,1,1,136,1088]{4,3,2,1,0:T(8,128)(2,1)} %constant_dynamic-slice_fusion.1), channel_id=1, source_target_pairs={{0,8},{4,12},{8,0},{12,4},{16,24},{20,28},{24,16},{28,20},{1,9},{5... | collective-permute-start | bytes 1775624 | tf_op jit(solution)/shard_map/ppermute | solution.py:60
  218.7 41.5 %collective-permute-start.24 = (bf16[256,1088]{0,1:T(8,128)(2,1)}, bf16[256,1088]{0,1:T(8,128)(2,1)}, u32[]{:S(2)}, u32[]{:S(2)}) collective-permute-start(bf16[256,1088]{0,1:T(8,128)(2,1)} %slice.330), channel_id=1, source_target_pairs={{0,1},{1,0},{2,3},{3,2},{4,5},{5,4},{6,7},{7,6},{8,9},{9,8},{10,11... | collective-permute-start | bytes 1671176 | tf_op jit(solution)/shard_map/ppermute | solution.py:60
  224.2 71.4 %collective-permute-start.26 = (bf16[3,1,136,1088]{3,2,1,0:T(8,128)(2,1)}, bf16[3,1,136,1088]{3,2,1,0:T(8,128)(2,1)}, u32[]{:S(2)}, u32[]{:S(2)}) collective-permute-start(bf16[3,1,136,1088]{3,2,1,0:T(8,128)(2,1)} %dynamic-slice_convert_fusion.2), channel_id=1, source_target_pairs={{0,4},{4,0},{8,12},{12,8},{16,20},{20,16},{24,28},{28,24},{1,5},{5... | collective-permute-start | bytes 2663432 | tf_op jit(solution)/shard_map/ppermute | solution.py:60
  229.4 25.9 %collective-permute-start.32 = (bf16[2,2,1,136,272]{4,3,2,1,0:T(8,128)(2,1)S(1)}, bf16[2,2,1,136,272]{4,3,2,1,0:T(8,128)(2,1)S(1)}, u32[]{:S(2)}, u32[]{:S(2)}) collective-permute-start(bf16[2,2,1,136,272]{4,3,2,1,0:T(8,128)(2,1)S(1)} %dynamic-slice_convert_fusion.3), channel_id=1, source_target_pairs={{0,4},{4,0},{8,12},{12,8},{16,20},{20,16},{24,28},{28,24},{1,5},{5... | collective-permute-start | bytes 887816 | tf_op jit(solution)/shard_map/ppermute | solution.py:60
  232.0 25.8 %collective-permute-start.37 = (bf16[1,544,272]{2,1,0:T(8,128)(2,1)S(1)}, bf16[1,544,272]{2,1,0:T(8,128)(2,1)S(1)}, u32[]{:S(2)}, u32[]{:S(2)}) collective-permute-start(bf16[1,544,272]{2,1,0:T(8,128)(2,1)S(1)} %broadcast_select_fusion.3), channel_id=1, source_target_pairs={{0,16},{4,20},{8,24},{12,28},{16,0},{20,4},{24,8},{28,12},{1,17},{... | collective-permute-start | bytes 887816 | tf_op jit(solution)/shard_map/ppermute | solution.py:60
  255.3 17.8 %collective-permute-start.41 = (bf16[1,1,1,136,1088]{4,3,2,1,0:T(8,128)(2,1)S(1)}, bf16[1,1,1,136,1088]{4,3,2,1,0:T(8,128)(2,1)S(1)}, u32[]{:S(2)}, u32[]{:S(2)}) collective-permute-start(bf16[1,1,1,136,1088]{4,3,2,1,0:T(8,128)(2,1)S(1)} %constant_dynamic-slice_fusion), channel_id=1, source_target_pairs={{0,16},{4,20},{8,24},{12,28},{16,0},{20,4},{24,8},{28,12},{1,17},{... | collective-permute-start | bytes 887816 | tf_op jit(solution)/shard_map/ppermute | solution.py:60
  257.8 16.2 %collective-permute-start.33 = (bf16[2,1,1,136,272]{4,3,2,1,0:T(8,128)(2,1)S(1)}, bf16[2,1,1,136,272]{4,3,2,1,0:T(8,128)(2,1)S(1)}, u32[]{:S(2)}, u32[]{:S(2)}) collective-permute-start(bf16[2,1,1,136,272]{4,3,2,1,0:T(8,128)(2,1)S(1)} %constant_dynamic-slice_fusion.3), channel_id=1, source_target_pairs={{0,8},{4,12},{8,0},{12,4},{16,24},{20,28},{24,16},{28,20},{1,9},{5... | collective-permute-start | bytes 443912 | tf_op jit(solution)/shard_map/ppermute | solution.py:60
  260.2 46.2 %collective-permute-start.38 = (bf16[544,272]{1,0:T(8,128)(2,1)}, bf16[544,272]{1,0:T(8,128)(2,1)}, u32[]{:S(2)}, u32[]{:S(2)}) collective-permute-start(bf16[544,272]{1,0:T(8,128)(2,1)} %fusion.36), channel_id=1, source_target_pairs={{0,0},{1,8},{2,16},{3,24},{4,4},{5,12},{6,20},{7,28},{8,2},{9,10},... | collective-permute-start | bytes 887816 | tf_op jit(solution)/shard_map/ppermute | solution.py:616
  297.8 18.6 %collective-permute-start.27 = (bf16[3,1,136,544]{3,2,1,0:T(8,128)(2,1)S(1)}, bf16[3,1,136,544]{3,2,1,0:T(8,128)(2,1)S(1)}, u32[]{:S(2)}, u32[]{:S(2)}) collective-permute-start(bf16[3,1,136,544]{3,2,1,0:T(8,128)(2,1)S(1)} %broadcast_select_fusion.2), channel_id=1, source_target_pairs={{0,8},{4,12},{8,0},{12,4},{16,24},{20,28},{24,16},{28,20},{1,9},{5... | collective-permute-start | bytes 1331720 | tf_op jit(solution)/shard_map/ppermute | solution.py:60
  317.0 17.7 %collective-permute-start.28 = (bf16[3,1,136,272]{3,2,1,0:T(8,128)(2,1)S(1)}, bf16[3,1,136,272]{3,2,1,0:T(8,128)(2,1)S(1)}, u32[]{:S(2)}, u32[]{:S(2)}) collective-permute-start(bf16[3,1,136,272]{3,2,1,0:T(8,128)(2,1)S(1)} %broadcast_select_fusion.4), channel_id=1, source_target_pairs={{0,16},{4,20},{8,24},{12,28},{16,0},{20,4},{24,8},{28,12},{1,17},{... | collective-permute-start | bytes 665864 | tf_op jit(solution)/shard_map/ppermute | solution.py:60
  336.9 12.0 %collective-permute-start.31 = (bf16[136,272]{1,0:T(8,128)(2,1)S(1)}, bf16[136,272]{1,0:T(8,128)(2,1)S(1)}, u32[]{:S(2)}, u32[]{:S(2)}) collective-permute-start(bf16[136,272]{1,0:T(8,128)(2,1)S(1)} %get-tuple-element.111), channel_id=1, source_target_pairs={{0,0},{1,12},{2,24},{3,8},{4,20},{5,4},{6,16},{7,28},{8,2},{9,14},... | collective-permute-start | bytes 221960 | tf_op jit(solution)/shard_map/ppermute | solution.py:609
  340.0 12.2 %collective-permute-start.29 = (bf16[136,272]{1,0:T(8,128)(2,1)S(1)}, bf16[136,272]{1,0:T(8,128)(2,1)S(1)}, u32[]{:S(2)}, u32[]{:S(2)}) collective-permute-start(bf16[136,272]{1,0:T(8,128)(2,1)S(1)} %get-tuple-element.110), channel_id=1, source_target_pairs={{0,20},{1,24},{2,4},{3,16},{4,0},{5,12},{6,28},{7,8},{8,22},{9,26}... | collective-permute-start | bytes 221960 | tf_op jit(solution)/shard_map/ppermute | solution.py:609
  (88 other events, 1260.6 us)

commit v4 on v3

--- a/solution.py
+++ b/solution.py
@@ -274,14 +274,22 @@
 
 def mask_bias(bias_ref, bounds_ref, rank_ref, blocks):
     order = relative_order(blocks)
+    seq = bias_ref.shape[1]
     tokens = bias_ref.shape[0] // blocks
+    chunk = 32
+    begin = jnp.broadcast_to(bounds_ref[0:1, :], (chunk, seq))
+    end = jnp.broadcast_to(bounds_ref[1:2, :], (chunk, seq))
+    row = lax.broadcasted_iota(jnp.int32, (chunk, seq), 0)
     for block in range(blocks):
-        for part in range(bias_ref.shape[1] // 128):
-            lanes = slice(128 * part, 128 * (part + 1))
-            shape = (tokens, 128)
-            key_pos = (rank_ref[0] ^ order[block]) * tokens + lax.broadcasted_iota(jnp.int32, shape, 0)
-            inside = (key_pos >= bounds_ref[0:1, lanes]) & (key_pos <= bounds_ref[1:2, lanes])
-            bias_ref[pl.ds(block * tokens, tokens), lanes] = jnp.where(inside, 0.0, masked_score)
+
+        def fill(i, carry):
+            key_pos = (rank_ref[0] ^ order[block]) * tokens + i * chunk + row
+            inside = (key_pos >= begin) & (key_pos <= end)
+            place = pl.multiple_of(block * tokens + i * chunk, chunk)
+            bias_ref[pl.ds(place, chunk), :] = jnp.where(inside, 0.0, masked_score)
+            return carry
+
+        lax.fori_loop(0, tokens // chunk, fill, 0)
 
 
 def attend_kernel(blocks, rank_ref, bounds_ref, query_ref, key_ref, value_ref, mixed_ref, total_ref, bias_ref):
@@ -613,7 +621,8 @@
         row_part, lane_part = piece_of(r, reps, size)
         for g in range(size):
             route.append((r * size + g, (g * share + row_part) * size + lane_part))
-    final_up = lax.ppermute(add_parts(up_parts, bf16).reshape(hidden_own // share, own), (REP, GRP), route).astype(f32).T
+    up_piece = add_parts(up_parts, bf16).reshape(hidden_own // share, own).T
+    final_up = lax.ppermute(up_piece, (REP, GRP), route).astype(f32)
 
     received = jnp.stack(received)
     owner = jnp.array(origin, jnp.int32)[rep_rank]

time: 357 us -> 343 us (0.961)
  starting transfers between devices: 64.3 us -> 57 us
  waiting for transfers between devices: 142 us -> 138 us
    ppermute x40, starting transfers between devices: 47.4 us -> 39.6 us  [swap(): return lax.ppermute(value, axis, [(i, i ^ bit) for i in range(size)])]
    ppermute x40, waiting for transfers between devices: 134 us -> 129 us  [swap(): return lax.ppermute(value, axis, [(i, i ^ bit) for i in range(size)])]
  transfers between devices with their start and end apart: 47 -> 47, of which waited for: 21 -> 20; matrix products, arithmetic and copies ran while one was open for 28% -> 29% of each run, Pallas kernels for 4% -> 5%
where the time goes in v4:
time: 343 us; the launch traced here: 341 us
  waiting for transfers between devices  138 us (40%)
  starting transfers between devices  57 us (17%)
  local copies, waits for them, and re-layouts  47.9 us (14%)
  other arithmetic  36.2 us (11%)
  matrix products  32.4 us (9%)
  Pallas kernels  28.1 us (8%)
    ppermute x40, waiting for transfers between devices, swap(): return lax.ppermute(value, axis, [(i, i ^ bit) for i in range(size)])  129 us
    ppermute x40, starting transfers between devices, swap(): return lax.ppermute(value, axis, [(i, i ^ bit) for i in range(size)])  39.6 us
    dot_general x12, matrix products, contract(): lax.dot_general(left, right, (((left_dim,), (right_dim,)), ((), ())), pre...  32.4 us
    pallas_call x1, Pallas kernels, attend(): pl.pallas_call(lambda *refs: attend_kernel(blocks, *refs), grid_spec=pltp...  9.45 us
    ppermute x3, waiting for transfers between devices, shards(): received.append(lax.ppermute(sent, (REP, GRP), route))  9.18 us
    pallas_call x1, Pallas kernels, attend_back(): pl.pallas_call(lambda *refs: attend_back_kernel(blocks, *refs), grid_spec...  9.1 us
    convert_element_type x9, other arithmetic, add_parts(): return total.astype(dtype)  7.45 us
    dynamic_slice x15, local copies, waits for them, and re-layouts, cut(): return lax.dynamic_slice(value, starts, sizes, allow_negative_indices=False)  7.3 us
  transfers between devices with their start and end apart: 47, of which 20 were waited for; matrix products, arithmetic and copies ran while one was open for 29% of the time, Pallas kernels for 5%

profile of v4, /device:TPU:1, one launch (start us, length us, event | category | flops | bytes accessed | tf_op | source)
XLA Modules:
  0.0 341.2 jit_solution(6331276647052411769)
XLA Ops:
  0.7 3.2 pack.1
  3.9 2.7 collective-permute-start.1
  15.1 3.9 %slice_bitcast_fusion.3 = (bf16[1,272,1088]{2,1,0:T(8,128)(2,1)}, bf16[1,272,1088]{2,1,0:T(8,128)(2,1)}, bf16[1,272,1088]{2,1,0:T(8,128)(2,1)}, bf16[1,272,1088]{2,1,0:T(8,128)(2,1)}) fusion(bf16[272,4352]{1,0:T(8,128)(2,1)} %param.23), kind=kLoop, calls=%fused_computation.75 | loop fusion | bytes 4734976 | tf_op jit(solution)/shard_map/stack | solution.py:477
  20.1 11.8 %collective-permute-done.5 = bf16[8,272]{1,0:T(8,128)(2,1)} collective-permute-done((bf16[8,272]{1,0:T(8,128)(2,1)S(1)}, bf16[8,272]{1,0:T(8,128)(2,1)}, u32[]{:S(2)}, u32[]{:S(2)}) %collective-permute-start.5) | collective-permute-done | bytes 4384 | tf_op jit(solution)/shard_map/ppermute | solution.py:60
  31.9 2.7 concatenate.64
  46.8 3.1 shard_map.289
  53.5 3.7 %add_convert_fusion.2.refs_2_.refs_3_.refs_4_ = bf16[960,512]{1,0:T(8,128)(2,1)} fusion(bf16[1088,960]{1,0:T(8,128)(2,1)S(1)} %copy-done.22, f32[960]{0:T(1024)S(1)} %copy-done.52, f32[1088]{0:T(1024)S(1)} %copy-done.47, f32[1088]{0:T(1024)S(1)} %mul.196, f32[512]{0:T(512)S(1)} %add_rsqrt_fusion, f32[512]{0:T(512)S(1)} %broadcast_multiply_fusion, ...), kind=kOutput, calls=%fused_computation.25 | convolution fusion | flops 1076658176 | bytes 4202752 | tf_op jit(solution)/shard_map/dot_general | solution.py:54
  57.2 9.4 %attend.1 = (bf16[320,512]{1,0:T(8,128)(2,1)}, f32[5,1,512]{2,1,0:T(1,128)}) custom-call(s32[1]{0:T(128)} %bitcast.1.refs_0_.rank_ref, s32[8,512]{1,0:T(8,128)} %add_add_fusion.refs_1_, bf16[960,512]{1,0:T(8,128)(2,1)} %add_convert_fusion.2.refs_2_.refs_3_.refs_4_, bf16[960,512]{1,0:T(8,128)(2,1)} %add_convert_fusion.2.refs_2_.refs_3_.refs_4_, ...), custom_call_target="tpu_custom_call" | custom-call | flops 335544320 | bytes 1310720 | tf_op jit(solution)/shard_map/attend/pallas_call | solution.py:356
  73.9 18.2 %collective-permute-done.8 = bf16[128,1088]{0,1:T(8,128)(2,1)} collective-permute-done((bf16[128,1088]{0,1:T(8,128)(2,1)S(1)}, bf16[128,1088]{0,1:T(8,128)(2,1)}, u32[]{:S(2)}, u32[]{:S(2)}) %collective-permute-start.8) | collective-permute-done | bytes 278560 | tf_op jit(solution)/shard_map/ppermute | solution.py:60
  97.8 3.4 collective-permute-start.20
  110.1 2.7 collective-permute-start.21
  114.7 4.8 %collective-permute-done.13.refs_3_ = bf16[272,1088]{1,0:T(8,128)(2,1)} collective-permute-done((bf16[272,1088]{1,0:T(8,128)(2,1)}, bf16[272,1088]{1,0:T(8,128)(2,1)}, u32[]{:S(2)}, u32[]{:S(2)}) %collective-permute-start.13) | collective-permute-done | bytes 591904 | tf_op jit(solution)/shard_map/ppermute | solution.py:60
  119.5 3.3 shard_map.290
  123.3 3.7 %convolution_add_fusion = f32[512,1088]{0,1:T(8,128)S(1)} fusion(bf16[1088,1088]{1,0:T(8,128)(2,1)} %shard_map.290, f32[1088]{0:T(1024)S(1)} %convert_element_type.205, bf16[256,1088]{0,1:T(8,128)(2,1)} %collective-permute-done.10, bf16[128,1088]{0,1:T(8,128)(2,1)} %collective-permute-done.9, bf16[128,1088]{0,1:T(8,128)(2,1)} %add_convert_fusion.10), kind=kOutput, calls=%fused_computation.1 | convolution fusion | flops 1216053248 | bytes 5714176 | tf_op jit(solution)/shard_map/dot_general | solution.py:54
  128.9 4.8 %convert_reduce_fusion.1 = (f32[1088]{0:T(1024)S(1)}, bf16[512,1088]{0,1:T(8,128)(2,1)S(1)}) fusion(f32[512,1088]{0,1:T(8,128)S(1)} %convolution_add_fusion, bf16[1088,1088]{1,0:T(8,128)(2,1)S(1)} %copy-done, bf16[256,1088]{0,1:T(8,128)(2,1)} %collective-permute-done.17, bf16[128,1088]{0,1:T(8,128)(2,1)} %collective-permute-done.16, ...), kind=kOutput, calls=%fused_computation.23 | convolution fusion | flops 1227193344 | bytes 6828288 | tf_op jit(solution)/shard_map/dot_general | solution.py:54
  138.1 2.9 fusion.35
  146.2 3.8 %fusion.34 = f32[1088,1088]{1,0:T(8,128)S(1)} fusion(bf16[256,1088]{0,1:T(8,128)(2,1)} %collective-permute-done.17, bf16[128,1088]{0,1:T(8,128)(2,1)} %collective-permute-done.16, bf16[128,1088]{0,1:T(8,128)(2,1)S(1)} %bitcast.136, f32[512,1088]{0,1:T(8,128)} %copy-done.60), kind=kOutput, calls=%fused_computation.112 | convolution fusion | flops 1220509696 | bytes 8077312 | tf_op jit(solution)/shard_map/dot_general | solution.py:54
  153.0 6.0 %collective-permute-done.19 = bf16[128,1088]{0,1:T(8,128)(2,1)S(1)} collective-permute-done((bf16[128,1088]{0,1:T(8,128)(2,1)S(1)}, bf16[128,1088]{0,1:T(8,128)(2,1)S(1)}, u32[]{:S(2)}, u32[]{:S(2)}) %collective-permute-start.19) | collective-permute-done | bytes 278560 | tf_op jit(solution)/shard_map/ppermute | solution.py:60
  163.7 3.1 collective-permute-done.22
  168.2 5.2 %collective-permute-done.35 = bf16[1,544,1088]{2,1,0:T(8,128)(2,1)} collective-permute-done((bf16[1,544,1088]{2,1,0:T(8,128)(2,1)}, bf16[1,544,1088]{2,1,0:T(8,128)(2,1)}, u32[]{:S(2)}, u32[]{:S(2)}) %collective-permute-start.35) | collective-permute-done | bytes 1183776 | tf_op jit(solution)/shard_map/ppermute | solution.py:60
  178.4 21.7 %collective-permute-done.39 = bf16[2,2,1,136,1088]{4,3,2,1,0:T(8,128)(2,1)S(1)} collective-permute-done((bf16[2,2,1,136,1088]{4,3,2,1,0:T(8,128)(2,1)S(1)}, bf16[2,2,1,136,1088]{4,3,2,1,0:T(8,128)(2,1)S(1)}, u32[]{:S(2)}, u32[]{:S(2)}) %collective-permute-start.39) | collective-permute-done | bytes 1183776 | tf_op jit(solution)/shard_map/ppermute | solution.py:60
  205.3 9.1 %back.1 = bf16[3,320,512]{2,1,0:T(8,128)(2,1)} custom-call(s32[1]{0:T(128)} %bitcast.1.refs_0_.rank_ref, s32[8,512]{1,0:T(8,128)} %add_add_fusion.refs_1_, bf16[960,512]{1,0:T(8,128)(2,1)} %add_convert_fusion.2.refs_2_.refs_3_.refs_4_, bf16[960,512]{1,0:T(8,128)(2,1)} %add_convert_fusion.2.refs_2_.refs_3_.refs_4_, ...), custom_call_target="tpu_custom_call" | custom-call | flops 838860800 | bytes 2621440 | tf_op jit(solution)/shard_map/back/pallas_call | solution.py:381
  236.1 19.4 %collective-permute-done.32 = bf16[2,2,1,136,272]{4,3,2,1,0:T(8,128)(2,1)S(1)} collective-permute-done((bf16[2,2,1,136,272]{4,3,2,1,0:T(8,128)(2,1)S(1)}, bf16[2,2,1,136,272]{4,3,2,1,0:T(8,128)(2,1)S(1)}, u32[]{:S(2)}, u32[]{:S(2)}) %collective-permute-start.32) | collective-permute-done | bytes 295968 | tf_op jit(solution)/shard_map/ppermute | solution.py:60
  263.2 4.8 %collective-permute-done.33 = bf16[2,1,1,136,272]{4,3,2,1,0:T(8,128)(2,1)S(1)} collective-permute-done((bf16[2,1,1,136,272]{4,3,2,1,0:T(8,128)(2,1)S(1)}, bf16[2,1,1,136,272]{4,3,2,1,0:T(8,128)(2,1)S(1)}, u32[]{:S(2)}, u32[]{:S(2)}) %collective-permute-start.33) | collective-permute-done | bytes 148000 | tf_op jit(solution)/shard_map/ppermute | solution.py:60
  268.0 6.2 %collective-permute-start.38 = (bf16[272,544]{0,1:T(8,128)(2,1)}, bf16[272,544]{0,1:T(8,128)(2,1)}, u32[]{:S(2)}, u32[]{:S(2)}) collective-permute-start(bf16[272,544]{0,1:T(8,128)(2,1)} %fusion.36), channel_id=1, source_target_pairs={{0,0},{1,8},{2,16},{3,24},{4,4},{5,12},{6,20},{7,28},{8,2},{9,10},... | collective-permute-start | bytes 887816 | tf_op jit(solution)/shard_map/ppermute | solution.py:625
  274.9 2.5 fusion.26
  289.6 6.4 %collective-permute-done.34 = bf16[1,1,1,136,272]{4,3,2,1,0:T(8,128)(2,1)S(1)} collective-permute-done((bf16[1,1,1,136,272]{4,3,2,1,0:T(8,128)(2,1)S(1)}, bf16[1,1,1,136,272]{4,3,2,1,0:T(8,128)(2,1)S(1)}, u32[]{:S(2)}, u32[]{:S(2)}) %collective-permute-start.34) | collective-permute-done | bytes 74016 | tf_op jit(solution)/shard_map/ppermute | solution.py:60
  298.7 4.5 %collective-permute-done.45 = f32[102,128]{1,0:T(8,128)S(1)} collective-permute-done((f32[102,128]{1,0:T(8,128)S(1)}, f32[102,128]{1,0:T(8,128)S(1)}, u32[]{:S(2)}, u32[]{:S(2)}) %collective-permute-start.45) | collective-permute-done | bytes 52256 | tf_op jit(solution)/shard_map/ppermute | solution.py:60
  306.3 8.5 %collective-permute-done.46 = f32[102,128]{1,0:T(8,128)S(1)} collective-permute-done((f32[102,128]{1,0:T(8,128)S(1)}, f32[102,128]{1,0:T(8,128)S(1)}, u32[]{:S(2)}, u32[]{:S(2)}) %collective-permute-start.46) | collective-permute-done | bytes 52256 | tf_op jit(solution)/shard_map/ppermute | solution.py:60
  314.8 6.7 %collective-permute-done.28 = bf16[3,1,136,272]{3,2,1,0:T(8,128)(2,1)S(1)} collective-permute-done((bf16[3,1,136,272]{3,2,1,0:T(8,128)(2,1)S(1)}, bf16[3,1,136,272]{3,2,1,0:T(8,128)(2,1)S(1)}, u32[]{:S(2)}, u32[]{:S(2)}) %collective-permute-start.28) | collective-permute-done | bytes 221984 | tf_op jit(solution)/shard_map/ppermute | solution.py:60
  328.7 5.9 %collective-permute-done.31 = bf16[136,272]{1,0:T(8,128)(2,1)S(1)} collective-permute-done((bf16[136,272]{1,0:T(8,128)(2,1)S(1)}, bf16[136,272]{1,0:T(8,128)(2,1)S(1)}, u32[]{:S(2)}, u32[]{:S(2)}) %collective-permute-start.31) | collective-permute-done | bytes 74016 | tf_op jit(solution)/shard_map/ppermute | solution.py:617
  334.6 3.3 collective-permute-done.29
  (344 shorter events, 138.1 us)
Async XLA Ops:
  3.9 42.9 %collective-permute-start = (bf16[272,960]{1,0:T(8,128)(2,1)}, bf16[272,960]{1,0:T(8,128)(2,1)}, u32[]{:S(2)}, u32[]{:S(2)}) collective-permute-start(bf16[272,960]{1,0:T(8,128)(2,1)} %get-tuple-element.30), channel_id=1, source_target_pairs={{0,1},{1,0},{2,3},{3,2},{4,5},{5,4},{6,7},{7,6},{8,9},{9,8},{10,11... | collective-permute-start | bytes 1566728 | tf_op jit(solution)/shard_map/ppermute | solution.py:60
  3.9 42.9 %collective-permute-start.1 = (bf16[272,960]{1,0:T(8,128)(2,1)}, bf16[272,960]{1,0:T(8,128)(2,1)}, u32[]{:S(2)}, u32[]{:S(2)}) collective-permute-start(bf16[272,960]{1,0:T(8,128)(2,1)} %get-tuple-element.31), channel_id=1, source_target_pairs={{0,2},{1,3},{2,0},{3,1},{4,6},{5,7},{6,4},{7,5},{8,10},{9,11},{10,... | collective-permute-start | bytes 1566728 | tf_op jit(solution)/shard_map/ppermute | solution.py:60
  6.6 40.2 %collective-permute-start.2 = (bf16[272,960]{1,0:T(8,128)(2,1)}, bf16[272,960]{1,0:T(8,128)(2,1)}, u32[]{:S(2)}, u32[]{:S(2)}) collective-permute-start(bf16[272,960]{1,0:T(8,128)(2,1)} %get-tuple-element.32), channel_id=1, source_target_pairs={{0,3},{1,2},{2,1},{3,0},{4,7},{5,6},{6,5},{7,4},{8,11},{9,10},{10,... | collective-permute-start | bytes 1566728 | tf_op jit(solution)/shard_map/ppermute | solution.py:60
  12.2 19.7 %collective-permute-start.5 = (bf16[8,272]{1,0:T(8,128)(2,1)S(1)}, bf16[8,272]{1,0:T(8,128)(2,1)}, u32[]{:S(2)}, u32[]{:S(2)}) collective-permute-start(bf16[8,272]{1,0:T(8,128)(2,1)S(1)} %concatenate.63), channel_id=1, source_target_pairs={{0,2},{1,3},{2,0},{3,1},{4,6},{5,7},{6,4},{7,5},{8,10},{9,11},{10,... | collective-permute-start | bytes 13064 | tf_op jit(solution)/shard_map/ppermute | solution.py:60
  13.9 24.1 %collective-permute-start.3 = (bf16[128,1088]{0,1:T(8,128)(2,1)}, bf16[128,1088]{0,1:T(8,128)(2,1)}, u32[]{:S(2)}, u32[]{:S(2)}) collective-permute-start(bf16[128,1088]{0,1:T(8,128)(2,1)} %bitcast.121), channel_id=1, source_target_pairs={{0,2},{1,3},{2,0},{3,1},{4,6},{5,7},{6,4},{7,5},{8,10},{9,11},{10,... | collective-permute-start | bytes 835592 | tf_op jit(solution)/shard_map/ppermute | solution.py:60
  70.6 32.8 %collective-permute-start.12 = (bf16[272,1088]{1,0:T(8,128)(2,1)}, bf16[272,1088]{1,0:T(8,128)(2,1)}, u32[]{:S(2)}, u32[]{:S(2)}) collective-permute-start(bf16[272,1088]{1,0:T(8,128)(2,1)} %get-tuple-element.96), channel_id=1, source_target_pairs={{0,2},{1,3},{2,0},{3,1},{4,7},{5,6},{6,5},{7,4},{8,10},{9,11},{10,... | collective-permute-start | bytes 1775624 | tf_op jit(solution)/shard_map/ppermute | solution.py:482
  73.3 18.8 %collective-permute-start.8 = (bf16[128,1088]{0,1:T(8,128)(2,1)S(1)}, bf16[128,1088]{0,1:T(8,128)(2,1)}, u32[]{:S(2)}, u32[]{:S(2)}) collective-permute-start(bf16[128,1088]{0,1:T(8,128)(2,1)S(1)} %slice.337), channel_id=1, source_target_pairs={{0,2},{1,3},{2,0},{3,1},{4,6},{5,7},{6,4},{7,5},{8,10},{9,11},{10,... | collective-permute-start | bytes 835592 | tf_op jit(solution)/shard_map/ppermute | solution.py:60
  97.8 104.8 %collective-permute-start.20 = (bf16[48,1088]{1,0:T(8,128)(2,1)}, bf16[48,1088]{1,0:T(8,128)(2,1)}, u32[]{:S(2)}, u32[]{:S(2)}) collective-permute-start(bf16[48,1088]{1,0:T(8,128)(2,1)} %get-tuple-element.104), channel_id=1, source_target_pairs={{0,1},{1,2},{2,3},{4,5},{5,6},{6,7},{8,9},{9,10},{10,11},{12,13},{... | collective-permute-start | bytes 313352 | tf_op jit(solution)/shard_map/ppermute | solution.py:491
  101.2 13.5 %collective-permute-start.11 = (bf16[272,1088]{1,0:T(8,128)(2,1)}, bf16[272,1088]{1,0:T(8,128)(2,1)}, u32[]{:S(2)}, u32[]{:S(2)}) collective-permute-start(bf16[272,1088]{1,0:T(8,128)(2,1)} %get-tuple-element.97), channel_id=1, source_target_pairs={{0,1},{1,0},{2,3},{3,2},{4,5},{5,4},{6,7},{7,6},{8,9},{9,8},{10,11... | collective-permute-start | bytes 1775624 | tf_op jit(solution)/shard_map/ppermute | solution.py:60
  103.3 16.2 %collective-permute-start.13 = (bf16[272,1088]{1,0:T(8,128)(2,1)}, bf16[272,1088]{1,0:T(8,128)(2,1)}, u32[]{:S(2)}, u32[]{:S(2)}) collective-permute-start(bf16[272,1088]{1,0:T(8,128)(2,1)} %collective-permute-done.12.refs_2_), channel_id=1, source_target_pairs={{0,4},{4,0},{8,12},{12,8},{16,20},{20,16},{24,28},{28,24},{1,5},{5... | collective-permute-start | bytes 1775624 | tf_op jit(solution)/shard_map/ppermute | solution.py:60
  107.0 16.3 %collective-permute-start.10 = (bf16[256,1088]{0,1:T(8,128)(2,1)}, bf16[256,1088]{0,1:T(8,128)(2,1)}, u32[]{:S(2)}, u32[]{:S(2)}) collective-permute-start(bf16[256,1088]{0,1:T(8,128)(2,1)} %pad_maximum_fusion.6), channel_id=1, source_target_pairs={{0,1},{1,0},{2,3},{3,2},{4,5},{5,4},{6,7},{7,6},{8,9},{9,8},{10,11... | collective-permute-start | bytes 1671176 | tf_op jit(solution)/shard_map/ppermute | solution.py:60
  110.1 92.7 %collective-permute-start.21 = (bf16[48,1088]{1,0:T(8,128)(2,1)S(1)}, bf16[48,1088]{1,0:T(8,128)(2,1)}, u32[]{:S(2)}, u32[]{:S(2)}) collective-permute-start(bf16[48,1088]{1,0:T(8,128)(2,1)S(1)} %get-tuple-element.103), channel_id=1, source_target_pairs={{1,0},{2,1},{3,2},{5,4},{6,5},{7,6},{9,8},{10,9},{11,10},{13,12},{... | collective-permute-start | bytes 313352 | tf_op jit(solution)/shard_map/ppermute | solution.py:492
  114.7 14.2 %collective-permute-start.17 = (bf16[256,1088]{0,1:T(8,128)(2,1)}, bf16[256,1088]{0,1:T(8,128)(2,1)}, u32[]{:S(2)}, u32[]{:S(2)}) collective-permute-start(bf16[256,1088]{0,1:T(8,128)(2,1)} %pad_maximum_fusion.7), channel_id=1, source_target_pairs={{0,1},{1,0},{2,3},{3,2},{4,5},{5,4},{6,7},{7,6},{8,9},{9,8},{10,11... | collective-permute-start | bytes 1671176 | tf_op jit(solution)/shard_map/ppermute | solution.py:60
  136.3 13.7 %collective-permute-start.18 = (bf16[256,1088]{0,1:T(8,128)(2,1)}, bf16[256,1088]{0,1:T(8,128)(2,1)}, u32[]{:S(2)}, u32[]{:S(2)}) collective-permute-start(bf16[256,1088]{0,1:T(8,128)(2,1)} %slice.331), channel_id=1, source_target_pairs={{0,1},{1,0},{2,3},{3,2},{4,5},{5,4},{6,7},{7,6},{8,9},{9,8},{10,11... | collective-permute-start | bytes 1671176 | tf_op jit(solution)/shard_map/ppermute | solution.py:60
  138.1 22.0 %collective-permute-start.14 = (bf16[256,1088]{0,1:T(8,128)(2,1)}, bf16[256,1088]{0,1:T(8,128)(2,1)}, u32[]{:S(2)}, u32[]{:S(2)}) collective-permute-start(bf16[256,1088]{0,1:T(8,128)(2,1)} %slice.332), channel_id=1, source_target_pairs={{0,1},{1,0},{2,3},{3,2},{4,5},{5,4},{6,7},{7,6},{8,9},{9,8},{10,11... | collective-permute-start | bytes 1671176 | tf_op jit(solution)/shard_map/ppermute | solution.py:60
  144.4 28.9 %collective-permute-start.35 = (bf16[1,544,1088]{2,1,0:T(8,128)(2,1)}, bf16[1,544,1088]{2,1,0:T(8,128)(2,1)}, u32[]{:S(2)}, u32[]{:S(2)}) collective-permute-start(bf16[1,544,1088]{2,1,0:T(8,128)(2,1)} %dynamic-slice_convert_fusion.1), channel_id=1, source_target_pairs={{0,4},{4,0},{8,12},{12,8},{16,20},{20,16},{24,28},{28,24},{1,5},{5... | collective-permute-start | bytes 3551240 | tf_op jit(solution)/shard_map/ppermute | solution.py:60
  159.0 41.1 %collective-permute-start.39 = (bf16[2,2,1,136,1088]{4,3,2,1,0:T(8,128)(2,1)S(1)}, bf16[2,2,1,136,1088]{4,3,2,1,0:T(8,128)(2,1)S(1)}, u32[]{:S(2)}, u32[]{:S(2)}) collective-permute-start(bf16[2,2,1,136,1088]{4,3,2,1,0:T(8,128)(2,1)S(1)} %dynamic-slice_convert_fusion), channel_id=1, source_target_pairs={{0,4},{4,0},{8,12},{12,8},{16,20},{20,16},{24,28},{28,24},{1,5},{5... | collective-permute-start | bytes 3551240 | tf_op jit(solution)/shard_map/ppermute | solution.py:60
  166.8 108.1 %collective-permute-start.15 = (bf16[128,1088]{0,1:T(8,128)(2,1)}, bf16[128,1088]{0,1:T(8,128)(2,1)}, u32[]{:S(2)}, u32[]{:S(2)}) collective-permute-start(bf16[128,1088]{0,1:T(8,128)(2,1)} %slice.336), channel_id=1, source_target_pairs={{0,2},{1,3},{2,0},{3,1},{4,6},{5,7},{6,4},{7,5},{8,10},{9,11},{10,... | collective-permute-start | bytes 835592 | tf_op jit(solution)/shard_map/ppermute | solution.py:60
  173.4 29.4 %collective-permute-start.23 = (bf16[256,1088]{0,1:T(8,128)(2,1)S(1)}, bf16[256,1088]{0,1:T(8,128)(2,1)S(1)}, u32[]{:S(2)}, u32[]{:S(2)}) collective-permute-start(bf16[256,1088]{0,1:T(8,128)(2,1)S(1)} %pad_maximum_fusion.8), channel_id=1, source_target_pairs={{0,1},{1,0},{2,3},{3,2},{4,5},{5,4},{6,7},{7,6},{8,9},{9,8},{10,11... | collective-permute-start | bytes 1671176 | tf_op jit(solution)/shard_map/ppermute | solution.py:60
  200.1 29.0 %collective-permute-start.36 = (bf16[1,544,544]{2,1,0:T(8,128)(2,1)}, bf16[1,544,544]{2,1,0:T(8,128)(2,1)}, u32[]{:S(2)}, u32[]{:S(2)}) collective-permute-start(bf16[1,544,544]{2,1,0:T(8,128)(2,1)} %broadcast_select_fusion.1), channel_id=1, source_target_pairs={{0,8},{4,12},{8,0},{12,4},{16,24},{20,28},{24,16},{28,20},{1,9},{5... | collective-permute-start | bytes 1775624 | tf_op jit(solution)/shard_map/ppermute | solution.py:60
  202.6 29.0 %collective-permute-start.40 = (bf16[2,1,1,136,1088]{4,3,2,1,0:T(8,128)(2,1)}, bf16[2,1,1,136,1088]{4,3,2,1,0:T(8,128)(2,1)}, u32[]{:S(2)}, u32[]{:S(2)}) collective-permute-start(bf16[2,1,1,136,1088]{4,3,2,1,0:T(8,128)(2,1)} %constant_dynamic-slice_fusion.1), channel_id=1, source_target_pairs={{0,8},{4,12},{8,0},{12,4},{16,24},{20,28},{24,16},{28,20},{1,9},{5... | collective-permute-start | bytes 1775624 | tf_op jit(solution)/shard_map/ppermute | solution.py:60
  218.9 39.1 %collective-permute-start.24 = (bf16[256,1088]{0,1:T(8,128)(2,1)}, bf16[256,1088]{0,1:T(8,128)(2,1)}, u32[]{:S(2)}, u32[]{:S(2)}) collective-permute-start(bf16[256,1088]{0,1:T(8,128)(2,1)} %slice.330), channel_id=1, source_target_pairs={{0,1},{1,0},{2,3},{3,2},{4,5},{5,4},{6,7},{7,6},{8,9},{9,8},{10,11... | collective-permute-start | bytes 1671176 | tf_op jit(solution)/shard_map/ppermute | solution.py:60
  224.4 55.6 %collective-permute-start.26 = (bf16[3,1,136,1088]{3,2,1,0:T(8,128)(2,1)}, bf16[3,1,136,1088]{3,2,1,0:T(8,128)(2,1)}, u32[]{:S(2)}, u32[]{:S(2)}) collective-permute-start(bf16[3,1,136,1088]{3,2,1,0:T(8,128)(2,1)} %dynamic-slice_convert_fusion.2), channel_id=1, source_target_pairs={{0,4},{4,0},{8,12},{12,8},{16,20},{20,16},{24,28},{28,24},{1,5},{5... | collective-permute-start | bytes 2663432 | tf_op jit(solution)/shard_map/ppermute | solution.py:60
  229.1 26.4 %collective-permute-start.32 = (bf16[2,2,1,136,272]{4,3,2,1,0:T(8,128)(2,1)S(1)}, bf16[2,2,1,136,272]{4,3,2,1,0:T(8,128)(2,1)S(1)}, u32[]{:S(2)}, u32[]{:S(2)}) collective-permute-start(bf16[2,2,1,136,272]{4,3,2,1,0:T(8,128)(2,1)S(1)} %dynamic-slice_convert_fusion.3), channel_id=1, source_target_pairs={{0,4},{4,0},{8,12},{12,8},{16,20},{20,16},{24,28},{28,24},{1,5},{5... | collective-permute-start | bytes 887816 | tf_op jit(solution)/shard_map/ppermute | solution.py:60
  231.6 29.1 %collective-permute-start.37 = (bf16[1,544,272]{2,1,0:T(8,128)(2,1)S(1)}, bf16[1,544,272]{2,1,0:T(8,128)(2,1)S(1)}, u32[]{:S(2)}, u32[]{:S(2)}) collective-permute-start(bf16[1,544,272]{2,1,0:T(8,128)(2,1)S(1)} %broadcast_select_fusion.3), channel_id=1, source_target_pairs={{0,16},{4,20},{8,24},{12,28},{16,0},{20,4},{24,8},{28,12},{1,17},{... | collective-permute-start | bytes 887816 | tf_op jit(solution)/shard_map/ppermute | solution.py:60
  255.5 31.1 %collective-permute-start.41 = (bf16[1,1,1,136,1088]{4,3,2,1,0:T(8,128)(2,1)}, bf16[1,1,1,136,1088]{4,3,2,1,0:T(8,128)(2,1)}, u32[]{:S(2)}, u32[]{:S(2)}) collective-permute-start(bf16[1,1,1,136,1088]{4,3,2,1,0:T(8,128)(2,1)} %constant_dynamic-slice_fusion), channel_id=1, source_target_pairs={{0,16},{4,20},{8,24},{12,28},{16,0},{20,4},{24,8},{28,12},{1,17},{... | collective-permute-start | bytes 887816 | tf_op jit(solution)/shard_map/ppermute | solution.py:60
  260.7 13.5 %collective-permute-start.25 = (bf16[128,1088]{0,1:T(8,128)(2,1)S(1)}, bf16[128,1088]{0,1:T(8,128)(2,1)S(1)}, u32[]{:S(2)}, u32[]{:S(2)}) collective-permute-start(bf16[128,1088]{0,1:T(8,128)(2,1)S(1)} %slice.334), channel_id=1, source_target_pairs={{0,2},{1,3},{2,0},{3,1},{4,6},{5,7},{6,4},{7,5},{8,10},{9,11},{10,... | collective-permute-start | bytes 835592 | tf_op jit(solution)/shard_map/ppermute | solution.py:60
  268.0 28.7 %collective-permute-start.38 = (bf16[272,544]{0,1:T(8,128)(2,1)}, bf16[272,544]{0,1:T(8,128)(2,1)}, u32[]{:S(2)}, u32[]{:S(2)}) collective-permute-start(bf16[272,544]{0,1:T(8,128)(2,1)} %fusion.36), channel_id=1, source_target_pairs={{0,0},{1,8},{2,16},{3,24},{4,4},{5,12},{6,20},{7,28},{8,2},{9,10},... | collective-permute-start | bytes 887816 | tf_op jit(solution)/shard_map/ppermute | solution.py:625
  278.5 17.5 %collective-permute-start.34 = (bf16[1,1,1,136,272]{4,3,2,1,0:T(8,128)(2,1)S(1)}, bf16[1,1,1,136,272]{4,3,2,1,0:T(8,128)(2,1)S(1)}, u32[]{:S(2)}, u32[]{:S(2)}) collective-permute-start(bf16[1,1,1,136,272]{4,3,2,1,0:T(8,128)(2,1)S(1)} %constant_dynamic-slice_fusion.2), channel_id=1, source_target_pairs={{0,16},{4,20},{8,24},{12,28},{16,0},{20,4},{24,8},{28,12},{1,17},{... | collective-permute-start | bytes 221960 | tf_op jit(solution)/shard_map/ppermute | solution.py:60
  282.2 21.2 %collective-permute-start.27 = (bf16[3,1,136,544]{3,2,1,0:T(8,128)(2,1)S(1)}, bf16[3,1,136,544]{3,2,1,0:T(8,128)(2,1)S(1)}, u32[]{:S(2)}, u32[]{:S(2)}) collective-permute-start(bf16[3,1,136,544]{3,2,1,0:T(8,128)(2,1)S(1)} %broadcast_select_fusion.2), channel_id=1, source_target_pairs={{0,8},{4,12},{8,0},{12,4},{16,24},{20,28},{24,16},{28,20},{1,9},{5... | collective-permute-start | bytes 1331720 | tf_op jit(solution)/shard_map/ppermute | solution.py:60
  288.5 14.8 %collective-permute-start.45 = (f32[102,128]{1,0:T(8,128)S(1)}, f32[102,128]{1,0:T(8,128)S(1)}, u32[]{:S(2)}, u32[]{:S(2)}) collective-permute-start(f32[102,128]{1,0:T(8,128)S(1)} %add.251), channel_id=1, source_target_pairs={{0,8},{4,12},{8,0},{12,4},{16,24},{20,28},{24,16},{28,20},{1,9},{5... | collective-permute-start | bytes 156680 | tf_op jit(solution)/shard_map/ppermute | solution.py:60
  303.9 17.6 %collective-permute-start.28 = (bf16[3,1,136,272]{3,2,1,0:T(8,128)(2,1)S(1)}, bf16[3,1,136,272]{3,2,1,0:T(8,128)(2,1)S(1)}, u32[]{:S(2)}, u32[]{:S(2)}) collective-permute-start(bf16[3,1,136,272]{3,2,1,0:T(8,128)(2,1)S(1)} %broadcast_select_fusion.4), channel_id=1, source_target_pairs={{0,16},{4,20},{8,24},{12,28},{16,0},{20,4},{24,8},{28,12},{1,17},{... | collective-permute-start | bytes 665864 | tf_op jit(solution)/shard_map/ppermute | solution.py:60
  (78 other events, 827.2 us)
